TPU v7x, 128 devices: a whole 4x4x4 slice. The times are simulated.
128 devices in a mesh: grp: 4 (over z), tile: 32 (over y, x, core).
Axes of the slice: x: 4, y: 4, z: 4, core: 2. Of those that a mesh axis runs over, the one named last changes fastest.
Arguments:
- shot_data: bfloat16 [128, 256, 512], P('grp', 'tile'), may hold values from -6 to 6
- weight_first: bfloat16 [9, 64], replicated, may hold values from -2 to 2
- weight_middle: bfloat16 [1, 9, 64, 64], replicated, may hold values from -0.25 to 0.25
- weight_last: bfloat16 [9, 64], replicated, may hold values from -0.25 to 0.25
- moveout_maps: bfloat16 [8, 512, 512], replicated, may hold values from -0.25 to 0.25
- block_offset: int32 [256], P(('grp', 'tile')), may hold values from 0 to 7
- block_target: int32 [256, 1], P(('grp', 'tile')), may hold values from 0 to 31
Outputs:
- denoised: bfloat16 [128, 256, 512], P('grp', 'tile')
- stacked: float32 [32, 128, 512], P('grp', 'tile')
All inputs are finite; a program needn't handle non-finite values.
Results may differ from a plain program's by a relative error of at most 0.0038.
Values may be sent and summed in bfloat16 or wider, within the bound.
No kernel may reach another device: no remote copies, remote signals or barrier semaphores. Data moves between devices by JAX's collectives and lax.ppermute only.
A program may use at most 512 MiB of HBM per device.

v0:
```python
import jax
import jax.numpy as jnp
from jax import lax
from jax.sharding import PartitionSpec as P

CH = 64
LAYERS = 3
RD = 8
SH = 32
NT = 512
MB_G = 8
BLK = 128


def padded_2(block, sides, width):
    for axis, dim in sides:
        count = lax.axis_size(axis)
        forward = [(i, i + 1) for i in range(count - 1)]
        backward = [(target, source) for source, target in forward]
        low = lax.ppermute(
            lax.slice_in_dim(block, block.shape[dim] - width, None, axis=dim), axis, forward
        )
        high = lax.ppermute(lax.slice_in_dim(block, 0, width, axis=dim), axis, backward)
        block = jnp.concatenate([low, block, high], axis=dim)
    return block


def convolve(signal, kernel):
    breadth = signal.shape[1] - 2
    length = signal.shape[3]
    padded = jnp.pad(signal, ((0, 0), (0, 0), (0, 0), (1, 1)))
    delayed = jnp.stack([padded[:, :, :, delay : delay + length] for delay in range(3)], axis=2)
    summed = None
    for across in range(3):
        window = delayed[:, across : across + breadth]
        term = jnp.einsum(
            "srdct,doc->srot",
            window,
            kernel[3 * across : 3 * across + 3],
            preferred_element_type=jnp.float32,
        )
        summed = term if summed is None else summed + term
    return summed


def on_device(
    shot_data, weight_first, weight_middle, weight_last, moveout_maps, block_offset, block_target
):
    kernels = [weight_first.reshape(9, CH, 1)]
    number = 0
    kernels.append(weight_middle[number])
    kernels.append(weight_last.reshape(9, 1, CH))
    signal = shot_data[:, :, None, :]
    summed = None
    for number in range(LAYERS):
        padded = padded_2(signal, (("tile", 1),), 1)
        summed = convolve(padded, kernels[number])
        if number < LAYERS - 1:
            activated = jnp.maximum(summed, 0.0)
            signal = activated.astype(jnp.bfloat16)
    denoised = (shot_data.astype(jnp.float32) - summed[:, :, 0, :]).astype(jnp.bfloat16)
    block_count = SH * RD // BLK
    traces = denoised.reshape(block_count, BLK, NT)
    group_count = lax.axis_size("grp")
    matrices = moveout_maps[block_offset]
    corrected = jnp.einsum("bit,btu->biu", traces, matrices, preferred_element_type=jnp.float32)
    selector = (
        block_target[:, 0][:, None] == jnp.arange(MB_G * group_count, dtype=jnp.int32)[None, :]
    ).astype(jnp.float32)
    spread_blocks = jnp.einsum("bm,biu->miu", selector, corrected, precision=lax.Precision.HIGHEST)
    partial_value = lax.psum_scatter(spread_blocks, "tile", scatter_dimension=1, tiled=True)
    stacked = lax.psum_scatter(partial_value, "grp", scatter_dimension=0, tiled=True)
    return (denoised, stacked)


def solution(mesh):
    in_specs = (
        P("grp", "tile", None),
        P(),
        P(),
        P(),
        P(),
        P(("grp", "tile")),
        P(("grp", "tile"), None),
    )
    out_specs = (P("grp", "tile", None), P("grp", "tile", None))
    return jax.shard_map(
        on_device, mesh=mesh, in_specs=in_specs, out_specs=out_specs, check_vma=False
    )
```

profile of v0, /device:TPU:0, one launch (start us, length us, event | category | flops | bytes accessed | tf_op | source)
XLA Modules:
  0.0 685.0 jit_solution(17702988673851677746)
XLA Ops:
  18.6 14.0 %fusion.14 = f32[32,8,512,64]{2,3,1,0:T(8,128)} fusion(bf16[32,10,3,1,512]{4,2,1,0,3:T(4,128)(2,1)S(1)} %pad_maximum_fusion.4, bf16[9,64]{1,0:T(8,128)(2,1)} %param.8), kind=kOutput, calls=%fused_computation.29 | convolution fusion | flops 50331648 | bytes 34604032 | tf_op jit(solution)/shard_map/srdct,doc->srot/dot_general | solution.py:36
  32.6 13.3 %fusion.15 = f32[32,8,512,64]{2,3,1,0:T(8,128)} fusion(bf16[32,10,3,1,512]{4,2,1,0,3:T(4,128)(2,1)S(1)} %pad_maximum_fusion.4, bf16[9,64]{1,0:T(8,128)(2,1)S(1)} %copy-done.6), kind=kOutput, calls=%fused_computation.31 | convolution fusion | flops 50331648 | bytes 34604032 | tf_op jit(solution)/shard_map/srdct,doc->srot/dot_general | solution.py:36
  45.9 28.7 %fusion.12 = bf16[32,8,64,512]{3,2,1,0:T(8,128)(2,1)} fusion(f32[32,8,512,64]{2,3,1,0:T(8,128)} %fusion.15, f32[32,8,512,64]{2,3,1,0:T(8,128)} %fusion.14, bf16[32,10,3,1,512]{4,2,1,0,3:T(4,128)(2,1)S(1)} %pad_maximum_fusion.4, bf16[9,64]{1,0:T(8,128)(2,1)S(1)} %copy-done.6), kind=kOutput, calls=%fused_computation.24 | convolution fusion | flops 83886080 | bytes 84935680 | tf_op jit(solution)/shard_map/srdct,doc->srot/dot_general | solution.py:36
  77.2 4.6 collective-permute-start.2
  88.0 21.3 %fusion.46 = (bf16[32,10,1,64,512]{4,3,1,0,2:T(8,128)(2,1)}, bf16[32,10,64,512]{3,2,1,0:T(8,128)(2,1)}) fusion(bf16[32,1,64,512]{3,2,1,0:T(8,128)(2,1)} %collective-permute-done.3, bf16[32,8,64,512]{3,2,1,0:T(8,128)(2,1)} %fusion.12, bf16[32,1,64,512]{3,2,1,0:T(8,128)(2,1)S(1)} %collective-permute-done.2), kind=kLoop, calls=%fused_computation.73 | loop fusion | flops 20971520 | bytes 62914560 | tf_op jit(solution)/shard_map/stack | solution.py:32
  109.3 29.5 %fusion.8 = (bf16[32,10,1,64,512]{4,3,1,0,2:T(8,128)(2,1)}, bf16[32,10,1,64,512]{4,3,1,0,2:T(8,128)(2,1)}) fusion(bf16[32,10,64,512]{3,2,1,0:T(8,128)(2,1)} %get-tuple-element.20), kind=kLoop, calls=%fused_computation.18 | loop fusion | bytes 62914560 | tf_op jit(solution)/shard_map/stack | solution.py:32
  138.8 40.6 %pad_maximum_fusion = bf16[32,10,3,64,512]{4,3,1,0,2:T(8,128)(2,1)} fusion(bf16[32,10,1,64,512]{4,3,1,0,2:T(8,128)(2,1)} %get-tuple-element.18, bf16[32,10,1,64,512]{4,3,1,0,2:T(8,128)(2,1)} %get-tuple-element.19, bf16[32,10,1,64,512]{4,3,1,0,2:T(8,128)(2,1)} %get-tuple-element.17), kind=kLoop, calls=%fused_computation.1 | loop fusion | flops 62914560 | bytes 125829120 | tf_op jit(solution)/shard_map/stack | solution.py:32
  179.4 96.9 %fusion.47 = (bf16[32,8,3,64,512]{4,3,1,0,2:T(8,128)(2,1)}, bf16[32,8,3,64,512]{4,3,1,0,2:T(8,128)(2,1)}, bf16[32,8,3,64,512]{4,3,1,0,2:T(8,128)(2,1)}) fusion(bf16[32,10,3,64,512]{4,3,1,0,2:T(8,128)(2,1)} %pad_maximum_fusion), kind=kLoop, calls=%fused_computation.74 | loop fusion | bytes 301989888 | tf_op jit(solution)/shard_map/slice | solution.py:35
  276.2 27.4 %fusion = f32[32,8,512,64,1]{2,3,0,1,4:T(8,128)} fusion(bf16[32,8,3,64,512]{4,3,1,0,2:T(8,128)(2,1)} %get-tuple-element.11, bf16[1,9,64,64]{3,2,1,0:T(8,128)(2,1)S(1)} %copy-done.5), kind=kOutput, calls=%fused_computation.3 | convolution fusion | flops 3221225472 | bytes 83935232 | tf_op jit(solution)/shard_map/srdct,doc->srot/dot_general | solution.py:36
  303.6 27.4 %fusion.2 = f32[32,8,512,64,1]{2,3,0,1,4:T(8,128)} fusion(bf16[32,8,3,64,512]{4,3,1,0,2:T(8,128)(2,1)} %get-tuple-element.12, bf16[1,9,64,64]{3,2,1,0:T(8,128)(2,1)S(1)} %copy-done.5), kind=kOutput, calls=%fused_computation.5 | convolution fusion | flops 3221225472 | bytes 83935232 | tf_op jit(solution)/shard_map/srdct,doc->srot/dot_general | solution.py:36
  331.0 27.4 %fusion.4 = f32[32,8,512,64,1]{2,3,0,1,4:T(8,128)} fusion(bf16[32,8,3,64,512]{4,3,1,0,2:T(8,128)(2,1)} %get-tuple-element.10, bf16[1,9,64,64]{3,2,1,0:T(8,128)(2,1)S(1)} %copy-done.5), kind=kOutput, calls=%fused_computation.7 | convolution fusion | flops 3221225472 | bytes 83935232 | tf_op jit(solution)/shard_map/srdct,doc->srot/dot_general | solution.py:36
  358.4 32.2 %fusion.13 = bf16[32,8,64,512]{3,2,1,0:T(8,128)(2,1)S(1)} fusion(f32[32,8,512,64,1]{2,3,0,1,4:T(8,128)} %fusion, f32[32,8,512,64,1]{2,3,0,1,4:T(8,128)} %fusion.2, f32[32,8,512,64,1]{2,3,0,1,4:T(8,128)} %fusion.4), kind=kLoop, calls=%fused_computation.25 | loop fusion | flops 33554432 | bytes 117440512 | tf_op jit(solution)/shard_map/convert_element_type | solution.py:60
  390.7 5.7 copy-done
  398.6 23.2 %collective-permute-start.4 = (bf16[32,1,64,512]{3,2,1,0:T(8,128)(2,1)}, bf16[32,1,64,512]{3,2,1,0:T(8,128)(2,1)S(1)}, u32[]{:S(2)}, u32[]{:S(2)}) collective-permute-start(bf16[32,1,64,512]{3,2,1,0:T(8,128)(2,1)} %get-tuple-element.21), channel_id=1, source_target_pairs={{0,1},{1,2},{2,3},{3,4},{4,5},{5,6},{6,7},{7,8},{8,9},{9,10},{10,1... | collective-permute-start | bytes 6291464 | tf_op jit(solution)/shard_map/ppermute | solution.py:20
  423.4 3.8 gather_fusion
  428.2 21.4 %fusion.45 = (bf16[32,10,1,64,512]{4,3,1,0,2:T(8,128)(2,1)}, bf16[32,10,64,512]{3,2,1,0:T(8,128)(2,1)}) fusion(bf16[32,1,64,512]{3,2,1,0:T(8,128)(2,1)} %collective-permute-done.5, bf16[32,8,64,512]{3,2,1,0:T(8,128)(2,1)} %copy-done, bf16[32,1,64,512]{3,2,1,0:T(8,128)(2,1)S(1)} %collective-permute-done.4), kind=kLoop, calls=%fused_computation.72 | loop fusion | flops 20971520 | bytes 62914560 | tf_op jit(solution)/shard_map/stack | solution.py:32
  449.6 29.6 %fusion.10 = (bf16[32,10,1,64,512]{4,3,1,0,2:T(8,128)(2,1)}, bf16[32,10,1,64,512]{4,3,1,0,2:T(8,128)(2,1)}) fusion(bf16[32,10,64,512]{3,2,1,0:T(8,128)(2,1)} %get-tuple-element.16), kind=kLoop, calls=%fused_computation.20 | loop fusion | bytes 62914560 | tf_op jit(solution)/shard_map/stack | solution.py:32
  479.2 17.5 %fusion.34 = f32[1,32,8,512,1]{3,0,2,1,4:T(1,128)S(1)} fusion(bf16[3,64,1,1,1]{1,0,2,3,4:T(4,128)(2,1)S(1)} %get-tuple-element.31, bf16[32,10,1,64,512]{4,3,1,0,2:T(8,128)(2,1)} %get-tuple-element.14, bf16[32,10,1,64,512]{4,3,1,0,2:T(8,128)(2,1)} %get-tuple-element.15, bf16[32,10,1,64,512]{4,3,1,0,2:T(8,128)(2,1)} %get-tuple-element.13), kind=kOutput, calls=%fused_computation.58 | convolution fusion | flops 239075328 | bytes 63439232 | tf_op jit(solution)/shard_map/srdct,doc->srot/dot_general | solution.py:36
  496.7 4.1 copy-done.1
  500.9 12.1 %fusion.32 = f32[1,32,8,512,1]{3,0,2,1,4:T(1,128)S(1)} fusion(bf16[3,64,1,1,1]{1,0,2,3,4:T(4,128)(2,1)S(1)} %get-tuple-element.33, bf16[32,10,1,64,512]{4,3,1,0,2:T(8,128)(2,1)} %get-tuple-element.14, bf16[32,10,1,64,512]{4,3,1,0,2:T(8,128)(2,1)S(1)} %copy-done.1, bf16[32,10,1,64,512]{4,3,1,0,2:T(8,128)(2,1)} %get-tuple-element.13), kind=kOutput, calls=%fused_computation.56 | convolution fusion | flops 239075328 | bytes 63439232 | tf_op jit(solution)/shard_map/srdct,doc->srot/dot_general | solution.py:36
  513.0 12.5 %fusion.30 = f32[1,32,8,512,1]{3,0,2,1,4:T(1,128)S(1)} fusion(bf16[3,64,1,1,1]{1,0,2,3,4:T(4,128)(2,1)S(1)} %get-tuple-element.32, bf16[32,10,1,64,512]{4,3,1,0,2:T(8,128)(2,1)} %get-tuple-element.14, bf16[32,10,1,64,512]{4,3,1,0,2:T(8,128)(2,1)S(1)} %copy-done.1, bf16[32,10,1,64,512]{4,3,1,0,2:T(8,128)(2,1)} %get-tuple-element.13), kind=kOutput, calls=%fused_computation.54 | convolution fusion | flops 239075328 | bytes 63439232 | tf_op jit(solution)/shard_map/srdct,doc->srot/dot_general | solution.py:36
  526.1 6.0 fusion.18
  532.2 121.6 %reduce-scatter.3.cloned.1.call-done = f32[32,4,512]{2,0,1:T(8,128)} async-done(((f32[32,128,512]{2,0,1:T(8,128)}), f32[32,4,512]{2,0,1:T(8,128)}) %reduce-scatter.3.cloned.1.call-update) | async-done | bytes 262160 | tf_op jit(solution)/shard_map/reduce_scatter | solution.py:71
  653.9 22.8 %reduce-scatter.5.cloned.1.call-done = f32[8,4,512]{2,0,1:T(8,128)} async-done(((f32[32,4,512]{2,0,1:T(8,128)}), f32[8,4,512]{2,0,1:T(8,128)}) %reduce-scatter.5.cloned.1.call-update) | async-done | bytes 65552 | tf_op jit(solution)/shard_map/reduce_scatter | solution.py:72
  (48 shorter events, 27.0 us)
Async XLA Ops:
  7.2 646.7 %reduce-scatter.3.cloned.1.call-start = ((), (), s32[]{:S(2)}) async-start(), calls=%async_computation.2 | async-start | bytes 8650752 | tf_op jit(solution)/shard_map/reduce_scatter | solution.py:71
  8.3 2.6 collective-permute-start
  9.6 4.9 collective-permute-start.1
  18.6 14.0 %copy-start.6 = (bf16[9,64]{1,0:T(8,128)(2,1)S(1)}, bf16[9,64]{1,0:T(8,128)(2,1)}, u32[]{:S(2)}) copy-start(bf16[9,64]{1,0:T(8,128)(2,1)} %param.8) | copy-start | bytes 3460
  77.2 8.3 %collective-permute-start.2 = (bf16[32,1,64,512]{3,2,1,0:T(8,128)(2,1)S(1)}, bf16[32,1,64,512]{3,2,1,0:T(8,128)(2,1)S(1)}, u32[]{:S(2)}, u32[]{:S(2)}) collective-permute-start(bf16[32,1,64,512]{3,2,1,0:T(8,128)(2,1)S(1)} %get-tuple-element.23), channel_id=1, source_target_pairs={{0,1},{1,2},{2,3},{3,4},{4,5},{5,6},{6,7},{7,8},{8,9},{9,10},{10,1... | collective-permute-start | bytes 6291464 | tf_op jit(solution)/shard_map/ppermute | solution.py:20
  81.8 6.2 collective-permute-start.3
  179.4 96.9 %copy-start.5 = (bf16[1,9,64,64]{3,2,1,0:T(8,128)(2,1)S(1)}, bf16[1,9,64,64]{3,2,1,0:T(8,128)(2,1)}, u32[]{:S(2)}) copy-start(bf16[1,9,64,64]{3,2,1,0:T(8,128)(2,1)} %param.9) | copy-start | bytes 221188
  358.4 64.9 %copy-start.9 = (s32[2]{0:T(128)S(1)}, s32[2]{0:T(128)}, u32[]{:S(2)}) copy-start(s32[2]{0:T(128)} %param.12) | copy-start | bytes 28
  358.4 68.8 %copy-start.7 = (bf16[9,64]{1,0:T(8,128)(2,1)S(1)}, bf16[9,64]{1,0:T(8,128)(2,1)}, u32[]{:S(2)}) copy-start(bf16[9,64]{1,0:T(8,128)(2,1)} %param.10) | copy-start | bytes 3460
  390.7 5.8 copy-start
  398.6 28.6 %collective-permute-start.4 = (bf16[32,1,64,512]{3,2,1,0:T(8,128)(2,1)}, bf16[32,1,64,512]{3,2,1,0:T(8,128)(2,1)S(1)}, u32[]{:S(2)}, u32[]{:S(2)}) collective-permute-start(bf16[32,1,64,512]{3,2,1,0:T(8,128)(2,1)} %get-tuple-element.21), channel_id=1, source_target_pairs={{0,1},{1,2},{2,3},{3,4},{4,5},{5,6},{6,7},{7,8},{8,9},{9,10},{10,1... | collective-permute-start | bytes 6291464 | tf_op jit(solution)/shard_map/ppermute | solution.py:20
  421.8 6.4 collective-permute-start.5
  479.2 21.6 %copy-start.1 = (bf16[32,10,1,64,512]{4,3,1,0,2:T(8,128)(2,1)S(1)}, bf16[32,10,1,64,512]{4,3,1,0,2:T(8,128)(2,1)}, u32[]{:S(2)}) copy-start(bf16[32,10,1,64,512]{4,3,1,0,2:T(8,128)(2,1)} %get-tuple-element.15) | copy-start | bytes 62914564
  513.0 12.5 %copy-start.4 = (bf16[32,8,512]{2,1,0:T(8,128)(2,1)S(1)}, bf16[32,8,512]{2,1,0:T(8,128)(2,1)}, u32[]{:S(2)}) copy-start(bf16[32,8,512]{2,1,0:T(8,128)(2,1)} %param.7) | copy-start | bytes 786436
  513.0 12.8 %copy-start.2 = (bf16[2,512,512]{2,1,0:T(8,128)(2,1)S(1)}, bf16[2,512,512]{2,1,0:T(8,128)(2,1)}, u32[]{:S(2)}) copy-start(bf16[2,512,512]{2,1,0:T(8,128)(2,1)} %gather_fusion) | copy-start | bytes 3145732
  513.0 13.1 %copy-start.8 = (s32[2,1]{0,1:T(1,128)S(1)}, s32[2,1]{0,1:T(1,128)}, u32[]{:S(2)}) copy-start(s32[2,1]{0,1:T(1,128)} %param.13) | copy-start | bytes 28
  525.7 152.4 %copy-start.3 = (bf16[32,8,512]{2,1,0:T(8,128)(2,1)}, bf16[32,8,512]{2,1,0:T(8,128)(2,1)S(1)}, u32[]{:S(2)}) copy-start(bf16[32,8,512]{2,1,0:T(8,128)(2,1)S(1)} %fusion.17) | copy-start | bytes 786436
  532.1 144.5 %reduce-scatter.5.cloned.1.call-start = ((), (), s32[]{:S(2)}) async-start(), calls=%async_computation.3 | async-start | bytes 327680 | tf_op jit(solution)/shard_map/reduce_scatter | solution.py:72
Sparse Core Ops, SparseCore 0:
  532.3 121.5 reduce-scatter.2
  656.3 20.2 reduce-scatter.4
where the time goes:
time: 686 us; the launch traced here: 685 us
  matrix products  187 us (27%)
  local copies, waits for them, and re-layouts  179 us (26%)
  waiting for transfers between devices  154 us (22%)
  other arithmetic  118 us (17%)
  starting transfers between devices  33.5 us (5%)
  between operations  14.3 us (2%)
    dot_general x9, matrix products, convolve(): jnp.einsum('srdct,doc->srot', window, kernel[3 * across:3 * across + 3],...  180 us
    reduce_scatter x1, waiting for transfers between devices, on_device(): lax.psum_scatter(spread_blocks, 'tile', scatter_dimension=1, tiled=True)  122 us
    slice x1, local copies, waits for them, and re-layouts, convolve(): window = delayed[:, across:across + breadth]  96.9 us
    another operation x5, other arithmetic, convolve(): jnp.stack([padded[:, :, :, delay:delay + length] for delay in range(3)],...  85.5 us
    another operation x6, local copies, waits for them, and re-layouts, convolve(): jnp.stack([padded[:, :, :, delay:delay + length] for delay in range(3)],...  61 us
    convert_element_type x1, other arithmetic, on_device(): signal = activated.astype(jnp.bfloat16)  32.2 us
    ppermute x3, starting transfers between devices, padded_2(): lax.ppermute(lax.slice_in_dim(block, block.shape[dim] - width, None, axis...  29.1 us
    reduce_scatter x1, waiting for transfers between devices, on_device(): lax.psum_scatter(partial_value, 'grp', scatter_dimension=0, tiled=True)  22.8 us
  transfers between devices with their start and end apart: 8, of which 6 were waited for; matrix products, arithmetic and copies ran while one was open for 1% of the time, Pallas kernels for 0%

commit v1 on v0

v1 whole, which is shorter than its diff:
```python
import jax
import jax.numpy as jnp
import numpy as np
from jax import lax
from jax.experimental import pallas as pl
from jax.experimental.pallas import tpu as pltpu
from jax.sharding import PartitionSpec as P

CH = 64
RD = 8
SH = 32
NT = 512
HALF = NT // 2
BLK = 128
PER_STEP = 2
SHOTS_PER_BLOCK = BLK // RD
F32 = jnp.float32
BF16 = jnp.bfloat16


def at_lane(shape, lane):
    return lax.broadcasted_iota(jnp.int32, shape, 1) % HALF == lane


def delayed(rows):
    return jnp.where(at_lane(rows.shape, 0), 0.0, pltpu.roll(rows, 1, 1))


def advanced(rows):
    return jnp.where(at_lane(rows.shape, HALF - 1), 0.0, pltpu.roll(rows, rows.shape[1] - 1, 1))


def denoise_body(
    offset_ref, low_ref, own_ref, high_ref, first_ref, middle_ref, last_ref, map_ref, *rest
):
    denoised_ref, corrected_ref, slots, h1, h2, cleaned = rest[-6:]
    step = pl.program_id(0)
    shots = own_ref.shape[0]

    @pl.when(step == 0)
    def split_samples():
        time = lax.broadcasted_iota(jnp.int32, (NT, 4 * HALF), 0)
        lane = lax.broadcasted_iota(jnp.int32, (NT, 4 * HALF), 1)
        split = (time == 2 * (lane % HALF) + lane // HALF - 1).astype(F32).astype(BF16)
        for side, ref in enumerate((low_ref, own_ref, high_ref)):
            taken = jnp.dot(ref[...].reshape(shots * RD, NT), split, preferred_element_type=F32)
            for slot in range(4):
                row = (4 * side + slot) * RD
                part = taken[:, slot * HALF : (slot + 1) * HALF]
                slots[:, row : row + RD, :] = part.reshape(shots, RD, HALF)

    for each in range(PER_STEP):
        lanes = slice(each * HALF, (each + 1) * HALF)
        taps = slots[step * PER_STEP + each].astype(BF16)
        summed = jnp.dot(first_ref[...], taps, preferred_element_type=F32)
        active = jnp.maximum(summed, 0.0)
        for receiver in range(RD + 4):
            pair = active[receiver * 2 * CH : (receiver + 1) * 2 * CH]
            row = receiver * 4 * CH
            h1[row + CH : row + 3 * CH, lanes] = pair.astype(BF16)
            h1[row : row + CH, lanes] = delayed(pair[CH:]).astype(BF16)
            h1[row + 3 * CH : row + 4 * CH, lanes] = advanced(pair[:CH]).astype(BF16)
    for receiver in range(RD + 2):
        window = h1[receiver * 4 * CH : (receiver + 3) * 4 * CH, :]
        summed = jnp.dot(middle_ref[...], window, preferred_element_type=F32)
        h2[receiver * 2 * CH : (receiver + 1) * 2 * CH, :] = jnp.maximum(summed, 0.0).astype(BF16)
    parts = jnp.dot(last_ref[...], h2[...], preferred_element_type=F32)
    even = parts[:RD] + delayed(parts[2 * RD : 3 * RD])
    odd = parts[RD : 2 * RD] + advanced(parts[3 * RD :])
    for each in range(PER_STEP):
        lanes = slice(each * HALF, (each + 1) * HALF)
        shot = step * PER_STEP + each
        rows = pl.ds(pl.multiple_of(shot * RD, RD), RD)
        cleaned[rows, :HALF] = slots[shot, 5 * RD : 6 * RD, :] - even[:, lanes]
        cleaned[rows, HALF:] = slots[shot, 6 * RD : 7 * RD, :] - odd[:, lanes]

    @pl.when(step == pl.num_programs(0) - 1)
    def merge_samples():
        lane = lax.broadcasted_iota(jnp.int32, (NT, NT), 0)
        time = lax.broadcasted_iota(jnp.int32, (NT, NT), 1)
        merge = (time == 2 * (lane % HALF) + lane // HALF).astype(F32).astype(BF16)
        traces = jnp.dot(cleaned[...].astype(BF16), merge, preferred_element_type=F32).astype(BF16)
        denoised_ref[...] = traces.reshape(shots, RD, NT)
        moved = jnp.dot(traces, map_ref[0], preferred_element_type=F32)
        corrected_ref[...] = moved.reshape(corrected_ref.shape)


def denoise_block(number, offsets, low, own, high, weights, moveout_maps, before):
    shots = SHOTS_PER_BLOCK
    part = pl.BlockSpec((shots, RD, NT), lambda i, o: (number, 0, 0))
    whole = [pl.BlockSpec(w.shape, lambda i, o: (0, 0)) for w in weights]
    chosen = pl.BlockSpec((1, NT, NT), lambda i, o: (o[number], 0, 0))
    held = [] if before is None else [before]
    owners = lax.axis_size("tile")
    return pl.pallas_call(
        denoise_body,
        out_shape=(
            jax.ShapeDtypeStruct((SH, RD, NT), BF16),
            jax.ShapeDtypeStruct((owners, BLK // owners, NT), F32),
        ),
        grid_spec=pltpu.PrefetchScalarGridSpec(
            num_scalar_prefetch=1,
            grid=(shots // PER_STEP,),
            in_specs=[part] * 3 + whole + [chosen] + [pl.BlockSpec(memory_space=pl.ANY)] * len(held),
            out_specs=(part, pl.BlockSpec((owners, BLK // owners, NT), lambda i, o: (0, 0, 0))),
            scratch_shapes=[
                pltpu.VMEM((shots, 12 * RD, HALF), F32),
                pltpu.VMEM(((RD + 4) * 4 * CH, PER_STEP * HALF), BF16),
                pltpu.VMEM(((RD + 2) * 2 * CH, PER_STEP * HALF), BF16),
                pltpu.VMEM((shots * RD, NT), F32),
            ],
        ),
        input_output_aliases={8: 0} if held else {},
        compiler_params=pltpu.CompilerParams(
            dimension_semantics=("arbitrary",), vmem_limit_bytes=48 << 20
        ),
        name="denoise",
    )(offsets, low, own, high, *weights, moveout_maps, *held)


def first_places():
    places = np.zeros((RD + 4, 2, 12 * RD, 9), np.float32)
    for receiver in range(RD + 4):
        for phase in range(2):
            for tap in range(9):
                across, delay = divmod(tap, 3)
                side, row = divmod(receiver - 2 + across - 1 + RD, RD)
                places[receiver, phase, (4 * side + phase + delay) * RD + row, tap] = 1
    return places


def place_weights(weight_first, weight_middle, weight_last):
    tile = lax.axis_index("tile")
    low = (tile > 0).astype(F32)
    high = (tile < lax.axis_size("tile") - 1).astype(F32)
    one = jnp.ones((), F32)
    inside = jnp.stack([low] * 2 + [one] * RD + [high] * 2)
    first = jnp.einsum(
        "rpkn,nc->rpck", jnp.asarray(first_places(), BF16), weight_first, preferred_element_type=F32
    )
    first = (first * inside[:, None, None, None]).astype(BF16).reshape((RD + 4) * 2 * CH, 12 * RD)
    taps = weight_middle.reshape(3, 3, CH, CH).transpose(2, 0, 1, 3)
    middle = jnp.stack(
        [jnp.pad(taps, ((0, 0), (0, 0), (phase, 1 - phase), (0, 0))) for phase in range(2)]
    ).reshape(2 * CH, 12 * CH)
    taps = weight_last.reshape(3, 3, CH)
    none = jnp.zeros((3, CH), BF16)
    kinds = jnp.stack(
        [
            jnp.stack([taps[:, 1], taps[:, 2]], 1),
            jnp.stack([taps[:, 0], taps[:, 1]], 1),
            jnp.stack([none, taps[:, 0]], 1),
            jnp.stack([taps[:, 2], none], 1),
        ]
    ).reshape(4, 6 * CH)
    last = jnp.stack(
        [jnp.pad(kinds, ((0, 0), (r * 2 * CH, (RD - 1 - r) * 2 * CH))) for r in range(RD)], 1
    )
    inside = jnp.repeat(inside[1:-1], 2 * CH, total_repeat_length=(RD + 2) * 2 * CH)
    last = (last.astype(F32) * inside).astype(BF16).reshape(4 * RD, (RD + 2) * 2 * CH)
    return first, middle, last


def stack_kernel(place_ref, early_ref, late_ref, total_ref):
    total_ref[...] = jnp.zeros_like(total_ref)
    for tile in range(early_ref.shape[0]):
        for number, ref in enumerate((early_ref, late_ref)):
            place = place_ref[tile, number]
            total_ref[place] = total_ref[place] + ref[tile]


def stack(places, early, late, count):
    return pl.pallas_call(
        stack_kernel,
        out_shape=jax.ShapeDtypeStruct((count, *early.shape[1:]), F32),
        in_specs=[
            pl.BlockSpec(memory_space=pltpu.SMEM),
            pl.BlockSpec(memory_space=pltpu.VMEM),
            pl.BlockSpec(memory_space=pltpu.VMEM),
        ],
        out_specs=pl.BlockSpec(memory_space=pltpu.VMEM),
        name="stack",
    )(places, early, late)


def on_device(
    shot_data, weight_first, weight_middle, weight_last, moveout_maps, block_offset, block_target
):
    tiles, groups = lax.axis_size("tile"), lax.axis_size("grp")
    low = lax.ppermute(shot_data, "tile", [(i, i + 1) for i in range(tiles - 1)])
    high = lax.ppermute(shot_data, "tile", [(i + 1, i) for i in range(tiles - 1)])
    weights = place_weights(weight_first, weight_middle, weight_last)
    targets = lax.all_gather(block_target[:, 0], "tile")
    count = 32
    owned = count // groups
    group = lax.axis_index("grp")
    places = ((targets // owned - group) % groups) * owned + targets % owned

    denoised, early = denoise_block(
        0, block_offset, low, shot_data, high, weights, moveout_maps, None
    )
    early = lax.all_to_all(early, "tile", 0, 0, tiled=True)
    denoised, late = denoise_block(
        1, block_offset, low, shot_data, high, weights, moveout_maps, denoised
    )
    late = lax.all_to_all(late, "tile", 0, 0, tiled=True)
    parts = stack(places, early, late, count).reshape(groups, owned, -1, NT)
    stacked = parts[0]
    for ahead in range(1, groups):
        route = [(g, (g + ahead) % groups) for g in range(groups)]
        stacked = stacked + lax.ppermute(parts[ahead], "grp", route)
    return denoised, stacked


def solution(mesh):
    in_specs = (
        P("grp", "tile", None),
        P(),
        P(),
        P(),
        P(),
        P(("grp", "tile")),
        P(("grp", "tile"), None),
    )
    out_specs = (P("grp", "tile", None), P("grp", "tile", None))
    return jax.shard_map(
        on_device, mesh=mesh, in_specs=in_specs, out_specs=out_specs, check_vma=False
    )
```

time: 686 us -> 107 us (0.16)
  matrix products: 187 us -> 1.2 us
  local copies, waits for them, and re-layouts: 179 us -> 9.33 us
  waiting for transfers between devices: 154 us -> 10.8 us
  other arithmetic: 118 us -> 2.62 us
  Pallas kernels: 0 us -> 37.9 us
  blocking collectives: 0 us -> 17.3 us
  between operations: 14.3 us -> 1.58 us
  starting transfers between devices: 33.5 us -> 25.5 us
    dot_general x11 -> x1, matrix products: 187 us -> 1.2 us  [place_weights(): jnp.einsum('rpkn,nc->rpck', jnp.asarray(first_places(), BF16), weight_fir...]
    reduce_scatter x2 -> x0, waiting for transfers between devices: 144 us -> none  [the longest x1 122 us: on_device(): lax.psum_scatter(spread_blocks, 'tile', scatter_dimension=1, tiled=True)]
    slice x5 -> x2, local copies, waits for them, and re-layouts: 102 us -> 0.92 us  [the longest x1 0.92 us: on_device(): stacked = stacked + lax.ppermute(parts[ahead], 'grp', route)]
    another operation x5 -> x2, other arithmetic: 85.5 us -> 0.35 us  [the longest x1 0.33 us: place_weights(): jnp.stack([jnp.pad(taps, ((0, 0), (0, 0), (phase, 1 - phase), (0, 0))) fo...]
    another operation x6 -> x20, local copies, waits for them, and re-layouts: 61 us -> 1.1 us  [the longest x10 0.41 us: place_weights(): jnp.stack([jnp.pad(kinds, ((0, 0), (r * 2 * CH, (RD - 1 - r) * 2 * CH)))...]
    pallas_call x0 -> x3, Pallas kernels: none -> 37.9 us  [the longest x2 36 us: denoise_block(): pl.pallas_call(denoise_body, out_shape=(jax.ShapeDtypeStruct((SH, RD, NT)...]
    convert_element_type x2 -> x1, other arithmetic: 32.4 us -> 0.02 us  [place_weights(): (last.astype(F32) * inside).astype(BF16).reshape(4 * RD, (RD + 2) * 2 * CH)]
    ppermute x6 -> x5, starting transfers between devices: 33.4 us -> 9.18 us  [the longest x3 6.58 us: on_device(): stacked = stacked + lax.ppermute(parts[ahead], 'grp', route)]
  transfers between devices with their start and end apart: 8 -> 7, of which waited for: 6 -> 3; matrix products, arithmetic and copies ran while one was open for 1% -> 6% of each run, Pallas kernels for 0% -> 0%
where the time goes in v1:
time: 107 us; the launch traced here: 106 us
  Pallas kernels  37.9 us (35%)
  starting transfers between devices  25.5 us (24%)
  blocking collectives  17.3 us (16%)
  waiting for transfers between devices  10.8 us (10%)
  local copies, waits for them, and re-layouts  9.33 us (9%)
  other arithmetic  2.62 us (2%)
  between operations  1.58 us (1%)
  matrix products  1.2 us (1%)
    pallas_call x2, Pallas kernels, denoise_block(): pl.pallas_call(denoise_body, out_shape=(jax.ShapeDtypeStruct((SH, RD, NT)...  36 us
    unnamed x1, blocking collectives  17.3 us
    all_to_all x1, starting transfers between devices, on_device(): late = lax.all_to_all(late, 'tile', 0, 0, tiled=True)  12.4 us
    all_to_all x1, waiting for transfers between devices, on_device(): late = lax.all_to_all(late, 'tile', 0, 0, tiled=True)  7.65 us
    ppermute x3, starting transfers between devices, on_device(): stacked = stacked + lax.ppermute(parts[ahead], 'grp', route)  6.58 us
    unnamed x19, local copies, waits for them, and re-layouts  5.2 us
    all_to_all x1, starting transfers between devices, on_device(): early = lax.all_to_all(early, 'tile', 0, 0, tiled=True)  3.87 us
    ppermute x3, waiting for transfers between devices, on_device(): stacked = stacked + lax.ppermute(parts[ahead], 'grp', route)  3.19 us
  transfers between devices with their start and end apart: 7, of which 3 were waited for; matrix products, arithmetic and copies ran while one was open for 6% of the time, Pallas kernels for 0%

profile of v1, /device:TPU:0, one launch (start us, length us, event | category | flops | bytes accessed | tf_op | source)
XLA Modules:
  0.0 106.3 jit_solution(16525635917345325993)
XLA Ops:
  0.6 1.3 %collective-permute-start = (bf16[32,8,512]{2,1,0:T(8,128)(2,1)}, bf16[32,8,512]{2,1,0:T(8,128)(2,1)S(1)}, u32[]{:S(2)}, u32[]{:S(2)}) collective-permute-start(bf16[32,8,512]{2,1,0:T(8,128)(2,1)} %own_ref.3), channel_id=1, source_target_pairs={{0,1},{1,2},{2,3},{3,4},{4,5},{5,6},{6,7},{7,8},{8,9},{9,10},{10,1... | collective-permute-start | bytes 786440 | tf_op jit(solution)/shard_map/ppermute | solution.py:190
  2.0 1.3 %collective-permute-start.1 = (bf16[32,8,512]{2,1,0:T(8,128)(2,1)}, bf16[32,8,512]{2,1,0:T(8,128)(2,1)S(1)}, u32[]{:S(2)}, u32[]{:S(2)}) collective-permute-start(bf16[32,8,512]{2,1,0:T(8,128)(2,1)} %own_ref.3), channel_id=1, source_target_pairs={{1,0},{2,1},{3,2},{4,3},{5,4},{6,5},{7,6},{8,7},{9,8},{10,9},{11,1... | collective-permute-start | bytes 786440 | tf_op jit(solution)/shard_map/ppermute | solution.py:191
  3.3 0.7 reshape.138
  4.7 1.0 copy.94
  7.0 1.2 %fusion = bf16[12,2,96,64]{2,3,1,0:T(8,128)(2,1)S(1)} fusion(bf16[12,2,96,9]{2,3,1,0:T(8,128)(2,1)} %constant.133.clone, f32[12]{0:T(128)S(1)} %stack.87, bf16[9,64]{1,0:T(8,128)(2,1)S(1)} %copy-done), kind=kOutput, calls=%fused_computation.1 | convolution fusion | flops 2949120 | bytes 337584 | tf_op jit(solution)/shard_map/rpkn,nc->rpck/dot_general | solution.py:138
  8.3 2.2 %copy-done.1 = bf16[8,512,512]{2,1,0:T(8,128)(2,1)S(1)} copy-done((bf16[8,512,512]{2,1,0:T(8,128)(2,1)S(1)}, bf16[8,512,512]{2,1,0:T(8,128)(2,1)}, u32[]{:S(2)}) %copy-start.1) | copy-done | bytes 4194328
  10.5 0.9 copy-done.2
  11.4 0.7 copy-done.3
  12.1 18.0 %denoise.2 = (bf16[32,8,512]{2,1,0:T(8,128)(2,1)}, f32[32,4,512]{2,1,0:T(4,128)}) custom-call(s32[2]{0:T(128)S(1)} %copy-done.3, bf16[32,8,512]{2,1,0:T(8,128)(2,1)S(1)} %collective-permute-done.low_ref, bf16[32,8,512]{2,1,0:T(8,128)(2,1)S(1)} %copy-done.2, bf16[32,8,512]{2,1,0:T(8,128)(2,1)S(1)} %collective-permute-done.1.high_ref, ...), custom_call_target="tpu_custom_call" | custom-call | tf_op jit(solution)/shard_map/denoise/pallas_call | solution.py:95
  30.1 18.0 %denoise.3 = (bf16[32,8,512]{2,1,0:T(8,128)(2,1)}, f32[32,4,512]{2,1,0:T(4,128)}) custom-call(s32[2]{0:T(128)S(1)} %copy-done.3, bf16[32,8,512]{2,1,0:T(8,128)(2,1)S(1)} %collective-permute-done.low_ref, bf16[32,8,512]{2,1,0:T(8,128)(2,1)S(1)} %copy-done.2, bf16[32,8,512]{2,1,0:T(8,128)(2,1)S(1)} %collective-permute-done.1.high_ref, ...), custom_call_target="tpu_custom_call", output_to_operand_aliasing={{0}: (8, {})} | custom-call | tf_op jit(solution)/shard_map/denoise/pallas_call | solution.py:95
  48.1 12.4 %all-to-all-start.1 = ((f32[32,4,512]{2,1,0:T(4,128)}), f32[32,4,512]{2,1,0:T(4,128)S(1)}, u32[]{:S(2)}, u32[]{:S(2)}) async-start(f32[32,4,512]{2,1,0:T(4,128)} %get-tuple-element.21), calls=%async_computation.1 | async-start | bytes 524288 | tf_op jit(solution)/shard_map/all_to_all | solution.py:206
  61.8 7.6 %all-to-all-done.1.late_ref = f32[32,4,512]{2,1,0:T(4,128)S(1)} async-done(((f32[32,4,512]{2,1,0:T(4,128)}), f32[32,4,512]{2,1,0:T(4,128)S(1)}, u32[]{:S(2)}, u32[]{:S(2)}) %all-to-all-start.1) | async-done | bytes 262176 | tf_op jit(solution)/shard_map/all_to_all | solution.py:206
  69.4 3.9 %all-to-all-start = ((f32[32,4,512]{2,1,0:T(4,128)}), f32[32,4,512]{2,1,0:T(4,128)S(1)}, u32[]{:S(2)}, u32[]{:S(2)}) async-start(f32[32,4,512]{2,1,0:T(4,128)} %get-tuple-element.20), calls=%async_computation | async-start | bytes 524288 | tf_op jit(solution)/shard_map/all_to_all | solution.py:202
  73.4 17.3 %all-reduce.12 = s32[64]{0:T(128)S(1)} all-reduce(s32[64]{0:T(128)S(1)} %bitcast_dynamic-update-slice_fusion), channel_id=2, replica_groups=mesh['grp'=4,'tile'=32] {'tile'}, use_global_device_ids=true, to_apply=%add.12 | all-reduce | flops 64 | bytes 512
  90.8 0.6 fusion.7.place_ref
  91.5 0.7 copy-done.5
  92.2 1.9 %stack.116 = f32[32,4,512]{2,1,0:T(4,128)} custom-call(s32[32,2]{1,0:T(8,128)} %fusion.7.place_ref, f32[32,4,512]{2,1,0:T(4,128)} %copy-done.5, f32[32,4,512]{2,1,0:T(4,128)} %copy-done.4), custom_call_target="tpu_custom_call" | custom-call | tf_op jit(solution)/shard_map/stack/pallas_call | solution.py:173
  94.1 0.9 fusion.18
  95.0 1.9 %collective-permute-start.2 = (f32[8,4,512]{2,1,0:T(4,128)S(1)}, f32[8,4,512]{2,1,0:T(4,128)S(1)}, u32[]{:S(2)}, u32[]{:S(2)}) collective-permute-start(f32[8,4,512]{2,1,0:T(4,128)S(1)} %get-tuple-element.27), channel_id=1, source_target_pairs={{0,32},{32,64},{64,96},{96,0},{1,33},{33,65},{65,97},{97,1},{2,34}... | collective-permute-start | bytes 196616 | tf_op jit(solution)/shard_map/ppermute | solution.py:211
  96.9 3.6 %collective-permute-start.3 = (f32[8,4,512]{2,1,0:T(4,128)S(1)}, f32[8,4,512]{2,1,0:T(4,128)S(1)}, u32[]{:S(2)}, u32[]{:S(2)}) collective-permute-start(f32[8,4,512]{2,1,0:T(4,128)S(1)} %get-tuple-element.29), channel_id=1, source_target_pairs={{0,64},{32,96},{64,0},{96,32},{1,65},{33,97},{65,1},{97,33},{2,66}... | collective-permute-start | bytes 196616 | tf_op jit(solution)/shard_map/ppermute | solution.py:211
  100.5 1.1 %collective-permute-start.4 = (f32[8,4,512]{2,1,0:T(4,128)S(1)}, f32[8,4,512]{2,1,0:T(4,128)S(1)}, u32[]{:S(2)}, u32[]{:S(2)}) collective-permute-start(f32[8,4,512]{2,1,0:T(4,128)S(1)} %get-tuple-element.28), channel_id=1, source_target_pairs={{0,96},{32,0},{64,32},{96,64},{1,97},{33,1},{65,33},{97,65},{2,98}... | collective-permute-start | bytes 196616 | tf_op jit(solution)/shard_map/ppermute | solution.py:211
  101.6 1.9 %collective-permute-done.3 = f32[8,4,512]{2,1,0:T(4,128)S(1)} collective-permute-done((f32[8,4,512]{2,1,0:T(4,128)S(1)}, f32[8,4,512]{2,1,0:T(4,128)S(1)}, u32[]{:S(2)}, u32[]{:S(2)}) %collective-permute-start.3) | collective-permute-done | bytes 65568 | tf_op jit(solution)/shard_map/ppermute | solution.py:211
  103.5 1.3 %collective-permute-done.4 = f32[8,4,512]{2,1,0:T(4,128)S(1)} collective-permute-done((f32[8,4,512]{2,1,0:T(4,128)S(1)}, f32[8,4,512]{2,1,0:T(4,128)S(1)}, u32[]{:S(2)}, u32[]{:S(2)}) %collective-permute-start.4) | collective-permute-done | bytes 65568 | tf_op jit(solution)/shard_map/ppermute | solution.py:211
  104.8 1.5 %fusion.3 = f32[8,4,512]{2,1,0:T(4,128)} fusion(f32[8,4,512]{2,1,0:T(4,128)S(1)} %collective-permute-done.4, f32[8,4,512]{2,1,0:T(4,128)S(1)} %collective-permute-done.3, f32[8,4,512]{2,1,0:T(4,128)S(1)} %collective-permute-done.2, f32[32,4,512]{2,1,0:T(4,128)} %stack.116), kind=kLoop, calls=%fused_computation.10 | loop fusion | flops 49152 | bytes 327680 | tf_op jit(solution)/shard_map/add | solution.py:211
  (49 shorter events, 2.7 us)
Async XLA Ops:
  0.6 6.4 %copy-start = (bf16[9,64]{1,0:T(8,128)(2,1)S(1)}, bf16[9,64]{1,0:T(8,128)(2,1)}, u32[]{:S(2)}) copy-start(bf16[9,64]{1,0:T(8,128)(2,1)} %param.11) | copy-start | bytes 3460
  0.6 7.6 %collective-permute-start = (bf16[32,8,512]{2,1,0:T(8,128)(2,1)}, bf16[32,8,512]{2,1,0:T(8,128)(2,1)S(1)}, u32[]{:S(2)}, u32[]{:S(2)}) collective-permute-start(bf16[32,8,512]{2,1,0:T(8,128)(2,1)} %own_ref.3), channel_id=1, source_target_pairs={{0,1},{1,2},{2,3},{3,4},{4,5},{5,6},{6,7},{7,8},{8,9},{9,10},{10,1... | collective-permute-start | bytes 786440 | tf_op jit(solution)/shard_map/ppermute | solution.py:190
  2.0 6.3 %collective-permute-start.1 = (bf16[32,8,512]{2,1,0:T(8,128)(2,1)}, bf16[32,8,512]{2,1,0:T(8,128)(2,1)S(1)}, u32[]{:S(2)}, u32[]{:S(2)}) collective-permute-start(bf16[32,8,512]{2,1,0:T(8,128)(2,1)} %own_ref.3), channel_id=1, source_target_pairs={{1,0},{2,1},{3,2},{4,3},{5,4},{6,5},{7,6},{8,7},{9,8},{10,9},{11,1... | collective-permute-start | bytes 786440 | tf_op jit(solution)/shard_map/ppermute | solution.py:191
  8.3 2.2 %copy-start.1 = (bf16[8,512,512]{2,1,0:T(8,128)(2,1)S(1)}, bf16[8,512,512]{2,1,0:T(8,128)(2,1)}, u32[]{:S(2)}) copy-start(bf16[8,512,512]{2,1,0:T(8,128)(2,1)} %map_ref.3) | copy-start | bytes 12582916
  10.5 0.9 copy-start.2
  11.4 0.7 copy-start.3
  30.1 30.5 %copy-start.7 = (u32[128]{0:T(128)S(1)}, u32[128]{0:T(128)}, u32[]{:S(2)}) copy-start(u32[128]{0:T(128)} %constant.173) | copy-start | bytes 1540
  30.1 43.2 %copy-start.6 = (s32[2,1]{0,1:T(1,128)S(1)}, s32[2,1]{0,1:T(1,128)}, u32[]{:S(2)}) copy-start(s32[2,1]{0,1:T(1,128)} %param.16) | copy-start | bytes 28
  48.1 21.3 %all-to-all-start.1 = ((f32[32,4,512]{2,1,0:T(4,128)}), f32[32,4,512]{2,1,0:T(4,128)S(1)}, u32[]{:S(2)}, u32[]{:S(2)}) async-start(f32[32,4,512]{2,1,0:T(4,128)} %get-tuple-element.21), calls=%async_computation.1 | async-start | bytes 524288 | tf_op jit(solution)/shard_map/all_to_all | solution.py:206
  69.4 22.1 %copy-start.4 = (f32[32,4,512]{2,1,0:T(4,128)}, f32[32,4,512]{2,1,0:T(4,128)S(1)}, u32[]{:S(2)}) copy-start(f32[32,4,512]{2,1,0:T(4,128)S(1)} %all-to-all-done.1.late_ref) | copy-start | bytes 786436
  69.4 22.1 %all-to-all-start = ((f32[32,4,512]{2,1,0:T(4,128)}), f32[32,4,512]{2,1,0:T(4,128)S(1)}, u32[]{:S(2)}, u32[]{:S(2)}) async-start(f32[32,4,512]{2,1,0:T(4,128)} %get-tuple-element.20), calls=%async_computation | async-start | bytes 524288 | tf_op jit(solution)/shard_map/all_to_all | solution.py:202
  91.5 0.7 copy-start.5
  95.0 6.6 %collective-permute-start.2 = (f32[8,4,512]{2,1,0:T(4,128)S(1)}, f32[8,4,512]{2,1,0:T(4,128)S(1)}, u32[]{:S(2)}, u32[]{:S(2)}) collective-permute-start(f32[8,4,512]{2,1,0:T(4,128)S(1)} %get-tuple-element.27), channel_id=1, source_target_pairs={{0,32},{32,64},{64,96},{96,0},{1,33},{33,65},{65,97},{97,1},{2,34}... | collective-permute-start | bytes 196616 | tf_op jit(solution)/shard_map/ppermute | solution.py:211
  96.9 6.5 %collective-permute-start.3 = (f32[8,4,512]{2,1,0:T(4,128)S(1)}, f32[8,4,512]{2,1,0:T(4,128)S(1)}, u32[]{:S(2)}, u32[]{:S(2)}) collective-permute-start(f32[8,4,512]{2,1,0:T(4,128)S(1)} %get-tuple-element.29), channel_id=1, source_target_pairs={{0,64},{32,96},{64,0},{96,32},{1,65},{33,97},{65,1},{97,33},{2,66}... | collective-permute-start | bytes 196616 | tf_op jit(solution)/shard_map/ppermute | solution.py:211
  100.5 4.3 %collective-permute-start.4 = (f32[8,4,512]{2,1,0:T(4,128)S(1)}, f32[8,4,512]{2,1,0:T(4,128)S(1)}, u32[]{:S(2)}, u32[]{:S(2)}) collective-permute-start(f32[8,4,512]{2,1,0:T(4,128)S(1)} %get-tuple-element.28), channel_id=1, source_target_pairs={{0,96},{32,0},{64,32},{96,64},{1,97},{33,1},{65,33},{97,65},{2,98}... | collective-permute-start | bytes 196616 | tf_op jit(solution)/shard_map/ppermute | solution.py:211

commit v2 on v1

--- a/solution.py
+++ b/solution.py
@@ -12,8 +12,8 @@
 NT = 512
 HALF = NT // 2
 BLK = 128
+MBLK = 32
 PER_STEP = 2
-SHOTS_PER_BLOCK = BLK // RD
 F32 = jnp.float32
 BF16 = jnp.bfloat16
 
@@ -31,9 +31,9 @@
 
 
 def denoise_body(
-    offset_ref, low_ref, own_ref, high_ref, first_ref, middle_ref, last_ref, map_ref, *rest
+    offset_ref, low_ref, own_ref, high_ref, first_ref, middle_ref, last_ref, *rest
 ):
-    denoised_ref, corrected_ref, slots, h1, h2, cleaned = rest[-6:]
+    *map_refs, denoised_ref, corrected_ref, slots, h1, h2, cleaned = rest
     step = pl.program_id(0)
     shots = own_ref.shape[0]
 
@@ -81,28 +81,36 @@
         merge = (time == 2 * (lane % HALF) + lane // HALF).astype(F32).astype(BF16)
         traces = jnp.dot(cleaned[...].astype(BF16), merge, preferred_element_type=F32).astype(BF16)
         denoised_ref[...] = traces.reshape(shots, RD, NT)
-        moved = jnp.dot(traces, map_ref[0], preferred_element_type=F32)
-        corrected_ref[...] = moved.reshape(corrected_ref.shape)
-
-
-def denoise_block(number, offsets, low, own, high, weights, moveout_maps, before):
-    shots = SHOTS_PER_BLOCK
-    part = pl.BlockSpec((shots, RD, NT), lambda i, o: (number, 0, 0))
+        owners = corrected_ref.shape[0]
+        moved = []
+        for number, ref in enumerate(map_refs):
+            block = traces[number * BLK : (number + 1) * BLK]
+            block = jnp.dot(block, ref[0], preferred_element_type=F32)
+            moved.append(block.reshape(owners, BLK // owners, NT))
+        corrected_ref[...] = jnp.concatenate(moved, axis=1)
+
+
+def denoise(offsets, low, own, high, weights, moveout_maps):
+    shots, blocks = own.shape[0], offsets.shape[0]
+    part = pl.BlockSpec(own.shape, lambda i, o: (0, 0, 0))
     whole = [pl.BlockSpec(w.shape, lambda i, o: (0, 0)) for w in weights]
-    chosen = pl.BlockSpec((1, NT, NT), lambda i, o: (o[number], 0, 0))
-    held = [] if before is None else [before]
+    chosen = [
+        pl.BlockSpec((1, NT, NT), lambda i, o, number=number: (o[number], 0, 0))
+        for number in range(blocks)
+    ]
     owners = lax.axis_size("tile")
+    sent = (owners, blocks * BLK // owners, NT)
+    own = pltpu.with_memory_space_constraint(own, pltpu.HBM)
+    maps = pltpu.with_memory_space_constraint(moveout_maps, pltpu.HBM)
+    macs = shots * RD * NT * CH * (9 * CH + 18)
     return pl.pallas_call(
         denoise_body,
-        out_shape=(
-            jax.ShapeDtypeStruct((SH, RD, NT), BF16),
-            jax.ShapeDtypeStruct((owners, BLK // owners, NT), F32),
-        ),
+        out_shape=(jax.ShapeDtypeStruct(own.shape, BF16), jax.ShapeDtypeStruct(sent, F32)),
         grid_spec=pltpu.PrefetchScalarGridSpec(
             num_scalar_prefetch=1,
             grid=(shots // PER_STEP,),
-            in_specs=[part] * 3 + whole + [chosen] + [pl.BlockSpec(memory_space=pl.ANY)] * len(held),
-            out_specs=(part, pl.BlockSpec((owners, BLK // owners, NT), lambda i, o: (0, 0, 0))),
+            in_specs=[part] * 3 + whole + chosen,
+            out_specs=(part, pl.BlockSpec(sent, lambda i, o: (0, 0, 0))),
             scratch_shapes=[
                 pltpu.VMEM((shots, 12 * RD, HALF), F32),
                 pltpu.VMEM(((RD + 4) * 4 * CH, PER_STEP * HALF), BF16),
@@ -110,12 +118,12 @@
                 pltpu.VMEM((shots * RD, NT), F32),
             ],
         ),
-        input_output_aliases={8: 0} if held else {},
         compiler_params=pltpu.CompilerParams(
             dimension_semantics=("arbitrary",), vmem_limit_bytes=48 << 20
         ),
+        cost_estimate=pl.CostEstimate(flops=2 * macs, transcendentals=0, bytes_accessed=8 << 20),
         name="denoise",
-    )(offsets, low, own, high, *weights, moveout_maps, *held)
+    )(offsets, low, own, high, *weights, *[maps] * blocks)
 
 
 def first_places():
@@ -161,26 +169,33 @@
     return first, middle, last
 
 
-def stack_kernel(place_ref, early_ref, late_ref, total_ref):
-    total_ref[...] = jnp.zeros_like(total_ref)
-    for tile in range(early_ref.shape[0]):
-        for number, ref in enumerate((early_ref, late_ref)):
+def stack_body(place_ref, corrected_ref, *refs):
+    *part_refs, total = refs
+    total[...] = jnp.zeros_like(total)
+    rows = total.shape[1]
+    for tile in range(corrected_ref.shape[0]):
+        for number in range(corrected_ref.shape[1] // rows):
             place = place_ref[tile, number]
-            total_ref[place] = total_ref[place] + ref[tile]
-
-
-def stack(places, early, late, count):
+            held = corrected_ref[tile, number * rows : (number + 1) * rows, :]
+            total[place] = total[place] + held
+    for ahead, ref in enumerate(part_refs):
+        ref[...] = total[ahead * ref.shape[0] : (ahead + 1) * ref.shape[0]]
+
+
+def stack(places, corrected, groups, owned):
+    rows = corrected.shape[1] // places.shape[1]
+    part = jax.ShapeDtypeStruct((owned, rows, NT), F32)
     return pl.pallas_call(
-        stack_kernel,
-        out_shape=jax.ShapeDtypeStruct((count, *early.shape[1:]), F32),
+        stack_body,
+        out_shape=(part,) * groups,
         in_specs=[
             pl.BlockSpec(memory_space=pltpu.SMEM),
             pl.BlockSpec(memory_space=pltpu.VMEM),
-            pl.BlockSpec(memory_space=pltpu.VMEM),
         ],
-        out_specs=pl.BlockSpec(memory_space=pltpu.VMEM),
+        out_specs=(pl.BlockSpec(memory_space=pltpu.VMEM),) * groups,
+        scratch_shapes=[pltpu.VMEM((groups * owned, rows, NT), F32)],
         name="stack",
-    )(places, early, late)
+    )(places, corrected)
 
 
 def on_device(
@@ -190,25 +205,18 @@
     low = lax.ppermute(shot_data, "tile", [(i, i + 1) for i in range(tiles - 1)])
     high = lax.ppermute(shot_data, "tile", [(i + 1, i) for i in range(tiles - 1)])
     weights = place_weights(weight_first, weight_middle, weight_last)
-    targets = lax.all_gather(block_target[:, 0], "tile")
-    count = 32
-    owned = count // groups
-    group = lax.axis_index("grp")
-    places = ((targets // owned - group) % groups) * owned + targets % owned
-
-    denoised, early = denoise_block(
-        0, block_offset, low, shot_data, high, weights, moveout_maps, None
-    )
-    early = lax.all_to_all(early, "tile", 0, 0, tiled=True)
-    denoised, late = denoise_block(
-        1, block_offset, low, shot_data, high, weights, moveout_maps, denoised
-    )
-    late = lax.all_to_all(late, "tile", 0, 0, tiled=True)
-    parts = stack(places, early, late, count).reshape(groups, owned, -1, NT)
-    stacked = parts[0]
-    for ahead in range(1, groups):
+    padded = jnp.pad(block_target.reshape(1, 1, -1), ((0, 0), (0, 0), (0, 126)))
+    targets = lax.all_gather(padded, "tile", tiled=True)[:, 0, :2]
+    owned = MBLK // groups
+    ahead = (targets // owned - lax.axis_index("grp")) % groups
+    places = ahead * owned + targets % owned
+
+    denoised, corrected = denoise(block_offset, low, shot_data, high, weights, moveout_maps)
+    corrected = lax.all_to_all(corrected, "tile", 0, 0, tiled=True)
+    stacked, *parts = stack(places, corrected, groups, owned)
+    for ahead, part in enumerate(parts, 1):
         route = [(g, (g + ahead) % groups) for g in range(groups)]
-        stacked = stacked + lax.ppermute(parts[ahead], "grp", route)
+        stacked = stacked + lax.ppermute(part, "grp", route)
     return denoised, stacked
 
 

time: 107 us -> 97.9 us (0.915)
  blocking collectives: 17.3 us -> 23.8 us
  starting transfers between devices: 25.5 us -> 20.3 us
  waiting for transfers between devices: 10.8 us -> 5.62 us
  local copies, waits for them, and re-layouts: 9.33 us -> 4.76 us
    all_gather x0 -> x1, blocking collectives: none -> 23.8 us  [on_device(): targets = lax.all_gather(padded, 'tile', tiled=True)[:, 0, :2]]
    unnamed x1 -> x0, blocking collectives: 17.3 us -> none
    all_to_all x2 -> x1, waiting for transfers between devices: 7.65 us -> 0.01 us  [on_device(): corrected = lax.all_to_all(corrected, 'tile', 0, 0, tiled=True)]
    all_to_all x2 -> x1, starting transfers between devices: 16.3 us -> 12.4 us  [on_device(): corrected = lax.all_to_all(corrected, 'tile', 0, 0, tiled=True)]
    unnamed x19 -> x8, local copies, waits for them, and re-layouts: 5.2 us -> 1.47 us
    ppermute x3, waiting for transfers between devices: 3.19 us -> 5.61 us  [on_device(): stacked = stacked + lax.ppermute(part, 'grp', route)]
    ppermute x3, starting transfers between devices: 6.58 us -> 5.31 us  [on_device(): stacked = stacked + lax.ppermute(part, 'grp', route)]
    pallas_call x3 -> x2, Pallas kernels: 37.9 us -> 37.7 us  [the longest x1 35.7 us: denoise(): pl.pallas_call(denoise_body, out_shape=(jax.ShapeDtypeStruct(own.shape, B...]
  transfers between devices with their start and end apart: 7 -> 6, of which waited for: 3 -> 3; matrix products, arithmetic and copies ran while one was open for 6% -> 6% of each run, Pallas kernels for 0% -> 0%
where the time goes in v2:
time: 97.9 us; the launch traced here: 96.8 us
  Pallas kernels  37.7 us (39%)
  blocking collectives  23.8 us (24%)
  starting transfers between devices  20.3 us (21%)
  waiting for transfers between devices  5.62 us (6%)
  local copies, waits for them, and re-layouts  4.76 us (5%)
  other arithmetic  2.6 us (3%)
  matrix products  1.2 us (1%)
    pallas_call x1, Pallas kernels, denoise(): pl.pallas_call(denoise_body, out_shape=(jax.ShapeDtypeStruct(own.shape, B...  35.7 us
    all_gather x1, blocking collectives, on_device(): targets = lax.all_gather(padded, 'tile', tiled=True)[:, 0, :2]  23.8 us
    all_to_all x1, starting transfers between devices, on_device(): corrected = lax.all_to_all(corrected, 'tile', 0, 0, tiled=True)  12.4 us
    ppermute x3, waiting for transfers between devices, on_device(): stacked = stacked + lax.ppermute(part, 'grp', route)  5.61 us
    ppermute x3, starting transfers between devices, on_device(): stacked = stacked + lax.ppermute(part, 'grp', route)  5.31 us
  transfers between devices with their start and end apart: 6, of which 3 were waited for; matrix products, arithmetic and copies ran while one was open for 6% of the time, Pallas kernels for 0%

profile of v2, /device:TPU:0, one launch (start us, length us, event | category | flops | bytes accessed | tf_op | source)
XLA Modules:
  0.0 96.8 jit_solution(18314276396027022575)
XLA Ops:
  0.6 1.3 %collective-permute-start = (bf16[32,8,512]{2,1,0:T(8,128)(2,1)}, bf16[32,8,512]{2,1,0:T(8,128)(2,1)S(1)}, u32[]{:S(2)}, u32[]{:S(2)}) collective-permute-start(bf16[32,8,512]{2,1,0:T(8,128)(2,1)} %own_ref.1), channel_id=1, source_target_pairs={{0,1},{1,2},{2,3},{3,4},{4,5},{5,6},{6,7},{7,8},{8,9},{9,10},{10,1... | collective-permute-start | bytes 786440 | tf_op jit(solution)/shard_map/ppermute | solution.py:205
  2.0 1.3 %collective-permute-start.1 = (bf16[32,8,512]{2,1,0:T(8,128)(2,1)}, bf16[32,8,512]{2,1,0:T(8,128)(2,1)S(1)}, u32[]{:S(2)}, u32[]{:S(2)}) collective-permute-start(bf16[32,8,512]{2,1,0:T(8,128)(2,1)} %own_ref.1), channel_id=1, source_target_pairs={{1,0},{2,1},{3,2},{4,3},{5,4},{6,5},{7,6},{8,7},{9,8},{10,9},{11,1... | collective-permute-start | bytes 786440 | tf_op jit(solution)/shard_map/ppermute | solution.py:206
  3.3 0.7 reshape.132
  4.7 1.0 %copy.150 = bf16[3,3,64,64]{3,1,0,2:T(4,128)(2,1)S(1)} copy(bf16[3,3,64,64]{3,2,1,0:T(8,128)(2,1)} %bitcast.86) | data formatting | bytes 147456 | tf_op jit(solution)/shard_map/reshape | solution.py:150
  5.8 0.2 pad_bitcast_fusion.1
  6.0 0.2 stack.108
  6.3 0.3 pad_maximum_fusion
  6.7 0.3 reshape.131.middle_ref
  6.9 0.1 stack.87
  7.0 1.2 %fusion = bf16[12,2,96,64]{2,3,1,0:T(8,128)(2,1)S(1)} fusion(bf16[12,2,96,9]{2,3,1,0:T(8,128)(2,1)} %constant.133.clone, f32[12]{0:T(128)S(1)} %stack.87, bf16[9,64]{1,0:T(8,128)(2,1)S(1)} %copy-done), kind=kOutput, calls=%fused_computation.1 | convolution fusion | flops 2949120 | bytes 337584 | tf_op jit(solution)/shard_map/rpkn,nc->rpck/dot_general | solution.py:146
  8.3 0.6 copy-done.1
  8.9 35.7 %denoise.1 = (bf16[32,8,512]{2,1,0:T(8,128)(2,1)}, f32[32,8,512]{2,1,0:T(8,128)}) custom-call(s32[2]{0:T(128)S(1)} %copy-done.1, bf16[32,8,512]{2,1,0:T(8,128)(2,1)S(1)} %collective-permute-done.low_ref, bf16[32,8,512]{2,1,0:T(8,128)(2,1)} %own_ref.1, bf16[32,8,512]{2,1,0:T(8,128)(2,1)S(1)} %collective-permute-done.1.high_ref, ...), custom_call_target="tpu_custom_call" | custom-call | flops 9965666304 | bytes 8388608 | tf_op jit(solution)/shard_map/denoise/pallas_call | solution.py:106
  44.7 12.4 %all-to-all-start = ((f32[32,8,512]{2,1,0:T(8,128)}), f32[32,8,512]{2,1,0:T(8,128)S(1)}, u32[]{:S(2)}, u32[]{:S(2)}) async-start(f32[32,8,512]{2,1,0:T(8,128)} %get-tuple-element.21), calls=%async_computation | async-start | bytes 1048576 | tf_op jit(solution)/shard_map/all_to_all | solution.py:215
  57.1 23.8 %all_gather.3 = s32[32,1,128]{2,1,0:T(1,128)S(1)} all-gather(s32[1,1,128]{2,1,0:T(1,128)S(1)} %pad.59), channel_id=1, replica_groups=mesh['grp'=4,'tile'=32] {'tile'}, dimensions={0}, use_global_device_ids=true | all-gather | bytes 16896 | tf_op jit(solution)/shard_map/all_gather | solution.py:209
  80.9 0.1 copy.138
  81.0 0.6 fusion.5.place_ref
  81.7 0.8 copy-done.2
  82.5 1.9 %stack.116 = (f32[8,4,512]{2,1,0:T(4,128)}, f32[8,4,512]{2,1,0:T(4,128)}, f32[8,4,512]{2,1,0:T(4,128)}, f32[8,4,512]{2,1,0:T(4,128)}) custom-call(s32[32,2]{1,0:T(8,128)} %fusion.5.place_ref, f32[32,8,512]{2,1,0:T(8,128)} %copy-done.2), custom_call_target="tpu_custom_call" | custom-call | tf_op jit(solution)/shard_map/stack/pallas_call | solution.py:188
  84.4 4.0 %collective-permute-start.4 = (f32[8,4,512]{2,1,0:T(4,128)}, f32[8,4,512]{2,1,0:T(4,128)S(1)}, u32[]{:S(2)}, u32[]{:S(2)}) collective-permute-start(f32[8,4,512]{2,1,0:T(4,128)} %get-tuple-element.25), channel_id=1, source_target_pairs={{0,96},{32,0},{64,32},{96,64},{1,97},{33,1},{65,33},{97,65},{2,98}... | collective-permute-start | bytes 196616 | tf_op jit(solution)/shard_map/ppermute | solution.py:219
  88.4 1.3 %collective-permute-start.2 = (f32[8,4,512]{2,1,0:T(4,128)}, f32[8,4,512]{2,1,0:T(4,128)S(1)}, u32[]{:S(2)}, u32[]{:S(2)}) collective-permute-start(f32[8,4,512]{2,1,0:T(4,128)} %get-tuple-element.23), channel_id=1, source_target_pairs={{0,32},{32,64},{64,96},{96,0},{1,33},{33,65},{65,97},{97,1},{2,34}... | collective-permute-start | bytes 196616 | tf_op jit(solution)/shard_map/ppermute | solution.py:219
  89.7 2.3 %collective-permute-done.4 = f32[8,4,512]{2,1,0:T(4,128)S(1)} collective-permute-done((f32[8,4,512]{2,1,0:T(4,128)}, f32[8,4,512]{2,1,0:T(4,128)S(1)}, u32[]{:S(2)}, u32[]{:S(2)}) %collective-permute-start.4) | collective-permute-done | bytes 65568 | tf_op jit(solution)/shard_map/ppermute | solution.py:219
  92.0 2.9 %collective-permute-done.3 = f32[8,4,512]{2,1,0:T(4,128)S(1)} collective-permute-done((f32[8,4,512]{2,1,0:T(4,128)}, f32[8,4,512]{2,1,0:T(4,128)S(1)}, u32[]{:S(2)}, u32[]{:S(2)}) %collective-permute-start.3) | collective-permute-done | bytes 65568 | tf_op jit(solution)/shard_map/ppermute | solution.py:219
  94.9 0.4 collective-permute-done.2
  95.3 1.5 %add_add_fusion = f32[4,8,512]{2,1,0:T(8,128)} fusion(f32[4,8,512]{2,1,0:T(8,128)S(1)} %bitcast.88, f32[4,8,512]{2,1,0:T(8,128)S(1)} %bitcast.89, f32[4,8,512]{2,1,0:T(8,128)} %bitcast.87, f32[4,8,512]{2,1,0:T(8,128)S(1)} %bitcast.90), kind=kLoop, calls=%fused_computation.8 | loop fusion | flops 49152 | bytes 327680 | tf_op jit(solution)/shard_map/add | solution.py:219
  (36 shorter events, 0.8 us)
Async XLA Ops:
  0.6 6.4 %copy-start = (bf16[9,64]{1,0:T(8,128)(2,1)S(1)}, bf16[9,64]{1,0:T(8,128)(2,1)}, u32[]{:S(2)}) copy-start(bf16[9,64]{1,0:T(8,128)(2,1)} %param.11) | copy-start | bytes 3460
  0.6 7.6 %collective-permute-start = (bf16[32,8,512]{2,1,0:T(8,128)(2,1)}, bf16[32,8,512]{2,1,0:T(8,128)(2,1)S(1)}, u32[]{:S(2)}, u32[]{:S(2)}) collective-permute-start(bf16[32,8,512]{2,1,0:T(8,128)(2,1)} %own_ref.1), channel_id=1, source_target_pairs={{0,1},{1,2},{2,3},{3,4},{4,5},{5,6},{6,7},{7,8},{8,9},{9,10},{10,1... | collective-permute-start | bytes 786440 | tf_op jit(solution)/shard_map/ppermute | solution.py:205
  2.0 6.3 %collective-permute-start.1 = (bf16[32,8,512]{2,1,0:T(8,128)(2,1)}, bf16[32,8,512]{2,1,0:T(8,128)(2,1)S(1)}, u32[]{:S(2)}, u32[]{:S(2)}) collective-permute-start(bf16[32,8,512]{2,1,0:T(8,128)(2,1)} %own_ref.1), channel_id=1, source_target_pairs={{1,0},{2,1},{3,2},{4,3},{5,4},{6,5},{7,6},{8,7},{9,8},{10,9},{11,1... | collective-permute-start | bytes 786440 | tf_op jit(solution)/shard_map/ppermute | solution.py:206
  8.3 0.7 copy-start.1
  8.9 48.1 %copy-start.3 = (s32[2,1]{0,1:T(1,128)S(1)}, s32[2,1]{0,1:T(1,128)}, u32[]{:S(2)}) copy-start(s32[2,1]{0,1:T(1,128)} %param.16) | copy-start | bytes 28
  44.7 37.0 %all-to-all-start = ((f32[32,8,512]{2,1,0:T(8,128)}), f32[32,8,512]{2,1,0:T(8,128)S(1)}, u32[]{:S(2)}, u32[]{:S(2)}) async-start(f32[32,8,512]{2,1,0:T(8,128)} %get-tuple-element.21), calls=%async_computation | async-start | bytes 1048576 | tf_op jit(solution)/shard_map/all_to_all | solution.py:215
  81.7 0.8 copy-start.2
  84.4 7.6 %collective-permute-start.4 = (f32[8,4,512]{2,1,0:T(4,128)}, f32[8,4,512]{2,1,0:T(4,128)S(1)}, u32[]{:S(2)}, u32[]{:S(2)}) collective-permute-start(f32[8,4,512]{2,1,0:T(4,128)} %get-tuple-element.25), channel_id=1, source_target_pairs={{0,96},{32,0},{64,32},{96,64},{1,97},{33,1},{65,33},{97,65},{2,98}... | collective-permute-start | bytes 196616 | tf_op jit(solution)/shard_map/ppermute | solution.py:219
  88.4 6.5 %collective-permute-start.3 = (f32[8,4,512]{2,1,0:T(4,128)}, f32[8,4,512]{2,1,0:T(4,128)S(1)}, u32[]{:S(2)}, u32[]{:S(2)}) collective-permute-start(f32[8,4,512]{2,1,0:T(4,128)} %get-tuple-element.24), channel_id=1, source_target_pairs={{0,64},{32,96},{64,0},{96,32},{1,65},{33,97},{65,1},{97,33},{2,66}... | collective-permute-start | bytes 196616 | tf_op jit(solution)/shard_map/ppermute | solution.py:219
  88.4 6.9 %collective-permute-start.2 = (f32[8,4,512]{2,1,0:T(4,128)}, f32[8,4,512]{2,1,0:T(4,128)S(1)}, u32[]{:S(2)}, u32[]{:S(2)}) collective-permute-start(f32[8,4,512]{2,1,0:T(4,128)} %get-tuple-element.23), channel_id=1, source_target_pairs={{0,32},{32,64},{64,96},{96,0},{1,33},{33,65},{65,97},{97,1},{2,34}... | collective-permute-start | bytes 196616 | tf_op jit(solution)/shard_map/ppermute | solution.py:219

commit v3 on v0

v3 whole, which is shorter than its diff:
```python
import jax
import jax.numpy as jnp
from jax import lax
from jax.experimental import pallas as pl
from jax.experimental.pallas import tpu as pltpu
from jax.sharding import PartitionSpec as P

CH = 64
RD = 8
SH = 32
NT = 512
OB = 8
BLK = 128
MBLK = 32
LANES = 128
UNIT = 256
UNITS = 2
HALF = NT // 2
OUTER = RD + 4
INNER = RD + 2
F32 = jnp.float32
BF16 = jnp.bfloat16


def at_lane(shape, lane):
    return lax.broadcasted_iota(jnp.int32, shape, 1) % HALF == lane


def delayed(rows):
    return jnp.where(at_lane(rows.shape, 0), jnp.zeros_like(rows), pltpu.roll(rows, 1, 1))


def advanced(rows):
    last = rows.shape[1] - 1
    return jnp.where(at_lane(rows.shape, HALF - 1), jnp.zeros_like(rows), pltpu.roll(rows, last, 1))


def one_hot(condition):
    return condition.astype(F32).astype(BF16)


def prepare_body(tap1_ref, tap2_ref, tap3_ref, own_ref, first_ref, middle_ref, last_ref, split_ref, slots_ref, wide):
    tile = lax.axis_index("tile")
    low = (tile > 0).astype(F32)
    high = (tile < lax.axis_size("tile") - 1).astype(F32)

    shape = (9, UNIT)
    tap = lax.broadcasted_iota(jnp.int32, shape, 0)
    column = lax.broadcasted_iota(jnp.int32, shape, 1)
    across = column // 32 * RD + column % RD - RD + 3
    delay = column // RD % 4
    for receiver in range(OUTER):
        inside = low if receiver < 2 else high if receiver >= OUTER - 2 else None
        for phase in range(2):
            a, d = across - receiver, delay - phase
            place = (tap == 3 * a + d) & (a >= 0) & (a <= 2) & (d >= 0) & (d <= 2) & (column < 96)
            place = place.astype(F32)
            if inside is not None:
                place = place * inside
            block = lax.dot_general(
                tap1_ref[...], place.astype(BF16), (((0,), (0,)), ((), ())), preferred_element_type=F32
            )
            row = (2 * receiver + phase) * CH
            first_ref[row : row + CH, :] = block.astype(BF16)

    none = jnp.zeros((CH, CH), BF16)
    for across in range(3):
        taps = [tap2_ref[(3 * across + d) * CH : (3 * across + d + 1) * CH, :] for d in range(3)]
        lanes = slice(across * UNIT, (across + 1) * UNIT)
        middle_ref[:CH, lanes] = jnp.concatenate([*taps, none], axis=1)
        middle_ref[CH:, lanes] = jnp.concatenate([none, *taps], axis=1)

    none = jnp.zeros((1, CH), F32)
    taps = [tap3_ref[k : k + 1, :].astype(F32) for k in range(9)]
    kinds = [
        [taps[3 * a + 1] for a in range(3)], [taps[3 * a + 2] for a in range(3)],
        [taps[3 * a] for a in range(3)], [taps[3 * a + 1] for a in range(3)],
        [none] * 3, [taps[3 * a] for a in range(3)],
        [taps[3 * a + 2] for a in range(3)], [none] * 3,
    ]
    wide[...] = jnp.zeros_like(wide)
    for kind in range(4):
        row = [t for pair in zip(kinds[2 * kind], kinds[2 * kind + 1]) for t in pair]
        row = jnp.concatenate(row, axis=1)
        for receiver in range(RD):
            at = kind * RD + receiver
            wide[at : at + 1, receiver * 2 * CH : (receiver + 3) * 2 * CH] = row
    wide[:, : 2 * CH] = wide[:, : 2 * CH] * low
    wide[:, (INNER - 1) * 2 * CH :] = wide[:, (INNER - 1) * 2 * CH :] * high
    last_ref[...] = wide[...].astype(BF16)

    time = lax.broadcasted_iota(jnp.int32, (NT, 4 * HALF), 0)
    lane = lax.broadcasted_iota(jnp.int32, (NT, 4 * HALF), 1)
    split = one_hot(time == 2 * (lane % HALF) + lane // HALF - 1)
    split_ref[...] = split
    shots = own_ref.shape[0]
    taken = jnp.dot(own_ref[...].reshape(shots * RD, NT), split, preferred_element_type=F32)
    parts = [taken[:, s * HALF : (s + 1) * HALF].reshape(shots, RD, HALF) for s in range(4)]
    slots_ref[...] = jnp.concatenate(parts, axis=1).astype(BF16)


def prepare(weight_first, weight_middle, weight_last, own):
    shapes = (
        (OUTER * 2 * CH, UNIT),
        (2 * CH, 3 * UNIT),
        (4 * RD, INNER * 2 * CH),
        (NT, 4 * HALF),
        (own.shape[0], 4 * RD, HALF),
    )
    return pl.pallas_call(
        prepare_body,
        out_shape=tuple(jax.ShapeDtypeStruct(s, BF16) for s in shapes),
        scratch_shapes=[pltpu.VMEM(shapes[2], F32)],
        compiler_params=pltpu.CompilerParams(vmem_limit_bytes=24 << 20),
        name="prepare",
    )(weight_first, weight_middle.reshape(9 * CH, CH), weight_last, own)


def product(accs, lhs, rhs, use):
    rows, depth = lhs.shape
    for n in range(rhs.shape[1] // UNIT):
        held = accs[n % UNITS]
        for k in range(depth // UNIT):
            piece = rhs[k * UNIT : (k + 1) * UNIT, n * UNIT : (n + 1) * UNIT]
            pltpu.matmul_push_rhs(piece, k % 2, n % UNITS)
            for c in range(rows // BLK):
                piece = lhs[c * BLK : (c + 1) * BLK, k * UNIT : (k + 1) * UNIT]
                pltpu.matmul_acc_lhs(held[c], piece, load_staged_rhs=k % 2 if c == 0 else None)
        for c in range(rows // BLK):
            use(n, c, pltpu.matmul_pop(held[c]))


def run(jobs):
    def push(number):
        for unit in range(UNITS):
            pltpu.matmul_push_rhs(jobs[number][0](unit), number % 2, unit)

    push(0)
    for number, (_, products, after) in enumerate(jobs):
        if number + 1 < len(jobs):
            push(number + 1)
        for n, (acc, lhs) in enumerate(products):
            for unit in range(UNITS):
                staged = number % 2 if n == 0 else None
                pltpu.matmul_acc_lhs(acc(unit), lhs(), load_staged_rhs=staged)
        for act in after:
            act()


def denoise_loop(
    offset_ref, target_ref, low_ref, high_ref, own, first_ref, middle_ref, last_ref, split_ref,
    denoised_ref, sent_ref, low, high, h1_even, h1_odd, h2_even, h2_odd, cleaned, rows4, accs,
):
    shots = own.shape[0]
    pairs = shots // UNITS
    per_block = BLK // RD

    for ref, held in ((low_ref, low), (high_ref, high)):
        def put(slot, c, part, held=held):
            part = part.astype(BF16).reshape(per_block, RD, HALF)
            held[c * per_block : (c + 1) * per_block, slot * RD : (slot + 1) * RD, :] = part

        product(accs, ref[...].reshape(shots * RD, NT), split_ref, put)

    def taps(pair):
        def right(unit):
            shot = pair * UNITS + unit
            rest = jnp.zeros((UNIT - 12 * RD, HALF), BF16)
            return jnp.concatenate([low[shot], own[shot], high[shot], rest], axis=0)

        return right

    def first_done(h1, receiver):
        def act():
            for unit in range(UNITS):
                both = jnp.maximum(pltpu.matmul_pop(accs[unit][receiver % 3]), 0.0).astype(BF16)
                h1[unit, receiver, CH : 3 * CH, :] = both
                h1[unit, receiver, :CH, :] = delayed(both[CH:])
                h1[unit, receiver, 3 * CH :, :] = advanced(both[:CH])

        return act

    def middle_done(h2, receiver):
        def act():
            for unit in range(UNITS):
                both = jnp.maximum(pltpu.matmul_pop(accs[unit][3 + receiver % 4]), 0.0)
                h2[unit, receiver * 2 * CH : (receiver + 1) * 2 * CH, :] = both.astype(BF16)

        return act

    def last_done(pair):
        def act():
            for unit in range(UNITS):
                shot = pair * UNITS + unit
                parts = pltpu.matmul_pop(accs[unit][7])
                seen = own[shot].astype(F32)
                rows = pl.ds(pl.multiple_of(shot * RD, RD), RD)
                even = parts[:RD] + delayed(parts[2 * RD : 3 * RD])
                odd = parts[RD : 2 * RD] + advanced(parts[3 * RD :])
                cleaned[rows, :HALF] = seen[RD : 2 * RD] - even
                cleaned[rows, HALF:] = seen[2 * RD : 3 * RD] - odd

        return act

    def first_job(pair, receivers):
        products = [
            (
                lambda unit, r=r: accs[unit][r % 3],
                lambda r=r: first_ref[r * 2 * CH : (r + 1) * 2 * CH, :],
            )
            for r in receivers
        ]
        return taps(pair), products, []

    def middle_job(h1, receiver):
        products = [
            (
                lambda unit, r=receiver - across: accs[unit][3 + r % 4],
                lambda across=across: middle_ref[:, across * UNIT : (across + 1) * UNIT],
            )
            for across in (2, 1, 0)
            if 0 <= receiver - across < INNER
        ]
        return lambda unit: h1[unit, receiver], products, []

    def last_job(h2, number):
        lanes = slice(number * UNIT, (number + 1) * UNIT)
        products = [(lambda unit: accs[unit][7], lambda: last_ref[:, lanes])]
        return lambda unit: h2[unit, lanes, :], products, []

    def stage(now, later, before):
        jobs = []
        for r in range(OUTER):
            if later and r % 3 == 0:
                jobs.append(first_job(later[0], range(r, r + 3)))
            if now:
                jobs.append(middle_job(now[0], r))
            if later:
                jobs[-1][2].append(first_done(later[1], r))
            if now and r >= 3:
                jobs[-1][2].append(middle_done(now[1], r - 3))
            if before and r % 2 == 1 and r < INNER:
                jobs.append(last_job(before[1], r // 2))
            if before and r == INNER:
                jobs[-1][2].append(last_done(before[0]))
        return jobs, [middle_done(now[1], INNER - 1)] if now else []

    def chain(*stages):
        jobs, tail = [], []
        for more, end in stages:
            more[0][2].extend(tail)
            jobs, tail = jobs + more, end
        jobs[-1][2].extend(tail)
        run(jobs)

    chain(stage(None, (0, h1_even), None))
    chain(stage((h1_even, h2_even), (1, h1_odd), None))

    def two(step, carry):
        pair = 2 * step + 1
        chain(
            stage((h1_odd, h2_odd), (pair + 1, h1_even), (pair - 1, h2_even)),
            stage((h1_even, h2_even), (pair + 2, h1_odd), (pair, h2_odd)),
        )
        return carry

    lax.fori_loop(0, (pairs - 2) // 2, two, 0)
    chain(stage((h1_odd, h2_odd), None, (pairs - 2, h2_even)))
    chain(([last_job(h2_odd, n) for n in range(INNER // 2)], [last_done(pairs - 1)]))

    lane = lax.broadcasted_iota(jnp.int32, (NT, NT), 0)
    time = lax.broadcasted_iota(jnp.int32, (NT, NT), 1)
    merge = one_hot(time == 2 * (lane % HALF) + lane // HALF)
    owners = sent_ref.shape[0]
    kept = BLK // owners

    def put(n, c, part):
        lanes = slice(n * UNIT, (n + 1) * UNIT)
        shot = slice(c * per_block, (c + 1) * per_block)
        denoised_ref[shot, :, lanes] = part.astype(BF16).reshape(per_block, RD, UNIT)
        rows4[:, c * kept : (c + 1) * kept, lanes] = part.reshape(owners, kept, UNIT)

    product(accs, cleaned[...].astype(BF16), merge, put)
    shape = (owners, kept, LANES // 2)
    for c in range(shots * RD // BLK):
        rows4[:, c * kept : (c + 1) * kept, NT : NT + LANES // 2] = jnp.full(shape, target_ref[c].astype(F32))
        rows4[:, c * kept : (c + 1) * kept, NT + LANES // 2 :] = jnp.full(shape, offset_ref[c].astype(F32))
    sent_ref[...] = rows4[...].astype(BF16)


def denoise_body(*refs):
    pl.run_scoped(
        lambda *accs: denoise_loop(*refs, (accs[:8], accs[8:])),
        *[
            pltpu.ACC(unit)((BLK if number < 7 else 4 * RD, UNIT), F32)
            for unit in range(UNITS)
            for number in range(8)
        ],
    )


def denoise(offsets, targets, low, high, slots, first, middle, last, split):
    shots, blocks = low.shape[0], offsets.shape[0]
    owners = lax.axis_size("tile")
    sent = (owners, blocks * BLK // owners, NT + LANES)
    scalars = pl.BlockSpec(memory_space=pltpu.SMEM)
    whole = pl.BlockSpec(memory_space=pltpu.VMEM)
    macs = shots * RD * NT * CH * (9 * CH + 18)
    return pl.pallas_call(
        denoise_body,
        out_shape=(jax.ShapeDtypeStruct((shots, RD, NT), BF16), jax.ShapeDtypeStruct(sent, BF16)),
        in_specs=[scalars] * 2 + [whole] * 7,
        out_specs=(whole, whole),
        scratch_shapes=[pltpu.VMEM((shots, 4 * RD, HALF), BF16)] * 2
        + [pltpu.VMEM((UNITS, OUTER, UNIT, HALF), BF16)] * 2
        + [pltpu.VMEM((UNITS, INNER * 2 * CH, HALF), BF16)] * 2
        + [pltpu.VMEM((shots * RD, NT), F32), pltpu.VMEM(sent, F32)],
        compiler_params=pltpu.CompilerParams(vmem_limit_bytes=40 << 20),
        cost_estimate=pl.CostEstimate(flops=2 * macs, transcendentals=0, bytes_accessed=4 << 20),
        name="denoise",
    )(offsets, targets, low, high, slots, first, middle, last, split)


def stack_body(came_ref, map_ref, *part_refs):
    tiles, kept, _ = came_ref.shape
    rows = kept * BLK // (SH * RD)
    count = tiles * kept
    came = came_ref[...].reshape(count, NT + LANES)
    target = came[:, NT : NT + 1].astype(F32).astype(jnp.int32)
    offset = came[:, NT + LANES // 2 : NT + LANES // 2 + 1].astype(F32)
    traces = came[:, :NT]
    none = jnp.zeros_like(traces)
    wide = [jnp.where(offset == o, traces, none) for o in range(OB)]
    corrected = jnp.dot(
        jnp.concatenate(wide, axis=1), map_ref[...], preferred_element_type=F32
    )
    groups = len(part_refs)
    owned = MBLK // groups
    ahead = (target // owned - lax.axis_index("grp") + groups) % groups
    place = ahead * owned + target % owned
    row = lax.broadcasted_iota(jnp.int32, (count, MBLK * rows), 0) % rows
    column = lax.broadcasted_iota(jnp.int32, (count, MBLK * rows), 1)
    chosen = one_hot((place == column // rows) & (row == column % rows))
    total = None
    for _ in range(3):
        part = corrected.astype(BF16)
        corrected = corrected - part.astype(F32)
        term = lax.dot_general(chosen, part, (((0,), (0,)), ((), ())), preferred_element_type=F32)
        total = term if total is None else total + term
    for number, ref in enumerate(part_refs):
        part = total[number * owned * rows : (number + 1) * owned * rows]
        ref[...] = part.reshape(ref.shape)


def stack(came, moveout_maps, groups):
    rows = came.shape[1] * BLK // (SH * RD)
    part = jax.ShapeDtypeStruct((MBLK // groups, rows, NT), F32)
    return pl.pallas_call(
        stack_body,
        out_shape=(part,) * groups,
        compiler_params=pltpu.CompilerParams(vmem_limit_bytes=40 << 20),
        name="stack",
    )(came, moveout_maps.reshape(OB * NT, NT))


def on_device(
    shot_data, weight_first, weight_middle, weight_last, moveout_maps, block_offset, block_target
):
    tiles, groups = lax.axis_size("tile"), lax.axis_size("grp")
    low = lax.ppermute(shot_data, "tile", [(i, i + 1) for i in range(tiles - 1)])
    high = lax.ppermute(shot_data, "tile", [(i + 1, i) for i in range(tiles - 1)])
    *weights, split, slots = prepare(weight_first, weight_middle, weight_last, shot_data)
    denoised, sent = denoise(
        block_offset, block_target.reshape(-1), low, high, slots, *weights, split
    )
    came = lax.all_to_all(sent, "tile", 0, 0, tiled=True)
    stacked, *parts = stack(came, moveout_maps, groups)
    for ahead, part in enumerate(parts, 1):
        route = [(g, (g + ahead) % groups) for g in range(groups)]
        stacked = stacked + lax.ppermute(part, "grp", route)
    return denoised, stacked


def solution(mesh):
    in_specs = (
        P("grp", "tile", None),
        P(),
        P(),
        P(),
        P(),
        P(("grp", "tile")),
        P(("grp", "tile"), None),
    )
    out_specs = (P("grp", "tile", None), P("grp", "tile", None))
    return jax.shard_map(
        on_device, mesh=mesh, in_specs=in_specs, out_specs=out_specs, check_vma=False
    )
```

time: 686 us -> 71.7 us (0.10)
  matrix products: 187 us -> 0 us
  local copies, waits for them, and re-layouts: 179 us -> 4.53 us
  waiting for transfers between devices: 154 us -> 3.26 us
  other arithmetic: 118 us -> 0.65 us
  Pallas kernels: 0 us -> 30.5 us
  starting transfers between devices: 33.5 us -> 9.17 us
  blocking collectives: 0 us -> 22.6 us
  between operations: 14.3 us -> 0.7 us
    dot_general x11 -> x0, matrix products: 187 us -> none  [the longest x9 180 us: convolve(): jnp.einsum('srdct,doc->srot', window, kernel[3 * across:3 * across + 3],...]
    reduce_scatter x2 -> x0, waiting for transfers between devices: 144 us -> none  [the longest x1 122 us: on_device(): lax.psum_scatter(spread_blocks, 'tile', scatter_dimension=1, tiled=True)]
    slice x5 -> x0, local copies, waits for them, and re-layouts: 102 us -> none  [the longest x1 96.9 us: convolve(): window = delayed[:, across:across + breadth]]
    another operation x5 -> x0, other arithmetic: 85.5 us -> none  [convolve(): jnp.stack([padded[:, :, :, delay:delay + length] for delay in range(3)],...]
    another operation x6 -> x0, local copies, waits for them, and re-layouts: 61 us -> none  [convolve(): jnp.stack([padded[:, :, :, delay:delay + length] for delay in range(3)],...]
    convert_element_type x2 -> x0, other arithmetic: 32.4 us -> none  [the longest x1 32.2 us: on_device(): signal = activated.astype(jnp.bfloat16)]
    pallas_call x0 -> x3, Pallas kernels: none -> 30.5 us  [the longest x1 28 us: denoise(): pl.pallas_call(denoise_body, out_shape=(jax.ShapeDtypeStruct((shots, RD,...]
    ppermute x6 -> x5, starting transfers between devices: 33.4 us -> 9.17 us  [the longest x3 6.57 us: on_device(): stacked = stacked + lax.ppermute(part, 'grp', route)]
  transfers between devices with their start and end apart: 8 -> 5, of which waited for: 6 -> 2; matrix products, arithmetic and copies ran while one was open for 1% -> 0% of each run, Pallas kernels for 0% -> 1%
where the time goes in v3:
time: 71.7 us; the launch traced here: 71.4 us
  Pallas kernels  30.5 us (43%)
  blocking collectives  22.6 us (32%)
  starting transfers between devices  9.17 us (13%)
  local copies, waits for them, and re-layouts  4.53 us (6%)
  waiting for transfers between devices  3.26 us (5%)
    pallas_call x1, Pallas kernels, denoise(): pl.pallas_call(denoise_body, out_shape=(jax.ShapeDtypeStruct((shots, RD,...  28 us
    all_to_all x1, blocking collectives, on_device(): came = lax.all_to_all(sent, 'tile', 0, 0, tiled=True)  22.6 us
    ppermute x3, starting transfers between devices, on_device(): stacked = stacked + lax.ppermute(part, 'grp', route)  6.57 us
    unnamed x14, local copies, waits for them, and re-layouts  4.53 us
    ppermute x3, waiting for transfers between devices, on_device(): stacked = stacked + lax.ppermute(part, 'grp', route)  3.25 us
    pallas_call x1, Pallas kernels, stack(): pl.pallas_call(stack_body, out_shape=(part,) * groups, compiler_params=pl...  1.59 us
  transfers between devices with their start and end apart: 5, of which 2 were waited for; matrix products, arithmetic and copies ran while one was open for 0% of the time, Pallas kernels for 1%

profile of v3, /device:TPU:0, one launch (start us, length us, event | category | flops | bytes accessed | tf_op | source)
XLA Modules:
  0.0 71.4 jit_solution(9455163681105034734)
XLA Ops:
  0.6 1.3 %collective-permute-start = (bf16[32,8,512]{2,1,0:T(8,128)(2,1)}, bf16[32,8,512]{2,1,0:T(8,128)(2,1)S(1)}, u32[]{:S(2)}, u32[]{:S(2)}) collective-permute-start(bf16[32,8,512]{2,1,0:T(8,128)(2,1)} %own_ref.1), channel_id=1, source_target_pairs={{0,1},{1,2},{2,3},{3,4},{4,5},{5,6},{6,7},{7,8},{8,9},{9,10},{10,1... | collective-permute-start | bytes 786440 | tf_op jit(solution)/shard_map/ppermute | solution.py:370
  1.9 1.3 %collective-permute-start.1 = (bf16[32,8,512]{2,1,0:T(8,128)(2,1)}, bf16[32,8,512]{2,1,0:T(8,128)(2,1)S(1)}, u32[]{:S(2)}, u32[]{:S(2)}) collective-permute-start(bf16[32,8,512]{2,1,0:T(8,128)(2,1)} %own_ref.1), channel_id=1, source_target_pairs={{1,0},{2,1},{3,2},{4,3},{5,4},{6,5},{7,6},{8,7},{9,8},{10,9},{11,1... | collective-permute-start | bytes 786440 | tf_op jit(solution)/shard_map/ppermute | solution.py:371
  3.2 0.0 copy-start.1
  3.3 0.9 %copy-done.1 = bf16[32,8,512]{2,1,0:T(8,128)(2,1)S(1)} copy-done((bf16[32,8,512]{2,1,0:T(8,128)(2,1)S(1)}, bf16[32,8,512]{2,1,0:T(8,128)(2,1)}, u32[]{:S(2)}) %copy-start.1) | copy-done | bytes 262168
  4.2 0.9 %copy-done.2 = bf16[1,9,64,64]{3,2,1,0:T(8,128)(2,1)S(1)} copy-done((bf16[1,9,64,64]{3,2,1,0:T(8,128)(2,1)S(1)}, bf16[1,9,64,64]{3,2,1,0:T(8,128)(2,1)}, u32[]{:S(2)}) %copy-start.2) | copy-done | bytes 73752
  5.1 0.7 copy-done.3
  5.8 0.7 copy-done.4
  6.5 0.9 %prepare.1 = (bf16[1536,256]{1,0:T(8,128)(2,1)S(1)}, bf16[128,768]{1,0:T(8,128)(2,1)S(1)}, bf16[32,1280]{1,0:T(8,128)(2,1)S(1)}, bf16[512,1024]{1,0:T(8,128)(2,1)S(1)}, bf16[32,32,256]{2,1,0:T(8,128)(2,1)S(1)}) custom-call(bf16[9,64]{1,0:T(8,128)(2,1)S(1)} %copy-done.3, bf16[576,64]{1,0:T(8,128)(2,1)S(1)} %bitcast.9, bf16[9,64]{1,0:T(8,128)(2,1)S(1)} %copy-done.4, ...), custom_call_target="tpu_custom_call" | custom-call | tf_op jit(solution)/shard_map/prepare/pallas_call | solution.py:110
  7.4 0.0 collective-permute-done.refs_2_
  7.4 0.0 collective-permute-done.1.refs_3_
  7.4 0.0 copy-start.5
  7.4 0.6 copy-done.5
  8.1 0.7 copy-done.6
  8.7 28.0 %denoise.1 = (bf16[32,8,512]{2,1,0:T(8,128)(2,1)}, bf16[32,8,640]{2,1,0:T(8,128)(2,1)S(1)}) custom-call(s32[2]{0:T(128)S(1)} %copy-done.5, s32[2]{0:T(128)S(1)} %bitcast.11, bf16[32,8,512]{2,1,0:T(8,128)(2,1)S(1)} %collective-permute-done.refs_2_, bf16[32,8,512]{2,1,0:T(8,128)(2,1)S(1)} %collective-permute-done.1.refs_3_, ...), custom_call_target="tpu_custom_call" | custom-call | flops 9965666304 | bytes 4194304 | tf_op jit(solution)/shard_map/denoise/pallas_call | solution.py:309
  36.7 22.6 %all_to_all.5.came_ref = bf16[32,8,640]{2,1,0:T(8,128)(2,1)S(1)} all-to-all(bf16[32,8,640]{2,1,0:T(8,128)(2,1)S(1)} %get-tuple-element.19), channel_id=1, replica_groups=mesh['grp'=4,'tile'=32] {'tile'}, dimensions={0} | all-to-all | bytes 655360 | tf_op jit(solution)/shard_map/all_to_all | solution.py:376
  59.3 0.0 copy-done
  59.3 1.6 %stack.1 = (f32[8,4,512]{2,1,0:T(4,128)S(1)}, f32[8,4,512]{2,1,0:T(4,128)S(1)}, f32[8,4,512]{2,1,0:T(4,128)S(1)}, f32[8,4,512]{2,1,0:T(4,128)S(1)}) custom-call(bf16[32,8,640]{2,1,0:T(8,128)(2,1)S(1)} %all_to_all.5.came_ref, bf16[4096,512]{1,0:T(8,128)(2,1)S(1)} %bitcast.8), custom_call_target="tpu_custom_call" | custom-call | tf_op jit(solution)/shard_map/stack/pallas_call | solution.py:358
  60.9 2.0 %collective-permute-start.2 = (f32[8,4,512]{2,1,0:T(4,128)S(1)}, f32[8,4,512]{2,1,0:T(4,128)S(1)}, u32[]{:S(2)}, u32[]{:S(2)}) collective-permute-start(f32[8,4,512]{2,1,0:T(4,128)S(1)} %get-tuple-element.21), channel_id=1, source_target_pairs={{0,32},{32,64},{64,96},{96,0},{1,33},{33,65},{65,97},{97,1},{2,34}... | collective-permute-start | bytes 196616 | tf_op jit(solution)/shard_map/ppermute | solution.py:380
  62.9 3.6 %collective-permute-start.3 = (f32[8,4,512]{2,1,0:T(4,128)S(1)}, f32[8,4,512]{2,1,0:T(4,128)S(1)}, u32[]{:S(2)}, u32[]{:S(2)}) collective-permute-start(f32[8,4,512]{2,1,0:T(4,128)S(1)} %get-tuple-element.22), channel_id=1, source_target_pairs={{0,64},{32,96},{64,0},{96,32},{1,65},{33,97},{65,1},{97,33},{2,66}... | collective-permute-start | bytes 196616 | tf_op jit(solution)/shard_map/ppermute | solution.py:380
  66.5 1.0 %collective-permute-start.4 = (f32[8,4,512]{2,1,0:T(4,128)S(1)}, f32[8,4,512]{2,1,0:T(4,128)S(1)}, u32[]{:S(2)}, u32[]{:S(2)}) collective-permute-start(f32[8,4,512]{2,1,0:T(4,128)S(1)} %get-tuple-element.23), channel_id=1, source_target_pairs={{0,96},{32,0},{64,32},{96,64},{1,97},{33,1},{65,33},{97,65},{2,98}... | collective-permute-start | bytes 196616 | tf_op jit(solution)/shard_map/ppermute | solution.py:380
  67.5 0.0 collective-permute-done.2
  67.5 2.6 %collective-permute-done.3 = f32[8,4,512]{2,1,0:T(4,128)S(1)} collective-permute-done((f32[8,4,512]{2,1,0:T(4,128)S(1)}, f32[8,4,512]{2,1,0:T(4,128)S(1)}, u32[]{:S(2)}, u32[]{:S(2)}) %collective-permute-start.3) | collective-permute-done | bytes 65568 | tf_op jit(solution)/shard_map/ppermute | solution.py:380
  70.1 0.7 collective-permute-done.4
  70.7 0.6 add_add_fusion
  (5 shorter events, 0.0 us)
Async XLA Ops:
  0.6 6.8 %collective-permute-start = (bf16[32,8,512]{2,1,0:T(8,128)(2,1)}, bf16[32,8,512]{2,1,0:T(8,128)(2,1)S(1)}, u32[]{:S(2)}, u32[]{:S(2)}) collective-permute-start(bf16[32,8,512]{2,1,0:T(8,128)(2,1)} %own_ref.1), channel_id=1, source_target_pairs={{0,1},{1,2},{2,3},{3,4},{4,5},{5,6},{6,7},{7,8},{8,9},{9,10},{10,1... | collective-permute-start | bytes 786440 | tf_op jit(solution)/shard_map/ppermute | solution.py:370
  1.9 5.5 %collective-permute-start.1 = (bf16[32,8,512]{2,1,0:T(8,128)(2,1)}, bf16[32,8,512]{2,1,0:T(8,128)(2,1)S(1)}, u32[]{:S(2)}, u32[]{:S(2)}) collective-permute-start(bf16[32,8,512]{2,1,0:T(8,128)(2,1)} %own_ref.1), channel_id=1, source_target_pairs={{1,0},{2,1},{3,2},{4,3},{5,4},{6,5},{7,6},{8,7},{9,8},{10,9},{11,1... | collective-permute-start | bytes 786440 | tf_op jit(solution)/shard_map/ppermute | solution.py:371
  3.2 1.0 %copy-start.1 = (bf16[32,8,512]{2,1,0:T(8,128)(2,1)S(1)}, bf16[32,8,512]{2,1,0:T(8,128)(2,1)}, u32[]{:S(2)}) copy-start(bf16[32,8,512]{2,1,0:T(8,128)(2,1)} %own_ref.1) | copy-start | bytes 786436
  4.2 0.9 %copy-start.2 = (bf16[1,9,64,64]{3,2,1,0:T(8,128)(2,1)S(1)}, bf16[1,9,64,64]{3,2,1,0:T(8,128)(2,1)}, u32[]{:S(2)}) copy-start(bf16[1,9,64,64]{3,2,1,0:T(8,128)(2,1)} %param.9) | copy-start | bytes 221188
  5.1 0.7 copy-start.3
  5.8 0.7 copy-start.4
  7.4 0.7 copy-start.5
  8.1 0.7 copy-start.6
  8.7 50.6 %copy-start = (bf16[8,512,512]{2,1,0:T(8,128)(2,1)S(1)}, bf16[8,512,512]{2,1,0:T(8,128)(2,1)}, u32[]{:S(2)}) copy-start(bf16[8,512,512]{2,1,0:T(8,128)(2,1)} %param.11) | copy-start | bytes 12582916
  60.9 6.6 %collective-permute-start.2 = (f32[8,4,512]{2,1,0:T(4,128)S(1)}, f32[8,4,512]{2,1,0:T(4,128)S(1)}, u32[]{:S(2)}, u32[]{:S(2)}) collective-permute-start(f32[8,4,512]{2,1,0:T(4,128)S(1)} %get-tuple-element.21), channel_id=1, source_target_pairs={{0,32},{32,64},{64,96},{96,0},{1,33},{33,65},{65,97},{97,1},{2,34}... | collective-permute-start | bytes 196616 | tf_op jit(solution)/shard_map/ppermute | solution.py:380
  62.9 7.2 %collective-permute-start.3 = (f32[8,4,512]{2,1,0:T(4,128)S(1)}, f32[8,4,512]{2,1,0:T(4,128)S(1)}, u32[]{:S(2)}, u32[]{:S(2)}) collective-permute-start(f32[8,4,512]{2,1,0:T(4,128)S(1)} %get-tuple-element.22), channel_id=1, source_target_pairs={{0,64},{32,96},{64,0},{96,32},{1,65},{33,97},{65,1},{97,33},{2,66}... | collective-permute-start | bytes 196616 | tf_op jit(solution)/shard_map/ppermute | solution.py:380
  66.5 4.3 %collective-permute-start.4 = (f32[8,4,512]{2,1,0:T(4,128)S(1)}, f32[8,4,512]{2,1,0:T(4,128)S(1)}, u32[]{:S(2)}, u32[]{:S(2)}) collective-permute-start(f32[8,4,512]{2,1,0:T(4,128)S(1)} %get-tuple-element.23), channel_id=1, source_target_pairs={{0,96},{32,0},{64,32},{96,64},{1,97},{33,1},{65,33},{97,65},{2,98}... | collective-permute-start | bytes 196616 | tf_op jit(solution)/shard_map/ppermute | solution.py:380

commit v4 on v3

--- a/solution.py
+++ b/solution.py
@@ -113,7 +113,7 @@
         scratch_shapes=[pltpu.VMEM(shapes[2], F32)],
         compiler_params=pltpu.CompilerParams(vmem_limit_bytes=24 << 20),
         name="prepare",
-    )(weight_first, weight_middle.reshape(9 * CH, CH), weight_last, own)
+    )(weight_first, weight_middle, weight_last, own)
 
 
 def product(accs, lhs, rhs, use):
@@ -367,12 +367,21 @@
     shot_data, weight_first, weight_middle, weight_last, moveout_maps, block_offset, block_target
 ):
     tiles, groups = lax.axis_size("tile"), lax.axis_size("grp")
+    (own, weight_first, weight_middle, weight_last, block_offset, block_target) = (
+        pltpu.with_memory_space_constraint(a, pltpu.HBM)
+        for a in (
+            shot_data,
+            weight_first,
+            weight_middle.reshape(9 * CH, CH),
+            weight_last,
+            block_offset,
+            block_target.reshape(-1),
+        )
+    )
     low = lax.ppermute(shot_data, "tile", [(i, i + 1) for i in range(tiles - 1)])
     high = lax.ppermute(shot_data, "tile", [(i + 1, i) for i in range(tiles - 1)])
-    *weights, split, slots = prepare(weight_first, weight_middle, weight_last, shot_data)
-    denoised, sent = denoise(
-        block_offset, block_target.reshape(-1), low, high, slots, *weights, split
-    )
+    *weights, split, slots = prepare(weight_first, weight_middle, weight_last, own)
+    denoised, sent = denoise(block_offset, block_target, low, high, slots, *weights, split)
     came = lax.all_to_all(sent, "tile", 0, 0, tiled=True)
     stacked, *parts = stack(came, moveout_maps, groups)
     for ahead, part in enumerate(parts, 1):

time: 71.7 us -> 70.5 us (0.983)
  local copies, waits for them, and re-layouts: 4.53 us -> 0.01 us
  waiting for transfers between devices: 3.26 us -> 5.38 us
  Pallas kernels: 30.5 us -> 31.8 us
    unnamed x14 -> x2, local copies, waits for them, and re-layouts: 4.53 us -> 0.01 us
    ppermute x1, waiting for transfers between devices: 0.01 us -> 2.14 us  [on_device(): lax.ppermute(shot_data, 'tile', [(i + 1, i) for i in range(tiles - 1)])]
    pallas_call x1, Pallas kernels: 0.92 us -> 1.98 us  [prepare(): pl.pallas_call(prepare_body, out_shape=tuple((jax.ShapeDtypeStruct(s, BF1...]
  transfers between devices with their start and end apart: 5 -> 5, of which waited for: 2 -> 3; matrix products, arithmetic and copies ran while one was open for 0% -> 0% of each run, Pallas kernels for 1% -> 3%
where the time goes in v4:
time: 70.5 us; the launch traced here: 70.3 us
  Pallas kernels  31.8 us (45%)
  blocking collectives  22.6 us (32%)
  starting transfers between devices  9.19 us (13%)
  waiting for transfers between devices  5.38 us (8%)
    pallas_call x1, Pallas kernels, denoise(): pl.pallas_call(denoise_body, out_shape=(jax.ShapeDtypeStruct((shots, RD,...  28.2 us
    all_to_all x1, blocking collectives, on_device(): came = lax.all_to_all(sent, 'tile', 0, 0, tiled=True)  22.6 us
    ppermute x3, starting transfers between devices, on_device(): stacked = stacked + lax.ppermute(part, 'grp', route)  6.6 us
    ppermute x3, waiting for transfers between devices, on_device(): stacked = stacked + lax.ppermute(part, 'grp', route)  3.24 us
    ppermute x1, waiting for transfers between devices, on_device(): lax.ppermute(shot_data, 'tile', [(i + 1, i) for i in range(tiles - 1)])  2.14 us
    pallas_call x1, Pallas kernels, prepare(): pl.pallas_call(prepare_body, out_shape=tuple((jax.ShapeDtypeStruct(s, BF1...  1.98 us
    pallas_call x1, Pallas kernels, stack(): pl.pallas_call(stack_body, out_shape=(part,) * groups, compiler_params=pl...  1.58 us
  transfers between devices with their start and end apart: 5, of which 3 were waited for; matrix products, arithmetic and copies ran while one was open for 0% of the time, Pallas kernels for 3%

profile of v4, /device:TPU:0, one launch (start us, length us, event | category | flops | bytes accessed | tf_op | source)
XLA Modules:
  0.0 70.3 jit_solution(3623273863087004394)
XLA Ops:
  0.6 1.3 %collective-permute-start = (bf16[32,8,512]{2,1,0:T(8,128)(2,1)}, bf16[32,8,512]{2,1,0:T(8,128)(2,1)S(1)}, u32[]{:S(2)}, u32[]{:S(2)}) collective-permute-start(bf16[32,8,512]{2,1,0:T(8,128)(2,1)} %own_ref.1), channel_id=1, source_target_pairs={{0,1},{1,2},{2,3},{3,4},{4,5},{5,6},{6,7},{7,8},{8,9},{9,10},{10,1... | collective-permute-start | bytes 786440 | tf_op jit(solution)/shard_map/ppermute | solution.py:381
  1.9 1.3 %collective-permute-start.1 = (bf16[32,8,512]{2,1,0:T(8,128)(2,1)}, bf16[32,8,512]{2,1,0:T(8,128)(2,1)S(1)}, u32[]{:S(2)}, u32[]{:S(2)}) collective-permute-start(bf16[32,8,512]{2,1,0:T(8,128)(2,1)} %own_ref.1), channel_id=1, source_target_pairs={{1,0},{2,1},{3,2},{4,3},{5,4},{6,5},{7,6},{8,7},{9,8},{10,9},{11,1... | collective-permute-start | bytes 786440 | tf_op jit(solution)/shard_map/ppermute | solution.py:382
  3.2 2.0 %prepare.1 = (bf16[1536,256]{1,0:T(8,128)(2,1)S(1)}, bf16[128,768]{1,0:T(8,128)(2,1)S(1)}, bf16[32,1280]{1,0:T(8,128)(2,1)S(1)}, bf16[512,1024]{1,0:T(8,128)(2,1)S(1)}, bf16[32,32,256]{2,1,0:T(8,128)(2,1)S(1)}) custom-call(bf16[9,64]{1,0:T(8,128)(2,1)} %tap1_ref.1, bf16[576,64]{1,0:T(8,128)(2,1)} %bitcast.10, bf16[9,64]{1,0:T(8,128)(2,1)} %tap3_ref.1, ...), custom_call_target="tpu_custom_call" | custom-call | tf_op jit(solution)/shard_map/prepare/pallas_call | solution.py:110
  5.2 0.0 collective-permute-done.refs_2_
  5.2 2.1 %collective-permute-done.1.refs_3_ = bf16[32,8,512]{2,1,0:T(8,128)(2,1)S(1)} collective-permute-done((bf16[32,8,512]{2,1,0:T(8,128)(2,1)}, bf16[32,8,512]{2,1,0:T(8,128)(2,1)S(1)}, u32[]{:S(2)}, u32[]{:S(2)}) %collective-permute-start.1) | collective-permute-done | bytes 262176 | tf_op jit(solution)/shard_map/ppermute | solution.py:382
  7.4 0.0 copy-start
  7.4 28.2 %denoise.1 = (bf16[32,8,512]{2,1,0:T(8,128)(2,1)}, bf16[32,8,640]{2,1,0:T(8,128)(2,1)S(1)}) custom-call(s32[2]{0:T(128)} %refs_0_.1, s32[2]{0:T(128)} %bitcast.15, bf16[32,8,512]{2,1,0:T(8,128)(2,1)S(1)} %collective-permute-done.refs_2_, bf16[32,8,512]{2,1,0:T(8,128)(2,1)S(1)} %collective-permute-done.1.refs_3_, ...), custom_call_target="tpu_custom_call" | custom-call | flops 9965666304 | bytes 4194304 | tf_op jit(solution)/shard_map/denoise/pallas_call | solution.py:309
  35.6 22.6 %all_to_all.5.came_ref = bf16[32,8,640]{2,1,0:T(8,128)(2,1)S(1)} all-to-all(bf16[32,8,640]{2,1,0:T(8,128)(2,1)S(1)} %get-tuple-element.19), channel_id=1, replica_groups=mesh['grp'=4,'tile'=32] {'tile'}, dimensions={0} | all-to-all | bytes 655360 | tf_op jit(solution)/shard_map/all_to_all | solution.py:385
  58.3 0.0 copy-done
  58.3 1.6 %stack.1 = (f32[8,4,512]{2,1,0:T(4,128)S(1)}, f32[8,4,512]{2,1,0:T(4,128)S(1)}, f32[8,4,512]{2,1,0:T(4,128)S(1)}, f32[8,4,512]{2,1,0:T(4,128)S(1)}) custom-call(bf16[32,8,640]{2,1,0:T(8,128)(2,1)S(1)} %all_to_all.5.came_ref, bf16[4096,512]{1,0:T(8,128)(2,1)S(1)} %bitcast.8), custom_call_target="tpu_custom_call" | custom-call | tf_op jit(solution)/shard_map/stack/pallas_call | solution.py:358
  59.8 2.0 %collective-permute-start.2 = (f32[8,4,512]{2,1,0:T(4,128)S(1)}, f32[8,4,512]{2,1,0:T(4,128)S(1)}, u32[]{:S(2)}, u32[]{:S(2)}) collective-permute-start(f32[8,4,512]{2,1,0:T(4,128)S(1)} %get-tuple-element.21), channel_id=1, source_target_pairs={{0,32},{32,64},{64,96},{96,0},{1,33},{33,65},{65,97},{97,1},{2,34}... | collective-permute-start | bytes 196616 | tf_op jit(solution)/shard_map/ppermute | solution.py:389
  61.8 3.6 %collective-permute-start.3 = (f32[8,4,512]{2,1,0:T(4,128)S(1)}, f32[8,4,512]{2,1,0:T(4,128)S(1)}, u32[]{:S(2)}, u32[]{:S(2)}) collective-permute-start(f32[8,4,512]{2,1,0:T(4,128)S(1)} %get-tuple-element.22), channel_id=1, source_target_pairs={{0,64},{32,96},{64,0},{96,32},{1,65},{33,97},{65,1},{97,33},{2,66}... | collective-permute-start | bytes 196616 | tf_op jit(solution)/shard_map/ppermute | solution.py:389
  65.4 1.0 %collective-permute-start.4 = (f32[8,4,512]{2,1,0:T(4,128)S(1)}, f32[8,4,512]{2,1,0:T(4,128)S(1)}, u32[]{:S(2)}, u32[]{:S(2)}) collective-permute-start(f32[8,4,512]{2,1,0:T(4,128)S(1)} %get-tuple-element.23), channel_id=1, source_target_pairs={{0,96},{32,0},{64,32},{96,64},{1,97},{33,1},{65,33},{97,65},{2,98}... | collective-permute-start | bytes 196616 | tf_op jit(solution)/shard_map/ppermute | solution.py:389
  66.4 0.0 collective-permute-done.2
  66.4 2.6 %collective-permute-done.3 = f32[8,4,512]{2,1,0:T(4,128)S(1)} collective-permute-done((f32[8,4,512]{2,1,0:T(4,128)S(1)}, f32[8,4,512]{2,1,0:T(4,128)S(1)}, u32[]{:S(2)}, u32[]{:S(2)}) %collective-permute-start.3) | collective-permute-done | bytes 65568 | tf_op jit(solution)/shard_map/ppermute | solution.py:389
  69.0 0.7 collective-permute-done.4
  69.7 0.6 add_add_fusion
Async XLA Ops:
  0.6 4.6 %collective-permute-start = (bf16[32,8,512]{2,1,0:T(8,128)(2,1)}, bf16[32,8,512]{2,1,0:T(8,128)(2,1)S(1)}, u32[]{:S(2)}, u32[]{:S(2)}) collective-permute-start(bf16[32,8,512]{2,1,0:T(8,128)(2,1)} %own_ref.1), channel_id=1, source_target_pairs={{0,1},{1,2},{2,3},{3,4},{4,5},{5,6},{6,7},{7,8},{8,9},{9,10},{10,1... | collective-permute-start | bytes 786440 | tf_op jit(solution)/shard_map/ppermute | solution.py:381
  1.9 5.4 %collective-permute-start.1 = (bf16[32,8,512]{2,1,0:T(8,128)(2,1)}, bf16[32,8,512]{2,1,0:T(8,128)(2,1)S(1)}, u32[]{:S(2)}, u32[]{:S(2)}) collective-permute-start(bf16[32,8,512]{2,1,0:T(8,128)(2,1)} %own_ref.1), channel_id=1, source_target_pairs={{1,0},{2,1},{3,2},{4,3},{5,4},{6,5},{7,6},{8,7},{9,8},{10,9},{11,1... | collective-permute-start | bytes 786440 | tf_op jit(solution)/shard_map/ppermute | solution.py:382
  7.4 50.9 %copy-start = (bf16[8,512,512]{2,1,0:T(8,128)(2,1)S(1)}, bf16[8,512,512]{2,1,0:T(8,128)(2,1)}, u32[]{:S(2)}) copy-start(bf16[8,512,512]{2,1,0:T(8,128)(2,1)} %param.11) | copy-start | bytes 12582916
  59.8 6.6 %collective-permute-start.2 = (f32[8,4,512]{2,1,0:T(4,128)S(1)}, f32[8,4,512]{2,1,0:T(4,128)S(1)}, u32[]{:S(2)}, u32[]{:S(2)}) collective-permute-start(f32[8,4,512]{2,1,0:T(4,128)S(1)} %get-tuple-element.21), channel_id=1, source_target_pairs={{0,32},{32,64},{64,96},{96,0},{1,33},{33,65},{65,97},{97,1},{2,34}... | collective-permute-start | bytes 196616 | tf_op jit(solution)/shard_map/ppermute | solution.py:389
  61.8 7.2 %collective-permute-start.3 = (f32[8,4,512]{2,1,0:T(4,128)S(1)}, f32[8,4,512]{2,1,0:T(4,128)S(1)}, u32[]{:S(2)}, u32[]{:S(2)}) collective-permute-start(f32[8,4,512]{2,1,0:T(4,128)S(1)} %get-tuple-element.22), channel_id=1, source_target_pairs={{0,64},{32,96},{64,0},{96,32},{1,65},{33,97},{65,1},{97,33},{2,66}... | collective-permute-start | bytes 196616 | tf_op jit(solution)/shard_map/ppermute | solution.py:389
  65.4 4.3 %collective-permute-start.4 = (f32[8,4,512]{2,1,0:T(4,128)S(1)}, f32[8,4,512]{2,1,0:T(4,128)S(1)}, u32[]{:S(2)}, u32[]{:S(2)}) collective-permute-start(f32[8,4,512]{2,1,0:T(4,128)S(1)} %get-tuple-element.23), channel_id=1, source_target_pairs={{0,96},{32,0},{64,32},{96,64},{1,97},{33,1},{65,33},{97,65},{2,98}... | collective-permute-start | bytes 196616 | tf_op jit(solution)/shard_map/ppermute | solution.py:389

commit v5 on v4

--- a/solution.py
+++ b/solution.py
@@ -18,6 +18,8 @@
 HALF = NT // 2
 OUTER = RD + 4
 INNER = RD + 2
+EDGE = 3
+SIDE = 16
 F32 = jnp.float32
 BF16 = jnp.bfloat16
 
@@ -47,13 +49,17 @@
     shape = (9, UNIT)
     tap = lax.broadcasted_iota(jnp.int32, shape, 0)
     column = lax.broadcasted_iota(jnp.int32, shape, 1)
-    across = column // 32 * RD + column % RD - RD + 3
-    delay = column // RD % 4
+    inner = column - SIDE
+    outer = inner - 4 * RD
+    is_low, is_own = column < SIDE, inner < 4 * RD
+    across = jnp.where(is_low, column % 4, jnp.where(is_own, inner % RD + EDGE, outer % 4 + EDGE + RD))
+    delay = jnp.where(is_low, column // 4, jnp.where(is_own, inner // RD, outer // 4))
+    used = (column < 2 * SIDE + 4 * RD) & ((is_low & (column % 4 < EDGE)) | (inner >= 0) & (is_own | (outer % 4 < EDGE)))
     for receiver in range(OUTER):
         inside = low if receiver < 2 else high if receiver >= OUTER - 2 else None
         for phase in range(2):
             a, d = across - receiver, delay - phase
-            place = (tap == 3 * a + d) & (a >= 0) & (a <= 2) & (d >= 0) & (d <= 2) & (column < 96)
+            place = (tap == 3 * a + d) & (a >= 0) & (a <= 2) & (d >= 0) & (d <= 2) & used
             place = place.astype(F32)
             if inside is not None:
                 place = place * inside
@@ -157,16 +163,26 @@
 
     for ref, held in ((low_ref, low), (high_ref, high)):
         def put(slot, c, part, held=held):
-            part = part.astype(BF16).reshape(per_block, RD, HALF)
-            held[c * per_block : (c + 1) * per_block, slot * RD : (slot + 1) * RD, :] = part
-
-        product(accs, ref[...].reshape(shots * RD, NT), split_ref, put)
+            for row in range(4):
+                at = pl.ds(slot * 4 + row, shots, stride=SIDE)
+                for half in range(HALF // LANES):
+                    lanes = slice(half * LANES, (half + 1) * LANES)
+                    held[half, at, :] = part[row * shots : (row + 1) * shots, lanes]
+
+        edge = ref[...].reshape(EDGE * shots, NT)
+        rest = jnp.zeros((BLK - EDGE * shots, NT), BF16)
+        product(accs, jnp.concatenate([edge, rest], axis=0), split_ref, put)
 
     def taps(pair):
         def right(unit):
             shot = pair * UNITS + unit
-            rest = jnp.zeros((UNIT - 12 * RD, HALF), BF16)
-            return jnp.concatenate([low[shot], own[shot], high[shot], rest], axis=0)
+            rows = pl.ds(pl.multiple_of(shot * SIDE, SIDE), SIDE)
+            rest = jnp.zeros((UNIT - 4 * RD - 2 * SIDE, HALF), BF16)
+            sides = [
+                jnp.concatenate([side[0, rows, :], side[1, rows, :]], axis=1).astype(BF16)
+                for side in (low, high)
+            ]
+            return jnp.concatenate([sides[0], own[shot], sides[1], rest], axis=0)
 
         return right
 
@@ -300,7 +316,7 @@
 
 
 def denoise(offsets, targets, low, high, slots, first, middle, last, split):
-    shots, blocks = low.shape[0], offsets.shape[0]
+    shots, blocks = slots.shape[0], offsets.shape[0]
     owners = lax.axis_size("tile")
     sent = (owners, blocks * BLK // owners, NT + LANES)
     scalars = pl.BlockSpec(memory_space=pltpu.SMEM)
@@ -311,7 +327,7 @@
         out_shape=(jax.ShapeDtypeStruct((shots, RD, NT), BF16), jax.ShapeDtypeStruct(sent, BF16)),
         in_specs=[scalars] * 2 + [whole] * 7,
         out_specs=(whole, whole),
-        scratch_shapes=[pltpu.VMEM((shots, 4 * RD, HALF), BF16)] * 2
+        scratch_shapes=[pltpu.VMEM((HALF // LANES, shots * SIDE, LANES), F32)] * 2
         + [pltpu.VMEM((UNITS, OUTER, UNIT, HALF), BF16)] * 2
         + [pltpu.VMEM((UNITS, INNER * 2 * CH, HALF), BF16)] * 2
         + [pltpu.VMEM((shots * RD, NT), F32), pltpu.VMEM(sent, F32)],
@@ -334,10 +350,10 @@
     corrected = jnp.dot(
         jnp.concatenate(wide, axis=1), map_ref[...], preferred_element_type=F32
     )
-    groups = len(part_refs)
-    owned = MBLK // groups
-    ahead = (target // owned - lax.axis_index("grp") + groups) % groups
-    place = ahead * owned + target % owned
+    owned = part_refs[0].shape[0]
+    apart = (target // owned) ^ lax.axis_index("grp")
+    order = jnp.where(apart == 0, 0, jnp.where(apart == 3, 1, apart + 1))
+    place = order * owned + target % owned
     row = lax.broadcasted_iota(jnp.int32, (count, MBLK * rows), 0) % rows
     column = lax.broadcasted_iota(jnp.int32, (count, MBLK * rows), 1)
     chosen = one_hot((place == column // rows) & (row == column % rows))
@@ -347,20 +363,28 @@
         corrected = corrected - part.astype(F32)
         term = lax.dot_general(chosen, part, (((0,), (0,)), ((), ())), preferred_element_type=F32)
         total = term if total is None else total + term
-    for number, ref in enumerate(part_refs):
-        part = total[number * owned * rows : (number + 1) * owned * rows]
-        ref[...] = part.reshape(ref.shape)
+    start = 0
+    for ref in part_refs:
+        end = start + ref.shape[0] * rows
+        ref[...] = total[start:end].reshape(ref.shape)
+        start = end
 
 
 def stack(came, moveout_maps, groups):
     rows = came.shape[1] * BLK // (SH * RD)
-    part = jax.ShapeDtypeStruct((MBLK // groups, rows, NT), F32)
+    owned = MBLK // groups
     return pl.pallas_call(
         stack_body,
-        out_shape=(part,) * groups,
+        out_shape=tuple(
+            jax.ShapeDtypeStruct((n * owned, rows, NT), F32) for n in (1, 1, 2)
+        ),
         compiler_params=pltpu.CompilerParams(vmem_limit_bytes=40 << 20),
         name="stack",
     )(came, moveout_maps.reshape(OB * NT, NT))
+
+
+def edges(own):
+    return own[:, -EDGE:, :].transpose(1, 0, 2), own[:, :EDGE, :].transpose(1, 0, 2)
 
 
 def on_device(
@@ -378,16 +402,17 @@
             block_target.reshape(-1),
         )
     )
-    low = lax.ppermute(shot_data, "tile", [(i, i + 1) for i in range(tiles - 1)])
-    high = lax.ppermute(shot_data, "tile", [(i + 1, i) for i in range(tiles - 1)])
+    low, high = edges(shot_data)
+    low = lax.ppermute(low, "tile", [(i, i + 1) for i in range(tiles - 1)])
+    high = lax.ppermute(high, "tile", [(i + 1, i) for i in range(tiles - 1)])
     *weights, split, slots = prepare(weight_first, weight_middle, weight_last, own)
     denoised, sent = denoise(block_offset, block_target, low, high, slots, *weights, split)
     came = lax.all_to_all(sent, "tile", 0, 0, tiled=True)
-    stacked, *parts = stack(came, moveout_maps, groups)
-    for ahead, part in enumerate(parts, 1):
-        route = [(g, (g + ahead) % groups) for g in range(groups)]
-        stacked = stacked + lax.ppermute(part, "grp", route)
-    return denoised, stacked
+    kept, far, near = stack(came, moveout_maps, groups)
+    near = lax.ppermute(near, "grp", [(g, g ^ 1) for g in range(groups)])
+    owned = kept.shape[0]
+    far = lax.ppermute(far + near[owned:], "grp", [(g, g ^ 3) for g in range(groups)])
+    return denoised, kept + near[:owned] + far
 
 
 def solution(mesh):

time: 70.5 us -> 72.1 us (1.023)
  waiting for transfers between devices: 5.38 us -> 7.81 us
  blocking collectives: 22.6 us -> 21.1 us
  local copies, waits for them, and re-layouts: 0.01 us -> 1.19 us
    ppermute x5 -> x4, waiting for transfers between devices: 5.38 us -> 7.81 us  [the longest x1 3.87 us: on_device(): near = lax.ppermute(near, 'grp', [(g, g ^ 1) for g in range(groups)])]
    all_to_all x1, blocking collectives: 22.6 us -> 21.1 us  [on_device(): came = lax.all_to_all(sent, 'tile', 0, 0, tiled=True)]
    slice x0 -> x1, local copies, waits for them, and re-layouts: none -> 1.14 us  [edges(): own[:, :EDGE, :].transpose(1, 0, 2)]
    ppermute x5 -> x4, starting transfers between devices: 9.19 us -> 8.51 us  [the longest x1 3.93 us: on_device(): lax.ppermute(far + near[owned:], 'grp', [(g, g ^ 3) for g in range(groups)])]
  transfers between devices with their start and end apart: 5 -> 4, of which waited for: 3 -> 3; matrix products, arithmetic and copies ran while one was open for 0% -> 0% of each run, Pallas kernels for 3% -> 3%
where the time goes in v5:
time: 72.1 us; the launch traced here: 71.8 us
  Pallas kernels  31.9 us (44%)
  blocking collectives  21.1 us (29%)
  starting transfers between devices  8.51 us (12%)
  waiting for transfers between devices  7.81 us (11%)
  local copies, waits for them, and re-layouts  1.19 us (2%)
    pallas_call x1, Pallas kernels, denoise(): pl.pallas_call(denoise_body, out_shape=(jax.ShapeDtypeStruct((shots, RD,...  28.3 us
    all_to_all x1, blocking collectives, on_device(): came = lax.all_to_all(sent, 'tile', 0, 0, tiled=True)  21.1 us
    ppermute x1, starting transfers between devices, on_device(): lax.ppermute(far + near[owned:], 'grp', [(g, g ^ 3) for g in range(groups)])  3.93 us
    ppermute x1, waiting for transfers between devices, on_device(): near = lax.ppermute(near, 'grp', [(g, g ^ 1) for g in range(groups)])  3.87 us
    ppermute x1, waiting for transfers between devices, on_device(): lax.ppermute(far + near[owned:], 'grp', [(g, g ^ 3) for g in range(groups)])  2.25 us
    ppermute x1, starting transfers between devices, on_device(): near = lax.ppermute(near, 'grp', [(g, g ^ 1) for g in range(groups)])  1.99 us
    pallas_call x1, Pallas kernels, prepare(): pl.pallas_call(prepare_body, out_shape=tuple((jax.ShapeDtypeStruct(s, BF1...  1.99 us
    ppermute x1, waiting for transfers between devices, on_device(): high = lax.ppermute(high, 'tile', [(i + 1, i) for i in range(tiles - 1)])  1.69 us
  transfers between devices with their start and end apart: 4, of which 3 were waited for; matrix products, arithmetic and copies ran while one was open for 0% of the time, Pallas kernels for 3%

profile of v5, /device:TPU:0, one launch (start us, length us, event | category | flops | bytes accessed | tf_op | source)
XLA Modules:
  0.0 71.8 jit_solution(2244767786580670434)
XLA Ops:
  0.6 1.1 %fusion.1 = (bf16[32,3,512]{2,1,0:T(4,128)(2,1)S(1)}, bf16[32,3,512]{2,1,0:T(4,128)(2,1)S(1)}) fusion(bf16[32,8,512]{2,1,0:T(8,128)(2,1)} %own_ref.1), kind=kLoop, calls=%fused_computation.5 | loop fusion | bytes 393216 | tf_op jit(solution)/shard_map/slice | solution.py:387
  1.8 1.3 %collective-permute-start = (bf16[3,32,512]{2,1,0:T(8,128)(2,1)S(1)}, bf16[3,32,512]{2,1,0:T(8,128)(2,1)S(1)}, u32[]{:S(2)}, u32[]{:S(2)}) collective-permute-start(bf16[3,32,512]{2,1,0:T(8,128)(2,1)S(1)} %bitcast.11), channel_id=1, source_target_pairs={{0,1},{1,2},{2,3},{3,4},{4,5},{5,6},{6,7},{7,8},{8,9},{9,10},{10,1... | collective-permute-start | bytes 294920 | tf_op jit(solution)/shard_map/ppermute | solution.py:406
  3.1 1.3 %collective-permute-start.1 = (bf16[3,32,512]{2,1,0:T(8,128)(2,1)S(1)}, bf16[3,32,512]{2,1,0:T(8,128)(2,1)S(1)}, u32[]{:S(2)}, u32[]{:S(2)}) collective-permute-start(bf16[3,32,512]{2,1,0:T(8,128)(2,1)S(1)} %bitcast.12), channel_id=1, source_target_pairs={{1,0},{2,1},{3,2},{4,3},{5,4},{6,5},{7,6},{8,7},{9,8},{10,9},{11,1... | collective-permute-start | bytes 294920 | tf_op jit(solution)/shard_map/ppermute | solution.py:407
  4.4 2.0 %prepare.1 = (bf16[1536,256]{1,0:T(8,128)(2,1)S(1)}, bf16[128,768]{1,0:T(8,128)(2,1)S(1)}, bf16[32,1280]{1,0:T(8,128)(2,1)S(1)}, bf16[512,1024]{1,0:T(8,128)(2,1)S(1)}, bf16[32,32,256]{2,1,0:T(8,128)(2,1)S(1)}) custom-call(bf16[9,64]{1,0:T(8,128)(2,1)} %tap1_ref.1, bf16[576,64]{1,0:T(8,128)(2,1)} %bitcast.10, bf16[9,64]{1,0:T(8,128)(2,1)} %tap3_ref.1, ...), custom_call_target="tpu_custom_call" | custom-call | tf_op jit(solution)/shard_map/prepare/pallas_call | solution.py:116
  6.4 0.0 collective-permute-done.refs_2_
  6.4 1.7 %collective-permute-done.1.refs_3_ = bf16[3,32,512]{2,1,0:T(8,128)(2,1)S(1)} collective-permute-done((bf16[3,32,512]{2,1,0:T(8,128)(2,1)S(1)}, bf16[3,32,512]{2,1,0:T(8,128)(2,1)S(1)}, u32[]{:S(2)}, u32[]{:S(2)}) %collective-permute-start.1) | collective-permute-done | bytes 98336 | tf_op jit(solution)/shard_map/ppermute | solution.py:407
  8.1 0.0 copy-start
  8.1 28.3 %denoise.1 = (bf16[32,8,512]{2,1,0:T(8,128)(2,1)}, bf16[32,8,640]{2,1,0:T(8,128)(2,1)S(1)}) custom-call(s32[2]{0:T(128)} %refs_0_.1, s32[2]{0:T(128)} %bitcast.13, bf16[3,32,512]{2,1,0:T(8,128)(2,1)S(1)} %collective-permute-done.refs_2_, bf16[3,32,512]{2,1,0:T(8,128)(2,1)S(1)} %collective-permute-done.1.refs_3_, ...), custom_call_target="tpu_custom_call" | custom-call | flops 9965666304 | bytes 4194304 | tf_op jit(solution)/shard_map/denoise/pallas_call | solution.py:325
  36.4 21.1 %all_to_all.5.came_ref = bf16[32,8,640]{2,1,0:T(8,128)(2,1)S(1)} all-to-all(bf16[32,8,640]{2,1,0:T(8,128)(2,1)S(1)} %get-tuple-element.18), channel_id=1, replica_groups=mesh['grp'=4,'tile'=32] {'tile'}, dimensions={0} | all-to-all | bytes 655360 | tf_op jit(solution)/shard_map/all_to_all | solution.py:410
  57.5 0.0 copy-done
  57.5 1.6 %stack.1 = (f32[8,4,512]{2,1,0:T(4,128)S(1)}, f32[8,4,512]{2,1,0:T(4,128)S(1)}, f32[16,4,512]{2,1,0:T(4,128)S(1)}) custom-call(bf16[32,8,640]{2,1,0:T(8,128)(2,1)S(1)} %all_to_all.5.came_ref, bf16[4096,512]{1,0:T(8,128)(2,1)S(1)} %bitcast.9), custom_call_target="tpu_custom_call" | custom-call | tf_op jit(solution)/shard_map/stack/pallas_call | solution.py:376
  59.1 2.0 %collective-permute-start.2 = (f32[16,4,512]{2,1,0:T(4,128)S(1)}, f32[16,4,512]{2,1,0:T(4,128)S(1)}, u32[]{:S(2)}, u32[]{:S(2)}) collective-permute-start(f32[16,4,512]{2,1,0:T(4,128)S(1)} %get-tuple-element.20), channel_id=1, source_target_pairs={{0,32},{32,0},{64,96},{96,64},{1,33},{33,1},{65,97},{97,65},{2,34}... | collective-permute-start | bytes 393224 | tf_op jit(solution)/shard_map/ppermute | solution.py:412
  61.1 3.9 %collective-permute-done.2 = f32[16,4,512]{2,1,0:T(4,128)S(1)} collective-permute-done((f32[16,4,512]{2,1,0:T(4,128)S(1)}, f32[16,4,512]{2,1,0:T(4,128)S(1)}, u32[]{:S(2)}, u32[]{:S(2)}) %collective-permute-start.2) | collective-permute-done | bytes 131104 | tf_op jit(solution)/shard_map/ppermute | solution.py:412
  65.0 3.9 %collective-permute-start.3 = (f32[8,4,512]{2,1,0:T(4,128)S(1)}, f32[8,4,512]{2,1,0:T(4,128)S(1)}, u32[]{:S(2)}, u32[]{:S(2)}) collective-permute-start(f32[8,4,512]{2,1,0:T(4,128)S(1)} %slice_add_fusion), channel_id=1, source_target_pairs={{0,96},{32,64},{64,32},{96,0},{1,97},{33,65},{65,33},{97,1},{2,98}... | collective-permute-start | bytes 196616 | tf_op jit(solution)/shard_map/ppermute | solution.py:414
  68.9 2.2 %collective-permute-done.3 = f32[8,4,512]{2,1,0:T(4,128)S(1)} collective-permute-done((f32[8,4,512]{2,1,0:T(4,128)S(1)}, f32[8,4,512]{2,1,0:T(4,128)S(1)}, u32[]{:S(2)}, u32[]{:S(2)}) %collective-permute-start.3) | collective-permute-done | bytes 65568 | tf_op jit(solution)/shard_map/ppermute | solution.py:414
  71.2 0.7 fusion
  (3 shorter events, 0.1 us)
Async XLA Ops:
  1.8 4.6 %collective-permute-start = (bf16[3,32,512]{2,1,0:T(8,128)(2,1)S(1)}, bf16[3,32,512]{2,1,0:T(8,128)(2,1)S(1)}, u32[]{:S(2)}, u32[]{:S(2)}) collective-permute-start(bf16[3,32,512]{2,1,0:T(8,128)(2,1)S(1)} %bitcast.11), channel_id=1, source_target_pairs={{0,1},{1,2},{2,3},{3,4},{4,5},{5,6},{6,7},{7,8},{8,9},{9,10},{10,1... | collective-permute-start | bytes 294920 | tf_op jit(solution)/shard_map/ppermute | solution.py:406
  3.1 5.0 %collective-permute-start.1 = (bf16[3,32,512]{2,1,0:T(8,128)(2,1)S(1)}, bf16[3,32,512]{2,1,0:T(8,128)(2,1)S(1)}, u32[]{:S(2)}, u32[]{:S(2)}) collective-permute-start(bf16[3,32,512]{2,1,0:T(8,128)(2,1)S(1)} %bitcast.12), channel_id=1, source_target_pairs={{1,0},{2,1},{3,2},{4,3},{5,4},{6,5},{7,6},{8,7},{9,8},{10,9},{11,1... | collective-permute-start | bytes 294920 | tf_op jit(solution)/shard_map/ppermute | solution.py:407
  8.1 49.4 %copy-start = (bf16[8,512,512]{2,1,0:T(8,128)(2,1)S(1)}, bf16[8,512,512]{2,1,0:T(8,128)(2,1)}, u32[]{:S(2)}) copy-start(bf16[8,512,512]{2,1,0:T(8,128)(2,1)} %param.11) | copy-start | bytes 12582916
  59.1 5.9 %collective-permute-start.2 = (f32[16,4,512]{2,1,0:T(4,128)S(1)}, f32[16,4,512]{2,1,0:T(4,128)S(1)}, u32[]{:S(2)}, u32[]{:S(2)}) collective-permute-start(f32[16,4,512]{2,1,0:T(4,128)S(1)} %get-tuple-element.20), channel_id=1, source_target_pairs={{0,32},{32,0},{64,96},{96,64},{1,33},{33,1},{65,97},{97,65},{2,34}... | collective-permute-start | bytes 393224 | tf_op jit(solution)/shard_map/ppermute | solution.py:412
  65.0 6.2 %collective-permute-start.3 = (f32[8,4,512]{2,1,0:T(4,128)S(1)}, f32[8,4,512]{2,1,0:T(4,128)S(1)}, u32[]{:S(2)}, u32[]{:S(2)}) collective-permute-start(f32[8,4,512]{2,1,0:T(4,128)S(1)} %slice_add_fusion), channel_id=1, source_target_pairs={{0,96},{32,64},{64,32},{96,0},{1,97},{33,65},{65,33},{97,1},{2,98}... | collective-permute-start | bytes 196616 | tf_op jit(solution)/shard_map/ppermute | solution.py:414

commit v6 on v5

--- a/solution.py
+++ b/solution.py
@@ -51,10 +51,12 @@
     column = lax.broadcasted_iota(jnp.int32, shape, 1)
     inner = column - SIDE
     outer = inner - 4 * RD
-    is_low, is_own = column < SIDE, inner < 4 * RD
-    across = jnp.where(is_low, column % 4, jnp.where(is_own, inner % RD + EDGE, outer % 4 + EDGE + RD))
-    delay = jnp.where(is_low, column // 4, jnp.where(is_own, inner // RD, outer // 4))
-    used = (column < 2 * SIDE + 4 * RD) & ((is_low & (column % 4 < EDGE)) | (inner >= 0) & (is_own | (outer % 4 < EDGE)))
+    is_near, is_own = column < SIDE, inner < 4 * RD
+    odd = tile % 2
+    near, far = (EDGE + RD) * (1 - odd), (EDGE + RD) * odd
+    across = jnp.where(is_near, column % 4 + near, jnp.where(is_own, inner % RD + EDGE, outer % 4 + far))
+    delay = jnp.where(is_near, column // 4, jnp.where(is_own, inner // RD, outer // 4))
+    used = (column < 2 * SIDE + 4 * RD) & ((is_near | (inner >= 4 * RD)) & (column % 4 < EDGE) | (inner >= 0) & is_own)
     for receiver in range(OUTER):
         inside = low if receiver < 2 else high if receiver >= OUTER - 2 else None
         for phase in range(2):
@@ -154,14 +156,14 @@
 
 
 def denoise_loop(
-    offset_ref, target_ref, low_ref, high_ref, own, first_ref, middle_ref, last_ref, split_ref,
-    denoised_ref, sent_ref, low, high, h1_even, h1_odd, h2_even, h2_odd, cleaned, rows4, accs,
+    offset_ref, target_ref, near_ref, far_ref, own, first_ref, middle_ref, last_ref, split_ref,
+    denoised_ref, sent_ref, near, far, h1_even, h1_odd, h2_even, h2_odd, cleaned, rows4, accs,
 ):
     shots = own.shape[0]
     pairs = shots // UNITS
     per_block = BLK // RD
 
-    for ref, held in ((low_ref, low), (high_ref, high)):
+    for ref, held in ((near_ref, near), (far_ref, far)):
         def put(slot, c, part, held=held):
             for row in range(4):
                 at = pl.ds(slot * 4 + row, shots, stride=SIDE)
@@ -180,7 +182,7 @@
             rest = jnp.zeros((UNIT - 4 * RD - 2 * SIDE, HALF), BF16)
             sides = [
                 jnp.concatenate([side[0, rows, :], side[1, rows, :]], axis=1).astype(BF16)
-                for side in (low, high)
+                for side in (near, far)
             ]
             return jnp.concatenate([sides[0], own[shot], sides[1], rest], axis=0)
 
@@ -315,7 +317,7 @@
     )
 
 
-def denoise(offsets, targets, low, high, slots, first, middle, last, split):
+def denoise(offsets, targets, near, far, slots, first, middle, last, split):
     shots, blocks = slots.shape[0], offsets.shape[0]
     owners = lax.axis_size("tile")
     sent = (owners, blocks * BLK // owners, NT + LANES)
@@ -334,7 +336,7 @@
         compiler_params=pltpu.CompilerParams(vmem_limit_bytes=40 << 20),
         cost_estimate=pl.CostEstimate(flops=2 * macs, transcendentals=0, bytes_accessed=4 << 20),
         name="denoise",
-    )(offsets, targets, low, high, slots, first, middle, last, split)
+    )(offsets, targets, near, far, slots, first, middle, last, split)
 
 
 def stack_body(came_ref, map_ref, *part_refs):
@@ -350,10 +352,9 @@
     corrected = jnp.dot(
         jnp.concatenate(wide, axis=1), map_ref[...], preferred_element_type=F32
     )
-    owned = part_refs[0].shape[0]
-    apart = (target // owned) ^ lax.axis_index("grp")
-    order = jnp.where(apart == 0, 0, jnp.where(apart == 3, 1, apart + 1))
-    place = order * owned + target % owned
+    groups = len(part_refs)
+    owned = MBLK // groups
+    place = ((target // owned) ^ lax.axis_index("grp")) * owned + target % owned
     row = lax.broadcasted_iota(jnp.int32, (count, MBLK * rows), 0) % rows
     column = lax.broadcasted_iota(jnp.int32, (count, MBLK * rows), 1)
     chosen = one_hot((place == column // rows) & (row == column % rows))
@@ -363,28 +364,26 @@
         corrected = corrected - part.astype(F32)
         term = lax.dot_general(chosen, part, (((0,), (0,)), ((), ())), preferred_element_type=F32)
         total = term if total is None else total + term
-    start = 0
-    for ref in part_refs:
-        end = start + ref.shape[0] * rows
-        ref[...] = total[start:end].reshape(ref.shape)
-        start = end
+    for number, ref in enumerate(part_refs):
+        part = total[number * owned * rows : (number + 1) * owned * rows]
+        ref[...] = part.reshape(ref.shape)
 
 
 def stack(came, moveout_maps, groups):
     rows = came.shape[1] * BLK // (SH * RD)
-    owned = MBLK // groups
+    part = jax.ShapeDtypeStruct((MBLK // groups, rows, NT), F32)
     return pl.pallas_call(
         stack_body,
-        out_shape=tuple(
-            jax.ShapeDtypeStruct((n * owned, rows, NT), F32) for n in (1, 1, 2)
-        ),
+        out_shape=(part,) * groups,
         compiler_params=pltpu.CompilerParams(vmem_limit_bytes=40 << 20),
         name="stack",
     )(came, moveout_maps.reshape(OB * NT, NT))
 
 
 def edges(own):
-    return own[:, -EDGE:, :].transpose(1, 0, 2), own[:, :EDGE, :].transpose(1, 0, 2)
+    odd = lax.axis_index("tile") % 2 == 1
+    start, end = own[:, :EDGE, :].transpose(1, 0, 2), own[:, -EDGE:, :].transpose(1, 0, 2)
+    return jnp.where(odd, start, end), jnp.where(odd, end, start)
 
 
 def on_device(
@@ -402,17 +401,17 @@
             block_target.reshape(-1),
         )
     )
-    low, high = edges(shot_data)
-    low = lax.ppermute(low, "tile", [(i, i + 1) for i in range(tiles - 1)])
-    high = lax.ppermute(high, "tile", [(i + 1, i) for i in range(tiles - 1)])
+    near, far = edges(shot_data)
+    near = lax.ppermute(near, "tile", [(i, i ^ 1) for i in range(tiles)])
+    pairs = [(i, i + 1) for i in range(1, tiles - 1, 2)]
+    far = lax.ppermute(far, "tile", pairs + [(j, i) for i, j in pairs])
     *weights, split, slots = prepare(weight_first, weight_middle, weight_last, own)
-    denoised, sent = denoise(block_offset, block_target, low, high, slots, *weights, split)
+    denoised, sent = denoise(block_offset, block_target, near, far, slots, *weights, split)
     came = lax.all_to_all(sent, "tile", 0, 0, tiled=True)
-    kept, far, near = stack(came, moveout_maps, groups)
-    near = lax.ppermute(near, "grp", [(g, g ^ 1) for g in range(groups)])
-    owned = kept.shape[0]
-    far = lax.ppermute(far + near[owned:], "grp", [(g, g ^ 3) for g in range(groups)])
-    return denoised, kept + near[:owned] + far
+    stacked, *parts = stack(came, moveout_maps, groups)
+    for apart, part in enumerate(parts, 1):
+        stacked = stacked + lax.ppermute(part, "grp", [(g, g ^ apart) for g in range(groups)])
+    return denoised, stacked
 
 
 def solution(mesh):

time: 72.1 us -> 67.6 us (0.938)
  blocking collectives: 21.1 us -> 18.3 us
  waiting for transfers between devices: 7.81 us -> 5.48 us
  starting transfers between devices: 8.51 us -> 9.27 us
    all_to_all x1, blocking collectives: 21.1 us -> 18.3 us  [on_device(): came = lax.all_to_all(sent, 'tile', 0, 0, tiled=True)]
    ppermute x4 -> x5, waiting for transfers between devices: 7.81 us -> 5.48 us  [the longest x3 5.47 us: on_device(): lax.ppermute(part, 'grp', [(g, g ^ apart) for g in range(groups)])]
    ppermute x4 -> x5, starting transfers between devices: 8.51 us -> 9.27 us  [the longest x3 5.59 us: on_device(): lax.ppermute(part, 'grp', [(g, g ^ apart) for g in range(groups)])]
  transfers between devices with their start and end apart: 4 -> 5, of which waited for: 3 -> 2; matrix products, arithmetic and copies ran while one was open for 0% -> 0% of each run, Pallas kernels for 3% -> 3%
where the time goes in v6:
time: 67.6 us; the launch traced here: 67.4 us
  Pallas kernels  31.9 us (47%)
  blocking collectives  18.3 us (27%)
  starting transfers between devices  9.27 us (14%)
  waiting for transfers between devices  5.48 us (8%)
  local copies, waits for them, and re-layouts  1.14 us (2%)
  other arithmetic  0.7 us (1%)
  between operations  0.7 us (1%)
    pallas_call x1, Pallas kernels, denoise(): pl.pallas_call(denoise_body, out_shape=(jax.ShapeDtypeStruct((shots, RD,...  28.3 us
    all_to_all x1, blocking collectives, on_device(): came = lax.all_to_all(sent, 'tile', 0, 0, tiled=True)  18.3 us
    ppermute x3, starting transfers between devices, on_device(): lax.ppermute(part, 'grp', [(g, g ^ apart) for g in range(groups)])  5.59 us
    ppermute x3, waiting for transfers between devices, on_device(): lax.ppermute(part, 'grp', [(g, g ^ apart) for g in range(groups)])  5.47 us
    ppermute x1, starting transfers between devices, on_device(): near = lax.ppermute(near, 'tile', [(i, i ^ 1) for i in range(tiles)])  3.01 us
    pallas_call x1, Pallas kernels, prepare(): pl.pallas_call(prepare_body, out_shape=tuple((jax.ShapeDtypeStruct(s, BF1...  2 us
    pallas_call x1, Pallas kernels, stack(): pl.pallas_call(stack_body, out_shape=(part,) * groups, compiler_params=pl...  1.57 us
  transfers between devices with their start and end apart: 5, of which 2 were waited for; matrix products, arithmetic and copies ran while one was open for 0% of the time, Pallas kernels for 3%

profile of v6, /device:TPU:0, one launch (start us, length us, event | category | flops | bytes accessed | tf_op | source)
XLA Modules:
  0.0 67.4 jit_solution(7040279984293734801)
XLA Ops:
  0.6 1.1 %fusion = (bf16[32,3,512]{2,1,0:T(4,128)(2,1)S(1)}, bf16[32,3,512]{2,1,0:T(4,128)(2,1)S(1)}) fusion(bf16[32,8,512]{2,1,0:T(8,128)(2,1)} %own_ref.1), kind=kLoop, calls=%fused_computation.3 | loop fusion | bytes 393216 | tf_op jit(solution)/shard_map/slice | solution.py:385
  1.8 0.7 collective-permute-start.1
  2.5 3.0 %collective-permute-start = (bf16[3,32,512]{2,1,0:T(8,128)(2,1)S(1)}, bf16[3,32,512]{2,1,0:T(8,128)(2,1)S(1)}, u32[]{:S(2)}, u32[]{:S(2)}) collective-permute-start(bf16[3,32,512]{2,1,0:T(8,128)(2,1)S(1)} %get-tuple-element.25), channel_id=1, source_target_pairs={{0,1},{1,0},{2,3},{3,2},{4,5},{5,4},{6,7},{7,6},{8,9},{9,8},{10,11... | collective-permute-start | bytes 294920 | tf_op jit(solution)/shard_map/ppermute | solution.py:405
  5.5 2.0 %prepare.1 = (bf16[1536,256]{1,0:T(8,128)(2,1)S(1)}, bf16[128,768]{1,0:T(8,128)(2,1)S(1)}, bf16[32,1280]{1,0:T(8,128)(2,1)S(1)}, bf16[512,1024]{1,0:T(8,128)(2,1)S(1)}, bf16[32,32,256]{2,1,0:T(8,128)(2,1)S(1)}) custom-call(bf16[9,64]{1,0:T(8,128)(2,1)} %tap1_ref.1, bf16[576,64]{1,0:T(8,128)(2,1)} %bitcast.14, bf16[9,64]{1,0:T(8,128)(2,1)} %tap3_ref.1, ...), custom_call_target="tpu_custom_call" | custom-call | tf_op jit(solution)/shard_map/prepare/pallas_call | solution.py:118
  7.5 0.0 collective-permute-done.1.refs_3_
  7.5 0.0 collective-permute-done.refs_2_
  7.5 0.0 copy-start
  7.6 28.3 %denoise.1 = (bf16[32,8,512]{2,1,0:T(8,128)(2,1)}, bf16[32,8,640]{2,1,0:T(8,128)(2,1)S(1)}) custom-call(s32[2]{0:T(128)} %refs_0_.1, s32[2]{0:T(128)} %bitcast.19, bf16[3,32,512]{2,1,0:T(8,128)(2,1)S(1)} %collective-permute-done.refs_2_, bf16[3,32,512]{2,1,0:T(8,128)(2,1)S(1)} %collective-permute-done.1.refs_3_, ...), custom_call_target="tpu_custom_call" | custom-call | flops 9965666304 | bytes 4194304 | tf_op jit(solution)/shard_map/denoise/pallas_call | solution.py:327
  35.9 18.3 %all_to_all.5.came_ref = bf16[32,8,640]{2,1,0:T(8,128)(2,1)S(1)} all-to-all(bf16[32,8,640]{2,1,0:T(8,128)(2,1)S(1)} %get-tuple-element.19), channel_id=1, replica_groups=mesh['grp'=4,'tile'=32] {'tile'}, dimensions={0} | all-to-all | bytes 655360 | tf_op jit(solution)/shard_map/all_to_all | solution.py:410
  54.2 0.0 copy-done
  54.2 1.6 %stack.1 = (f32[8,4,512]{2,1,0:T(4,128)S(1)}, f32[8,4,512]{2,1,0:T(4,128)S(1)}, f32[8,4,512]{2,1,0:T(4,128)S(1)}, f32[8,4,512]{2,1,0:T(4,128)S(1)}) custom-call(bf16[32,8,640]{2,1,0:T(8,128)(2,1)S(1)} %all_to_all.5.came_ref, bf16[4096,512]{1,0:T(8,128)(2,1)S(1)} %bitcast.12), custom_call_target="tpu_custom_call" | custom-call | tf_op jit(solution)/shard_map/stack/pallas_call | solution.py:375
  55.7 2.0 %collective-permute-start.2 = (f32[8,4,512]{2,1,0:T(4,128)S(1)}, f32[8,4,512]{2,1,0:T(4,128)S(1)}, u32[]{:S(2)}, u32[]{:S(2)}) collective-permute-start(f32[8,4,512]{2,1,0:T(4,128)S(1)} %get-tuple-element.21), channel_id=1, source_target_pairs={{0,32},{32,0},{64,96},{96,64},{1,33},{33,1},{65,97},{97,65},{2,34}... | collective-permute-start | bytes 196616 | tf_op jit(solution)/shard_map/ppermute | solution.py:413
  57.7 3.6 %collective-permute-start.3 = (f32[8,4,512]{2,1,0:T(4,128)S(1)}, f32[8,4,512]{2,1,0:T(4,128)S(1)}, u32[]{:S(2)}, u32[]{:S(2)}) collective-permute-start(f32[8,4,512]{2,1,0:T(4,128)S(1)} %get-tuple-element.22), channel_id=1, source_target_pairs={{0,64},{32,96},{64,0},{96,32},{1,65},{33,97},{65,1},{97,33},{2,66}... | collective-permute-start | bytes 196616 | tf_op jit(solution)/shard_map/ppermute | solution.py:413
  61.3 0.0 collective-permute-start.4
  61.3 0.0 collective-permute-done.2
  61.3 3.6 %collective-permute-done.3 = f32[8,4,512]{2,1,0:T(4,128)S(1)} collective-permute-done((f32[8,4,512]{2,1,0:T(4,128)S(1)}, f32[8,4,512]{2,1,0:T(4,128)S(1)}, u32[]{:S(2)}, u32[]{:S(2)}) %collective-permute-start.3) | collective-permute-done | bytes 65568 | tf_op jit(solution)/shard_map/ppermute | solution.py:413
  64.9 1.9 %collective-permute-done.4 = f32[8,4,512]{2,1,0:T(4,128)S(1)} collective-permute-done((f32[8,4,512]{2,1,0:T(4,128)S(1)}, f32[8,4,512]{2,1,0:T(4,128)S(1)}, u32[]{:S(2)}, u32[]{:S(2)}) %collective-permute-start.4) | collective-permute-done | bytes 65568 | tf_op jit(solution)/shard_map/ppermute | solution.py:413
  66.8 0.6 add_add_fusion
  (1 shorter events, 0.0 us)
Async XLA Ops:
  1.8 5.7 %collective-permute-start.1 = (bf16[3,32,512]{2,1,0:T(8,128)(2,1)S(1)}, bf16[3,32,512]{2,1,0:T(8,128)(2,1)S(1)}, u32[]{:S(2)}, u32[]{:S(2)}) collective-permute-start(bf16[3,32,512]{2,1,0:T(8,128)(2,1)S(1)} %get-tuple-element.24), channel_id=1, source_target_pairs={{1,2},{3,4},{5,6},{7,8},{9,10},{11,12},{13,14},{15,16},{17,18},{19... | collective-permute-start | bytes 294920 | tf_op jit(solution)/shard_map/ppermute | solution.py:407
  2.5 5.0 %collective-permute-start = (bf16[3,32,512]{2,1,0:T(8,128)(2,1)S(1)}, bf16[3,32,512]{2,1,0:T(8,128)(2,1)S(1)}, u32[]{:S(2)}, u32[]{:S(2)}) collective-permute-start(bf16[3,32,512]{2,1,0:T(8,128)(2,1)S(1)} %get-tuple-element.25), channel_id=1, source_target_pairs={{0,1},{1,0},{2,3},{3,2},{4,5},{5,4},{6,7},{7,6},{8,9},{9,8},{10,11... | collective-permute-start | bytes 294920 | tf_op jit(solution)/shard_map/ppermute | solution.py:405
  7.5 46.6 %copy-start = (bf16[8,512,512]{2,1,0:T(8,128)(2,1)S(1)}, bf16[8,512,512]{2,1,0:T(8,128)(2,1)}, u32[]{:S(2)}) copy-start(bf16[8,512,512]{2,1,0:T(8,128)(2,1)} %param.11) | copy-start | bytes 12582916
  55.7 5.6 %collective-permute-start.2 = (f32[8,4,512]{2,1,0:T(4,128)S(1)}, f32[8,4,512]{2,1,0:T(4,128)S(1)}, u32[]{:S(2)}, u32[]{:S(2)}) collective-permute-start(f32[8,4,512]{2,1,0:T(4,128)S(1)} %get-tuple-element.21), channel_id=1, source_target_pairs={{0,32},{32,0},{64,96},{96,64},{1,33},{33,1},{65,97},{97,65},{2,34}... | collective-permute-start | bytes 196616 | tf_op jit(solution)/shard_map/ppermute | solution.py:413
  57.7 7.2 %collective-permute-start.3 = (f32[8,4,512]{2,1,0:T(4,128)S(1)}, f32[8,4,512]{2,1,0:T(4,128)S(1)}, u32[]{:S(2)}, u32[]{:S(2)}) collective-permute-start(f32[8,4,512]{2,1,0:T(4,128)S(1)} %get-tuple-element.22), channel_id=1, source_target_pairs={{0,64},{32,96},{64,0},{96,32},{1,65},{33,97},{65,1},{97,33},{2,66}... | collective-permute-start | bytes 196616 | tf_op jit(solution)/shard_map/ppermute | solution.py:413
  61.3 5.5 %collective-permute-start.4 = (f32[8,4,512]{2,1,0:T(4,128)S(1)}, f32[8,4,512]{2,1,0:T(4,128)S(1)}, u32[]{:S(2)}, u32[]{:S(2)}) collective-permute-start(f32[8,4,512]{2,1,0:T(4,128)S(1)} %get-tuple-element.23), channel_id=1, source_target_pairs={{0,96},{32,64},{64,32},{96,0},{1,97},{33,65},{65,33},{97,1},{2,98}... | collective-permute-start | bytes 196616 | tf_op jit(solution)/shard_map/ppermute | solution.py:413

commit v7 on v6

--- a/solution.py
+++ b/solution.py
@@ -20,6 +20,7 @@
 INNER = RD + 2
 EDGE = 3
 SIDE = 16
+STAGES = 4
 F32 = jnp.float32
 BF16 = jnp.bfloat16
 
@@ -156,7 +157,7 @@
 
 
 def denoise_loop(
-    offset_ref, target_ref, near_ref, far_ref, own, first_ref, middle_ref, last_ref, split_ref,
+    near_ref, far_ref, own, first_ref, middle_ref, last_ref, split_ref,
     denoised_ref, sent_ref, near, far, h1_even, h1_odd, h2_even, h2_odd, cleaned, rows4, accs,
 ):
     shots = own.shape[0]
@@ -271,20 +272,23 @@
         jobs[-1][2].extend(tail)
         run(jobs)
 
-    chain(stage(None, (0, h1_even), None))
-    chain(stage((h1_even, h2_even), (1, h1_odd), None))
-
-    def two(step, carry):
-        pair = 2 * step + 1
-        chain(
-            stage((h1_odd, h2_odd), (pair + 1, h1_even), (pair - 1, h2_even)),
-            stage((h1_even, h2_even), (pair + 2, h1_odd), (pair, h2_odd)),
-        )
+    buffers = ((h1_even, h2_even), (h1_odd, h2_odd))
+
+    def full(pair, parity):
+        now, other = buffers[parity], buffers[1 - parity]
+        return stage(now, (pair + 1, other[0]), (pair - 1, other[1]))
+
+    def several(step, carry):
+        pair = STAGES * step + 1
+        chain(*[full(pair + n, (n + 1) % 2) for n in range(STAGES)])
         return carry
 
-    lax.fori_loop(0, (pairs - 2) // 2, two, 0)
-    chain(stage((h1_odd, h2_odd), None, (pairs - 2, h2_even)))
-    chain(([last_job(h2_odd, n) for n in range(INNER // 2)], [last_done(pairs - 1)]))
+    chain(stage(None, (0, h1_even), None), stage(buffers[0], (1, h1_odd), None))
+    steps = (pairs - 2) // STAGES
+    lax.fori_loop(0, steps, several, 0)
+    rest = [full(pair, pair % 2) for pair in range(STAGES * steps + 1, pairs - 1)]
+    end = [last_job(h2_odd, n) for n in range(INNER // 2)], [last_done(pairs - 1)]
+    chain(*rest, stage(buffers[1], None, (pairs - 2, h2_even)), end)
 
     lane = lax.broadcasted_iota(jnp.int32, (NT, NT), 0)
     time = lax.broadcasted_iota(jnp.int32, (NT, NT), 1)
@@ -299,10 +303,6 @@
         rows4[:, c * kept : (c + 1) * kept, lanes] = part.reshape(owners, kept, UNIT)
 
     product(accs, cleaned[...].astype(BF16), merge, put)
-    shape = (owners, kept, LANES // 2)
-    for c in range(shots * RD // BLK):
-        rows4[:, c * kept : (c + 1) * kept, NT : NT + LANES // 2] = jnp.full(shape, target_ref[c].astype(F32))
-        rows4[:, c * kept : (c + 1) * kept, NT + LANES // 2 :] = jnp.full(shape, offset_ref[c].astype(F32))
     sent_ref[...] = rows4[...].astype(BF16)
 
 
@@ -317,17 +317,16 @@
     )
 
 
-def denoise(offsets, targets, near, far, slots, first, middle, last, split):
-    shots, blocks = slots.shape[0], offsets.shape[0]
+def denoise(near, far, slots, first, middle, last, split):
+    shots = slots.shape[0]
     owners = lax.axis_size("tile")
-    sent = (owners, blocks * BLK // owners, NT + LANES)
-    scalars = pl.BlockSpec(memory_space=pltpu.SMEM)
+    sent = (owners, shots * RD // owners, NT)
     whole = pl.BlockSpec(memory_space=pltpu.VMEM)
     macs = shots * RD * NT * CH * (9 * CH + 18)
     return pl.pallas_call(
         denoise_body,
         out_shape=(jax.ShapeDtypeStruct((shots, RD, NT), BF16), jax.ShapeDtypeStruct(sent, BF16)),
-        in_specs=[scalars] * 2 + [whole] * 7,
+        in_specs=[whole] * 7,
         out_specs=(whole, whole),
         scratch_shapes=[pltpu.VMEM((HALF // LANES, shots * SIDE, LANES), F32)] * 2
         + [pltpu.VMEM((UNITS, OUTER, UNIT, HALF), BF16)] * 2
@@ -336,17 +335,26 @@
         compiler_params=pltpu.CompilerParams(vmem_limit_bytes=40 << 20),
         cost_estimate=pl.CostEstimate(flops=2 * macs, transcendentals=0, bytes_accessed=4 << 20),
         name="denoise",
-    )(offsets, targets, near, far, slots, first, middle, last, split)
-
-
-def stack_body(came_ref, map_ref, *part_refs):
+    )(near, far, slots, first, middle, last, split)
+
+
+def stack_body(came_ref, choice_ref, map_ref, *part_refs):
     tiles, kept, _ = came_ref.shape
     rows = kept * BLK // (SH * RD)
     count = tiles * kept
-    came = came_ref[...].reshape(count, NT + LANES)
-    target = came[:, NT : NT + 1].astype(F32).astype(jnp.int32)
-    offset = came[:, NT + LANES // 2 : NT + LANES // 2 + 1].astype(F32)
-    traces = came[:, :NT]
+    traces = came_ref[...].reshape(count, NT)
+    blocks = kept // rows
+    choice = [
+        jnp.concatenate(
+            [
+                jnp.broadcast_to(choice_ref[:, n : n + 1, :], (tiles, rows, LANES))
+                for n in range(start, start + blocks)
+            ],
+            axis=1,
+        ).reshape(count, LANES)[:, :1]
+        for start in (0, blocks)
+    ]
+    target, offset = choice[0].astype(jnp.int32), choice[1]
     none = jnp.zeros_like(traces)
     wide = [jnp.where(offset == o, traces, none) for o in range(OB)]
     corrected = jnp.dot(
@@ -369,7 +377,7 @@
         ref[...] = part.reshape(ref.shape)
 
 
-def stack(came, moveout_maps, groups):
+def stack(came, choice, moveout_maps, groups):
     rows = came.shape[1] * BLK // (SH * RD)
     part = jax.ShapeDtypeStruct((MBLK // groups, rows, NT), F32)
     return pl.pallas_call(
@@ -377,7 +385,7 @@
         out_shape=(part,) * groups,
         compiler_params=pltpu.CompilerParams(vmem_limit_bytes=40 << 20),
         name="stack",
-    )(came, moveout_maps.reshape(OB * NT, NT))
+    )(came, choice, moveout_maps.reshape(OB * NT, NT))
 
 
 def edges(own):
@@ -390,27 +398,31 @@
     shot_data, weight_first, weight_middle, weight_last, moveout_maps, block_offset, block_target
 ):
     tiles, groups = lax.axis_size("tile"), lax.axis_size("grp")
-    (own, weight_first, weight_middle, weight_last, block_offset, block_target) = (
+    (own, weight_first, weight_middle, weight_last) = (
         pltpu.with_memory_space_constraint(a, pltpu.HBM)
         for a in (
             shot_data,
             weight_first,
             weight_middle.reshape(9 * CH, CH),
             weight_last,
-            block_offset,
-            block_target.reshape(-1),
         )
     )
+    choice = jnp.concatenate([block_target.reshape(-1), block_offset]).astype(F32)
+    mine = jnp.arange(tiles)[:, None, None] == lax.axis_index("tile")
+    choice = jnp.where(mine, choice[None, :, None], jnp.zeros((tiles, choice.shape[0], LANES), F32))
+    choice = lax.psum(choice, "tile")
     near, far = edges(shot_data)
     near = lax.ppermute(near, "tile", [(i, i ^ 1) for i in range(tiles)])
     pairs = [(i, i + 1) for i in range(1, tiles - 1, 2)]
     far = lax.ppermute(far, "tile", pairs + [(j, i) for i, j in pairs])
     *weights, split, slots = prepare(weight_first, weight_middle, weight_last, own)
-    denoised, sent = denoise(block_offset, block_target, near, far, slots, *weights, split)
+    denoised, sent = denoise(near, far, slots, *weights, split)
+    sent, choice = lax.optimization_barrier((sent, choice))
     came = lax.all_to_all(sent, "tile", 0, 0, tiled=True)
-    stacked, *parts = stack(came, moveout_maps, groups)
-    for apart, part in enumerate(parts, 1):
-        stacked = stacked + lax.ppermute(part, "grp", [(g, g ^ apart) for g in range(groups)])
+    stacked, *parts = stack(came, choice, moveout_maps, groups)
+    for apart in (2, 1, 3):
+        part = lax.ppermute(parts[apart - 1], "grp", [(g, g ^ apart) for g in range(groups)])
+        stacked = stacked + part
     return denoised, stacked
 
 

time: 67.6 us -> 146 us (2.16)
  waiting for transfers between devices: 5.48 us -> 75.7 us
  between operations: 0.7 us -> 14.1 us
  blocking collectives: 18.3 us -> 13.6 us
  starting transfers between devices: 9.27 us -> 4.98 us
  local copies, waits for them, and re-layouts: 1.14 us -> 4.16 us
  other arithmetic: 0.7 us -> 2.2 us
    psum x0 -> x1, waiting for transfers between devices: none -> 71.2 us  [on_device(): choice = lax.psum(choice, 'tile')]
    all_to_all x1, blocking collectives: 18.3 us -> 13.6 us  [on_device(): came = lax.all_to_all(sent, 'tile', 0, 0, tiled=True)]
    unnamed x2 -> x4, local copies, waits for them, and re-layouts: 0.01 us -> 3.03 us
    ppermute x1, starting transfers between devices: 3.01 us -> 0.09 us  [on_device(): near = lax.ppermute(near, 'tile', [(i, i ^ 1) for i in range(tiles)])]
  transfers between devices with their start and end apart: 5 -> 6, of which waited for: 2 -> 3; matrix products, arithmetic and copies ran while one was open for 0% -> 1% of each run, Pallas kernels for 3% -> 20%
where the time goes in v7:
time: 146 us; the launch traced here: 145 us
  waiting for transfers between devices  75.7 us (52%)
  Pallas kernels  30.6 us (21%)
  between operations  14.1 us (10%)
  blocking collectives  13.6 us (9%)
  starting transfers between devices  4.98 us (3%)
  local copies, waits for them, and re-layouts  4.16 us (3%)
  other arithmetic  2.2 us (2%)
    psum x1, waiting for transfers between devices, on_device(): choice = lax.psum(choice, 'tile')  71.2 us
    pallas_call x1, Pallas kernels, denoise(): pl.pallas_call(denoise_body, out_shape=(jax.ShapeDtypeStruct((shots, RD,...  27 us
    all_to_all x1, blocking collectives, on_device(): came = lax.all_to_all(sent, 'tile', 0, 0, tiled=True)  13.6 us
    ppermute x3, waiting for transfers between devices, on_device(): lax.ppermute(parts[apart - 1], 'grp', [(g, g ^ apart) for g in range(grou...  4.41 us
    ppermute x3, starting transfers between devices, on_device(): lax.ppermute(parts[apart - 1], 'grp', [(g, g ^ apart) for g in range(grou...  4.19 us
    unnamed x4, local copies, waits for them, and re-layouts  3.03 us
  transfers between devices with their start and end apart: 6, of which 3 were waited for; matrix products, arithmetic and copies ran while one was open for 1% of the time, Pallas kernels for 20%

profile of v7, /device:TPU:0, one launch (start us, length us, event | category | flops | bytes accessed | tf_op | source)
XLA Modules:
  0.0 145.3 jit_solution(15071908652179581804)
XLA Ops:
  7.2 0.0 all-reduce.2.cloned.1.call-start
  7.2 1.1 fusion
  8.4 0.1 collective-permute-start
  8.5 0.7 collective-permute-start.1
  9.2 0.8 add_convert_fusion
  9.9 0.7 broadcast_select_fusion
  10.7 0.0 all-reduce.2.cloned.1.call-update
  10.7 2.0 %prepare.1 = (bf16[1536,256]{1,0:T(8,128)(2,1)S(1)}, bf16[128,768]{1,0:T(8,128)(2,1)S(1)}, bf16[32,1280]{1,0:T(8,128)(2,1)S(1)}, bf16[512,1024]{1,0:T(8,128)(2,1)S(1)}, bf16[32,32,256]{2,1,0:T(8,128)(2,1)S(1)}) custom-call(bf16[9,64]{1,0:T(8,128)(2,1)} %tap1_ref.1, bf16[576,64]{1,0:T(8,128)(2,1)} %bitcast.14, bf16[9,64]{1,0:T(8,128)(2,1)} %tap3_ref.1, ...), custom_call_target="tpu_custom_call" | custom-call | tf_op jit(solution)/shard_map/prepare/pallas_call | solution.py:119
  12.7 0.0 collective-permute-done.refs_0_
  12.7 0.0 collective-permute-done.1.refs_1_
  12.7 27.0 %denoise.1 = (bf16[32,8,512]{2,1,0:T(8,128)(2,1)}, bf16[32,8,512]{2,1,0:T(8,128)(2,1)S(1)}) custom-call(bf16[3,32,512]{2,1,0:T(8,128)(2,1)S(1)} %collective-permute-done.refs_0_, bf16[3,32,512]{2,1,0:T(8,128)(2,1)S(1)} %collective-permute-done.1.refs_1_, bf16[32,32,256]{2,1,0:T(8,128)(2,1)S(1)} %get-tuple-element.15.refs_2_, ...), custom_call_target="tpu_custom_call" | custom-call | flops 9965666304 | bytes 4194304 | tf_op jit(solution)/shard_map/denoise/pallas_call | solution.py:326
  39.7 71.2 %all-reduce.2.cloned.1.call-done.choice_ref = f32[32,4,128]{2,1,0:T(4,128)} async-done(((f32[32,4,128]{2,1,0:T(4,128)}), f32[32,4,128]{2,1,0:T(4,128)}) %all-reduce.2.cloned.1.call-update) | async-done | bytes 65552 | tf_op jit(solution)/shard_map/psum | solution.py:413
  110.9 13.6 %all_to_all.5.came_ref = bf16[32,8,512]{2,1,0:T(8,128)(2,1)S(1)} all-to-all(bf16[32,8,512]{2,1,0:T(8,128)(2,1)S(1)} %get-tuple-element.22), channel_id=1, replica_groups=mesh['grp'=4,'tile'=32] {'tile'}, dimensions={0} | all-to-all | bytes 524288 | tf_op jit(solution)/shard_map/all_to_all | solution.py:421
  124.5 0.0 copy-start
  124.5 2.2 %copy-done = bf16[8,512,512]{2,1,0:T(8,128)(2,1)S(1)} copy-done((bf16[8,512,512]{2,1,0:T(8,128)(2,1)S(1)}, bf16[8,512,512]{2,1,0:T(8,128)(2,1)}, u32[]{:S(2)}) %copy-start) | copy-done | bytes 4194328
  126.7 0.8 copy-done.1
  127.5 1.7 %stack.1 = (f32[8,4,512]{2,1,0:T(4,128)S(1)}, f32[8,4,512]{2,1,0:T(4,128)S(1)}, f32[8,4,512]{2,1,0:T(4,128)S(1)}, f32[8,4,512]{2,1,0:T(4,128)S(1)}) custom-call(bf16[32,8,512]{2,1,0:T(8,128)(2,1)S(1)} %all_to_all.5.came_ref, f32[32,4,128]{2,1,0:T(4,128)S(1)} %copy-done.1, bf16[4096,512]{1,0:T(8,128)(2,1)S(1)} %bitcast.12), custom_call_target="tpu_custom_call" | custom-call | tf_op jit(solution)/shard_map/stack/pallas_call | solution.py:383
  129.2 3.1 %collective-permute-start.2 = (f32[8,4,512]{2,1,0:T(4,128)S(1)}, f32[8,4,512]{2,1,0:T(4,128)S(1)}, u32[]{:S(2)}, u32[]{:S(2)}) collective-permute-start(f32[8,4,512]{2,1,0:T(4,128)S(1)} %get-tuple-element.25), channel_id=1, source_target_pairs={{0,64},{32,96},{64,0},{96,32},{1,65},{33,97},{65,1},{97,33},{2,66}... | collective-permute-start | bytes 196616 | tf_op jit(solution)/shard_map/ppermute | solution.py:424
  132.3 1.1 collective-permute-start.4
  133.4 0.0 collective-permute-start.3
  133.4 1.7 %collective-permute-done.2 = f32[8,4,512]{2,1,0:T(4,128)S(1)} collective-permute-done((f32[8,4,512]{2,1,0:T(4,128)S(1)}, f32[8,4,512]{2,1,0:T(4,128)S(1)}, u32[]{:S(2)}, u32[]{:S(2)}) %collective-permute-start.2) | collective-permute-done | bytes 65568 | tf_op jit(solution)/shard_map/ppermute | solution.py:424
  135.1 2.7 %collective-permute-done.4 = f32[8,4,512]{2,1,0:T(4,128)S(1)} collective-permute-done((f32[8,4,512]{2,1,0:T(4,128)S(1)}, f32[8,4,512]{2,1,0:T(4,128)S(1)}, u32[]{:S(2)}, u32[]{:S(2)}) %collective-permute-start.4) | collective-permute-done | bytes 65568 | tf_op jit(solution)/shard_map/ppermute | solution.py:424
  137.8 0.0 collective-permute-done.3
  137.8 0.6 add_add_fusion
  (3 shorter events, 0.1 us)
Async XLA Ops:
  7.2 103.8 %all-reduce.2.cloned.1.call-start = ((), (), s32[]{:S(2)}) async-start(), calls=%async_computation.1 | async-start | bytes 131072 | tf_op jit(solution)/shard_map/psum | solution.py:413
  8.4 4.3 %collective-permute-start = (bf16[3,32,512]{2,1,0:T(8,128)(2,1)S(1)}, bf16[3,32,512]{2,1,0:T(8,128)(2,1)S(1)}, u32[]{:S(2)}, u32[]{:S(2)}) collective-permute-start(bf16[3,32,512]{2,1,0:T(8,128)(2,1)S(1)} %get-tuple-element.29), channel_id=1, source_target_pairs={{0,1},{1,0},{2,3},{3,2},{4,5},{5,4},{6,7},{7,6},{8,9},{9,8},{10,11... | collective-permute-start | bytes 294920 | tf_op jit(solution)/shard_map/ppermute | solution.py:415
  8.5 4.2 %collective-permute-start.1 = (bf16[3,32,512]{2,1,0:T(8,128)(2,1)S(1)}, bf16[3,32,512]{2,1,0:T(8,128)(2,1)S(1)}, u32[]{:S(2)}, u32[]{:S(2)}) collective-permute-start(bf16[3,32,512]{2,1,0:T(8,128)(2,1)S(1)} %get-tuple-element.28), channel_id=1, source_target_pairs={{1,2},{3,4},{5,6},{7,8},{9,10},{11,12},{13,14},{15,16},{17,18},{19... | collective-permute-start | bytes 294920 | tf_op jit(solution)/shard_map/ppermute | solution.py:417
  124.5 2.2 %copy-start = (bf16[8,512,512]{2,1,0:T(8,128)(2,1)S(1)}, bf16[8,512,512]{2,1,0:T(8,128)(2,1)}, u32[]{:S(2)}) copy-start(bf16[8,512,512]{2,1,0:T(8,128)(2,1)} %param.11) | copy-start | bytes 12582916
  126.7 0.8 copy-start.1
  129.2 5.9 %collective-permute-start.2 = (f32[8,4,512]{2,1,0:T(4,128)S(1)}, f32[8,4,512]{2,1,0:T(4,128)S(1)}, u32[]{:S(2)}, u32[]{:S(2)}) collective-permute-start(f32[8,4,512]{2,1,0:T(4,128)S(1)} %get-tuple-element.25), channel_id=1, source_target_pairs={{0,64},{32,96},{64,0},{96,32},{1,65},{33,97},{65,1},{97,33},{2,66}... | collective-permute-start | bytes 196616 | tf_op jit(solution)/shard_map/ppermute | solution.py:424
  132.3 5.5 %collective-permute-start.4 = (f32[8,4,512]{2,1,0:T(4,128)S(1)}, f32[8,4,512]{2,1,0:T(4,128)S(1)}, u32[]{:S(2)}, u32[]{:S(2)}) collective-permute-start(f32[8,4,512]{2,1,0:T(4,128)S(1)} %get-tuple-element.27), channel_id=1, source_target_pairs={{0,96},{32,64},{64,32},{96,0},{1,97},{33,65},{65,33},{97,1},{2,98}... | collective-permute-start | bytes 196616 | tf_op jit(solution)/shard_map/ppermute | solution.py:424
  133.4 4.4 %collective-permute-start.3 = (f32[8,4,512]{2,1,0:T(4,128)S(1)}, f32[8,4,512]{2,1,0:T(4,128)S(1)}, u32[]{:S(2)}, u32[]{:S(2)}) collective-permute-start(f32[8,4,512]{2,1,0:T(4,128)S(1)} %get-tuple-element.26), channel_id=1, source_target_pairs={{0,32},{32,0},{64,96},{96,64},{1,33},{33,1},{65,97},{97,65},{2,34}... | collective-permute-start | bytes 196616 | tf_op jit(solution)/shard_map/ppermute | solution.py:424
Sparse Core Ops, SparseCore 0:
  11.8 99.0 all-reduce.1

commit v8 on v6

--- a/solution.py
+++ b/solution.py
@@ -20,6 +20,7 @@
 INNER = RD + 2
 EDGE = 3
 SIDE = 16
+STAGES = 4
 F32 = jnp.float32
 BF16 = jnp.bfloat16
 
@@ -271,20 +272,23 @@
         jobs[-1][2].extend(tail)
         run(jobs)
 
-    chain(stage(None, (0, h1_even), None))
-    chain(stage((h1_even, h2_even), (1, h1_odd), None))
-
-    def two(step, carry):
-        pair = 2 * step + 1
-        chain(
-            stage((h1_odd, h2_odd), (pair + 1, h1_even), (pair - 1, h2_even)),
-            stage((h1_even, h2_even), (pair + 2, h1_odd), (pair, h2_odd)),
-        )
+    buffers = ((h1_even, h2_even), (h1_odd, h2_odd))
+
+    def full(pair, parity):
+        now, other = buffers[parity], buffers[1 - parity]
+        return stage(now, (pair + 1, other[0]), (pair - 1, other[1]))
+
+    def several(step, carry):
+        pair = STAGES * step + 1
+        chain(*[full(pair + n, (n + 1) % 2) for n in range(STAGES)])
         return carry
 
-    lax.fori_loop(0, (pairs - 2) // 2, two, 0)
-    chain(stage((h1_odd, h2_odd), None, (pairs - 2, h2_even)))
-    chain(([last_job(h2_odd, n) for n in range(INNER // 2)], [last_done(pairs - 1)]))
+    chain(stage(None, (0, h1_even), None), stage(buffers[0], (1, h1_odd), None))
+    steps = (pairs - 2) // STAGES
+    lax.fori_loop(0, steps, several, 0)
+    rest = [full(pair, pair % 2) for pair in range(STAGES * steps + 1, pairs - 1)]
+    end = [last_job(h2_odd, n) for n in range(INNER // 2)], [last_done(pairs - 1)]
+    chain(*rest, stage(buffers[1], None, (pairs - 2, h2_even)), end)
 
     lane = lax.broadcasted_iota(jnp.int32, (NT, NT), 0)
     time = lax.broadcasted_iota(jnp.int32, (NT, NT), 1)
@@ -299,11 +303,15 @@
         rows4[:, c * kept : (c + 1) * kept, lanes] = part.reshape(owners, kept, UNIT)
 
     product(accs, cleaned[...].astype(BF16), merge, put)
-    shape = (owners, kept, LANES // 2)
+    sent_ref[:, :, :NT] = rows4[...].astype(BF16)
+    shape = (sent_ref.shape[1], LANES)
+    block = lax.broadcasted_iota(jnp.int32, shape, 0) // kept
+    first_half = lax.broadcasted_iota(jnp.int32, shape, 1) < LANES // 2
+    tag = jnp.zeros(shape, jnp.int32)
     for c in range(shots * RD // BLK):
-        rows4[:, c * kept : (c + 1) * kept, NT : NT + LANES // 2] = jnp.full(shape, target_ref[c].astype(F32))
-        rows4[:, c * kept : (c + 1) * kept, NT + LANES // 2 :] = jnp.full(shape, offset_ref[c].astype(F32))
-    sent_ref[...] = rows4[...].astype(BF16)
+        tag = jnp.where(block == c, jnp.where(first_half, target_ref[c], offset_ref[c]), tag)
+    tag = tag.astype(F32).astype(BF16)
+    sent_ref[:, :, NT:] = jnp.broadcast_to(tag[None], (owners, *shape))
 
 
 def denoise_body(*refs):
@@ -332,7 +340,7 @@
         scratch_shapes=[pltpu.VMEM((HALF // LANES, shots * SIDE, LANES), F32)] * 2
         + [pltpu.VMEM((UNITS, OUTER, UNIT, HALF), BF16)] * 2
         + [pltpu.VMEM((UNITS, INNER * 2 * CH, HALF), BF16)] * 2
-        + [pltpu.VMEM((shots * RD, NT), F32), pltpu.VMEM(sent, F32)],
+        + [pltpu.VMEM((shots * RD, NT), F32), pltpu.VMEM((*sent[:2], NT), F32)],
         compiler_params=pltpu.CompilerParams(vmem_limit_bytes=40 << 20),
         cost_estimate=pl.CostEstimate(flops=2 * macs, transcendentals=0, bytes_accessed=4 << 20),
         name="denoise",
@@ -409,8 +417,9 @@
     denoised, sent = denoise(block_offset, block_target, near, far, slots, *weights, split)
     came = lax.all_to_all(sent, "tile", 0, 0, tiled=True)
     stacked, *parts = stack(came, moveout_maps, groups)
-    for apart, part in enumerate(parts, 1):
-        stacked = stacked + lax.ppermute(part, "grp", [(g, g ^ apart) for g in range(groups)])
+    for apart in (2, 1, 3):
+        part = lax.ppermute(parts[apart - 1], "grp", [(g, g ^ apart) for g in range(groups)])
+        stacked = stacked + part
     return denoised, stacked
 
 

time: 67.6 us -> 66.5 us (0.984)
  transfers between devices with their start and end apart: 5 -> 5, of which waited for: 2 -> 3; matrix products, arithmetic and copies ran while one was open for 0% -> 0% of each run, Pallas kernels for 3% -> 3%
where the time goes in v8:
time: 66.5 us; the launch traced here: 66.3 us
  Pallas kernels  31.3 us (47%)
  blocking collectives  18.3 us (28%)
  starting transfers between devices  8.65 us (13%)
  waiting for transfers between devices  5.48 us (8%)
  local copies, waits for them, and re-layouts  1.14 us (2%)
  other arithmetic  0.7 us (1%)
  between operations  0.7 us (1%)
    pallas_call x1, Pallas kernels, denoise(): pl.pallas_call(denoise_body, out_shape=(jax.ShapeDtypeStruct((shots, RD,...  27.8 us
    all_to_all x1, blocking collectives, on_device(): came = lax.all_to_all(sent, 'tile', 0, 0, tiled=True)  18.3 us
    ppermute x3, waiting for transfers between devices, on_device(): lax.ppermute(parts[apart - 1], 'grp', [(g, g ^ apart) for g in range(grou...  5.47 us
    ppermute x3, starting transfers between devices, on_device(): lax.ppermute(parts[apart - 1], 'grp', [(g, g ^ apart) for g in range(grou...  4.98 us
    ppermute x1, starting transfers between devices, on_device(): near = lax.ppermute(near, 'tile', [(i, i ^ 1) for i in range(tiles)])  3.01 us
    pallas_call x1, Pallas kernels, prepare(): pl.pallas_call(prepare_body, out_shape=tuple((jax.ShapeDtypeStruct(s, BF1...  1.99 us
    pallas_call x1, Pallas kernels, stack(): pl.pallas_call(stack_body, out_shape=(part,) * groups, compiler_params=pl...  1.57 us
  transfers between devices with their start and end apart: 5, of which 3 were waited for; matrix products, arithmetic and copies ran while one was open for 0% of the time, Pallas kernels for 3%

profile of v8, /device:TPU:0, one launch (start us, length us, event | category | flops | bytes accessed | tf_op | source)
XLA Modules:
  0.0 66.3 jit_solution(13657082070375677865)
XLA Ops:
  0.6 1.1 %fusion = (bf16[32,3,512]{2,1,0:T(4,128)(2,1)S(1)}, bf16[32,3,512]{2,1,0:T(4,128)(2,1)S(1)}) fusion(bf16[32,8,512]{2,1,0:T(8,128)(2,1)} %own_ref.1), kind=kLoop, calls=%fused_computation.3 | loop fusion | bytes 393216 | tf_op jit(solution)/shard_map/slice | solution.py:393
  1.8 0.7 %collective-permute-start.1 = (bf16[3,32,512]{2,1,0:T(8,128)(2,1)S(1)}, bf16[3,32,512]{2,1,0:T(8,128)(2,1)S(1)}, u32[]{:S(2)}, u32[]{:S(2)}) collective-permute-start(bf16[3,32,512]{2,1,0:T(8,128)(2,1)S(1)} %get-tuple-element.24), channel_id=1, source_target_pairs={{1,2},{3,4},{5,6},{7,8},{9,10},{11,12},{13,14},{15,16},{17,18},{19... | collective-permute-start | bytes 294920 | tf_op jit(solution)/shard_map/ppermute | solution.py:415
  2.5 3.0 %collective-permute-start = (bf16[3,32,512]{2,1,0:T(8,128)(2,1)S(1)}, bf16[3,32,512]{2,1,0:T(8,128)(2,1)S(1)}, u32[]{:S(2)}, u32[]{:S(2)}) collective-permute-start(bf16[3,32,512]{2,1,0:T(8,128)(2,1)S(1)} %get-tuple-element.25), channel_id=1, source_target_pairs={{0,1},{1,0},{2,3},{3,2},{4,5},{5,4},{6,7},{7,6},{8,9},{9,8},{10,11... | collective-permute-start | bytes 294920 | tf_op jit(solution)/shard_map/ppermute | solution.py:413
  5.5 2.0 %prepare.1 = (bf16[1536,256]{1,0:T(8,128)(2,1)S(1)}, bf16[128,768]{1,0:T(8,128)(2,1)S(1)}, bf16[32,1280]{1,0:T(8,128)(2,1)S(1)}, bf16[512,1024]{1,0:T(8,128)(2,1)S(1)}, bf16[32,32,256]{2,1,0:T(8,128)(2,1)S(1)}) custom-call(bf16[9,64]{1,0:T(8,128)(2,1)} %tap1_ref.1, bf16[576,64]{1,0:T(8,128)(2,1)} %bitcast.14, bf16[9,64]{1,0:T(8,128)(2,1)} %tap3_ref.1, ...), custom_call_target="tpu_custom_call" | custom-call | tf_op jit(solution)/shard_map/prepare/pallas_call | solution.py:119
  7.5 0.0 collective-permute-done.1.refs_3_
  7.5 0.0 collective-permute-done.refs_2_
  7.5 0.0 copy-start
  7.6 27.8 %denoise.1 = (bf16[32,8,512]{2,1,0:T(8,128)(2,1)}, bf16[32,8,640]{2,1,0:T(8,128)(2,1)S(1)}) custom-call(s32[2]{0:T(128)} %refs_0_.1, s32[2]{0:T(128)} %bitcast.19, bf16[3,32,512]{2,1,0:T(8,128)(2,1)S(1)} %collective-permute-done.refs_2_, bf16[3,32,512]{2,1,0:T(8,128)(2,1)S(1)} %collective-permute-done.1.refs_3_, ...), custom_call_target="tpu_custom_call" | custom-call | flops 9965666304 | bytes 4194304 | tf_op jit(solution)/shard_map/denoise/pallas_call | solution.py:335
  35.3 18.3 %all_to_all.5.came_ref = bf16[32,8,640]{2,1,0:T(8,128)(2,1)S(1)} all-to-all(bf16[32,8,640]{2,1,0:T(8,128)(2,1)S(1)} %get-tuple-element.19), channel_id=1, replica_groups=mesh['grp'=4,'tile'=32] {'tile'}, dimensions={0} | all-to-all | bytes 655360 | tf_op jit(solution)/shard_map/all_to_all | solution.py:418
  53.6 0.0 copy-done
  53.6 1.6 %stack.1 = (f32[8,4,512]{2,1,0:T(4,128)S(1)}, f32[8,4,512]{2,1,0:T(4,128)S(1)}, f32[8,4,512]{2,1,0:T(4,128)S(1)}, f32[8,4,512]{2,1,0:T(4,128)S(1)}) custom-call(bf16[32,8,640]{2,1,0:T(8,128)(2,1)S(1)} %all_to_all.5.came_ref, bf16[4096,512]{1,0:T(8,128)(2,1)S(1)} %bitcast.12), custom_call_target="tpu_custom_call" | custom-call | tf_op jit(solution)/shard_map/stack/pallas_call | solution.py:383
  55.2 4.0 %collective-permute-start.2 = (f32[8,4,512]{2,1,0:T(4,128)S(1)}, f32[8,4,512]{2,1,0:T(4,128)S(1)}, u32[]{:S(2)}, u32[]{:S(2)}) collective-permute-start(f32[8,4,512]{2,1,0:T(4,128)S(1)} %get-tuple-element.21), channel_id=1, source_target_pairs={{0,64},{32,96},{64,0},{96,32},{1,65},{33,97},{65,1},{97,33},{2,66}... | collective-permute-start | bytes 196616 | tf_op jit(solution)/shard_map/ppermute | solution.py:421
  59.1 1.0 %collective-permute-start.3 = (f32[8,4,512]{2,1,0:T(4,128)S(1)}, f32[8,4,512]{2,1,0:T(4,128)S(1)}, u32[]{:S(2)}, u32[]{:S(2)}) collective-permute-start(f32[8,4,512]{2,1,0:T(4,128)S(1)} %get-tuple-element.22), channel_id=1, source_target_pairs={{0,32},{32,0},{64,96},{96,64},{1,33},{33,1},{65,97},{97,65},{2,34}... | collective-permute-start | bytes 196616 | tf_op jit(solution)/shard_map/ppermute | solution.py:421
  60.2 0.0 collective-permute-start.4
  60.2 1.5 %collective-permute-done.2 = f32[8,4,512]{2,1,0:T(4,128)S(1)} collective-permute-done((f32[8,4,512]{2,1,0:T(4,128)S(1)}, f32[8,4,512]{2,1,0:T(4,128)S(1)}, u32[]{:S(2)}, u32[]{:S(2)}) %collective-permute-start.2) | collective-permute-done | bytes 65568 | tf_op jit(solution)/shard_map/ppermute | solution.py:421
  61.6 2.1 %collective-permute-done.3 = f32[8,4,512]{2,1,0:T(4,128)S(1)} collective-permute-done((f32[8,4,512]{2,1,0:T(4,128)S(1)}, f32[8,4,512]{2,1,0:T(4,128)S(1)}, u32[]{:S(2)}, u32[]{:S(2)}) %collective-permute-start.3) | collective-permute-done | bytes 65568 | tf_op jit(solution)/shard_map/ppermute | solution.py:421
  63.8 1.9 %collective-permute-done.4 = f32[8,4,512]{2,1,0:T(4,128)S(1)} collective-permute-done((f32[8,4,512]{2,1,0:T(4,128)S(1)}, f32[8,4,512]{2,1,0:T(4,128)S(1)}, u32[]{:S(2)}, u32[]{:S(2)}) %collective-permute-start.4) | collective-permute-done | bytes 65568 | tf_op jit(solution)/shard_map/ppermute | solution.py:421
  65.6 0.6 add_add_fusion
  (1 shorter events, 0.0 us)
Async XLA Ops:
  1.8 5.7 %collective-permute-start.1 = (bf16[3,32,512]{2,1,0:T(8,128)(2,1)S(1)}, bf16[3,32,512]{2,1,0:T(8,128)(2,1)S(1)}, u32[]{:S(2)}, u32[]{:S(2)}) collective-permute-start(bf16[3,32,512]{2,1,0:T(8,128)(2,1)S(1)} %get-tuple-element.24), channel_id=1, source_target_pairs={{1,2},{3,4},{5,6},{7,8},{9,10},{11,12},{13,14},{15,16},{17,18},{19... | collective-permute-start | bytes 294920 | tf_op jit(solution)/shard_map/ppermute | solution.py:415
  2.5 5.0 %collective-permute-start = (bf16[3,32,512]{2,1,0:T(8,128)(2,1)S(1)}, bf16[3,32,512]{2,1,0:T(8,128)(2,1)S(1)}, u32[]{:S(2)}, u32[]{:S(2)}) collective-permute-start(bf16[3,32,512]{2,1,0:T(8,128)(2,1)S(1)} %get-tuple-element.25), channel_id=1, source_target_pairs={{0,1},{1,0},{2,3},{3,2},{4,5},{5,4},{6,7},{7,6},{8,9},{9,8},{10,11... | collective-permute-start | bytes 294920 | tf_op jit(solution)/shard_map/ppermute | solution.py:413
  7.5 46.1 %copy-start = (bf16[8,512,512]{2,1,0:T(8,128)(2,1)S(1)}, bf16[8,512,512]{2,1,0:T(8,128)(2,1)}, u32[]{:S(2)}) copy-start(bf16[8,512,512]{2,1,0:T(8,128)(2,1)} %param.11) | copy-start | bytes 12582916
  55.2 6.4 %collective-permute-start.2 = (f32[8,4,512]{2,1,0:T(4,128)S(1)}, f32[8,4,512]{2,1,0:T(4,128)S(1)}, u32[]{:S(2)}, u32[]{:S(2)}) collective-permute-start(f32[8,4,512]{2,1,0:T(4,128)S(1)} %get-tuple-element.21), channel_id=1, source_target_pairs={{0,64},{32,96},{64,0},{96,32},{1,65},{33,97},{65,1},{97,33},{2,66}... | collective-permute-start | bytes 196616 | tf_op jit(solution)/shard_map/ppermute | solution.py:421
  59.1 4.6 %collective-permute-start.3 = (f32[8,4,512]{2,1,0:T(4,128)S(1)}, f32[8,4,512]{2,1,0:T(4,128)S(1)}, u32[]{:S(2)}, u32[]{:S(2)}) collective-permute-start(f32[8,4,512]{2,1,0:T(4,128)S(1)} %get-tuple-element.22), channel_id=1, source_target_pairs={{0,32},{32,0},{64,96},{96,64},{1,33},{33,1},{65,97},{97,65},{2,34}... | collective-permute-start | bytes 196616 | tf_op jit(solution)/shard_map/ppermute | solution.py:421
  60.2 5.5 %collective-permute-start.4 = (f32[8,4,512]{2,1,0:T(4,128)S(1)}, f32[8,4,512]{2,1,0:T(4,128)S(1)}, u32[]{:S(2)}, u32[]{:S(2)}) collective-permute-start(f32[8,4,512]{2,1,0:T(4,128)S(1)} %get-tuple-element.23), channel_id=1, source_target_pairs={{0,96},{32,64},{64,32},{96,0},{1,97},{33,65},{65,33},{97,1},{2,98}... | collective-permute-start | bytes 196616 | tf_op jit(solution)/shard_map/ppermute | solution.py:421

commit v9 on v8

--- a/solution.py
+++ b/solution.py
@@ -125,18 +125,24 @@
     )(weight_first, weight_middle, weight_last, own)
 
 
-def product(accs, lhs, rhs, use):
-    rows, depth = lhs.shape
-    for n in range(rhs.shape[1] // UNIT):
-        held = accs[n % UNITS]
-        for k in range(depth // UNIT):
-            piece = rhs[k * UNIT : (k + 1) * UNIT, n * UNIT : (n + 1) * UNIT]
-            pltpu.matmul_push_rhs(piece, k % 2, n % UNITS)
-            for c in range(rows // BLK):
-                piece = lhs[c * BLK : (c + 1) * BLK, k * UNIT : (k + 1) * UNIT]
-                pltpu.matmul_acc_lhs(held[c], piece, load_staged_rhs=k % 2 if c == 0 else None)
-        for c in range(rows // BLK):
-            use(n, c, pltpu.matmul_pop(held[c]))
+def products(accs, items):
+    taken = [0] * UNITS
+    done = []
+    for lhs, rhs, use in items:
+        rows, depth = lhs.shape
+        for n in range(rhs.shape[1] // UNIT):
+            unit = n % UNITS
+            held = accs[unit][taken[unit] : taken[unit] + rows // BLK]
+            taken[unit] += len(held)
+            for k in range(depth // UNIT):
+                piece = rhs[k * UNIT : (k + 1) * UNIT, n * UNIT : (n + 1) * UNIT]
+                pltpu.matmul_push_rhs(piece, k % 2, unit)
+                for c, acc in enumerate(held):
+                    piece = lhs[c * BLK : (c + 1) * BLK, k * UNIT : (k + 1) * UNIT]
+                    pltpu.matmul_acc_lhs(acc, piece, load_staged_rhs=k % 2 if c == 0 else None)
+            done += [(use, n, c, acc) for c, acc in enumerate(held)]
+    for use, n, c, acc in done:
+        use(n, c, pltpu.matmul_pop(acc))
 
 
 def run(jobs):
@@ -164,8 +170,9 @@
     pairs = shots // UNITS
     per_block = BLK // RD
 
+    items = []
     for ref, held in ((near_ref, near), (far_ref, far)):
-        def put(slot, c, part, held=held):
+        def keep(slot, c, part, held=held):
             for row in range(4):
                 at = pl.ds(slot * 4 + row, shots, stride=SIDE)
                 for half in range(HALF // LANES):
@@ -174,7 +181,8 @@
 
         edge = ref[...].reshape(EDGE * shots, NT)
         rest = jnp.zeros((BLK - EDGE * shots, NT), BF16)
-        product(accs, jnp.concatenate([edge, rest], axis=0), split_ref, put)
+        items.append((jnp.concatenate([edge, rest], axis=0), split_ref, keep))
+    products(accs, items)
 
     def taps(pair):
         def right(unit):
@@ -302,7 +310,7 @@
         denoised_ref[shot, :, lanes] = part.astype(BF16).reshape(per_block, RD, UNIT)
         rows4[:, c * kept : (c + 1) * kept, lanes] = part.reshape(owners, kept, UNIT)
 
-    product(accs, cleaned[...].astype(BF16), merge, put)
+    products(accs, [(cleaned[...].astype(BF16), merge, put)])
     sent_ref[:, :, :NT] = rows4[...].astype(BF16)
     shape = (sent_ref.shape[1], LANES)
     block = lax.broadcasted_iota(jnp.int32, shape, 0) // kept
@@ -334,7 +342,7 @@
     macs = shots * RD * NT * CH * (9 * CH + 18)
     return pl.pallas_call(
         denoise_body,
-        out_shape=(jax.ShapeDtypeStruct((shots, RD, NT), BF16), jax.ShapeDtypeStruct(sent, BF16)),
+        out_shape=(pltpu.VMEM((shots, RD, NT), BF16), jax.ShapeDtypeStruct(sent, BF16)),
         in_specs=[scalars] * 2 + [whole] * 7,
         out_specs=(whole, whole),
         scratch_shapes=[pltpu.VMEM((HALF // LANES, shots * SIDE, LANES), F32)] * 2

time: 66.5 us -> 65.5 us (0.985)
  Pallas kernels: 31.3 us -> 30.3 us
  waiting for transfers between devices: 5.48 us -> 4.77 us
  local copies, waits for them, and re-layouts: 1.14 us -> 1.85 us
    pallas_call x1, Pallas kernels: 27.8 us -> 26.8 us  [denoise(): pl.pallas_call(denoise_body, out_shape=(pltpu.VMEM((shots, RD, NT), BF16)...]
    ppermute x3, waiting for transfers between devices: 5.47 us -> 4.77 us  [on_device(): lax.ppermute(parts[apart - 1], 'grp', [(g, g ^ apart) for g in range(grou...]
    unnamed x2 -> x3, local copies, waits for them, and re-layouts: 0.01 us -> 0.71 us
  transfers between devices with their start and end apart: 5 -> 5, of which waited for: 3 -> 3; matrix products, arithmetic and copies ran while one was open for 0% -> 1% of each run, Pallas kernels for 3% -> 3%
where the time goes in v9:
time: 65.5 us; the launch traced here: 65.3 us
  Pallas kernels  30.3 us (46%)
  blocking collectives  18.3 us (28%)
  starting transfers between devices  8.67 us (13%)
  waiting for transfers between devices  4.77 us (7%)
  local copies, waits for them, and re-layouts  1.85 us (3%)
  between operations  0.71 us (1%)
  other arithmetic  0.7 us (1%)
    pallas_call x1, Pallas kernels, denoise(): pl.pallas_call(denoise_body, out_shape=(pltpu.VMEM((shots, RD, NT), BF16)...  26.8 us
    all_to_all x1, blocking collectives, on_device(): came = lax.all_to_all(sent, 'tile', 0, 0, tiled=True)  18.3 us
    ppermute x3, starting transfers between devices, on_device(): lax.ppermute(parts[apart - 1], 'grp', [(g, g ^ apart) for g in range(grou...  4.99 us
    ppermute x3, waiting for transfers between devices, on_device(): lax.ppermute(parts[apart - 1], 'grp', [(g, g ^ apart) for g in range(grou...  4.77 us
    ppermute x1, starting transfers between devices, on_device(): near = lax.ppermute(near, 'tile', [(i, i ^ 1) for i in range(tiles)])  3.01 us
    pallas_call x1, Pallas kernels, prepare(): pl.pallas_call(prepare_body, out_shape=tuple((jax.ShapeDtypeStruct(s, BF1...  1.99 us
    pallas_call x1, Pallas kernels, stack(): pl.pallas_call(stack_body, out_shape=(part,) * groups, compiler_params=pl...  1.57 us
  transfers between devices with their start and end apart: 5, of which 3 were waited for; matrix products, arithmetic and copies ran while one was open for 1% of the time, Pallas kernels for 3%

profile of v9, /device:TPU:0, one launch (start us, length us, event | category | flops | bytes accessed | tf_op | source)
XLA Modules:
  0.0 65.3 jit_solution(10109986656028496424)
XLA Ops:
  0.6 1.1 %fusion = (bf16[32,3,512]{2,1,0:T(4,128)(2,1)S(1)}, bf16[32,3,512]{2,1,0:T(4,128)(2,1)S(1)}) fusion(bf16[32,8,512]{2,1,0:T(8,128)(2,1)} %own_ref.1), kind=kLoop, calls=%fused_computation.3 | loop fusion | bytes 393216 | tf_op jit(solution)/shard_map/slice | solution.py:401
  1.8 0.7 %collective-permute-start.1 = (bf16[3,32,512]{2,1,0:T(8,128)(2,1)S(1)}, bf16[3,32,512]{2,1,0:T(8,128)(2,1)S(1)}, u32[]{:S(2)}, u32[]{:S(2)}) collective-permute-start(bf16[3,32,512]{2,1,0:T(8,128)(2,1)S(1)} %get-tuple-element.24), channel_id=1, source_target_pairs={{1,2},{3,4},{5,6},{7,8},{9,10},{11,12},{13,14},{15,16},{17,18},{19... | collective-permute-start | bytes 294920 | tf_op jit(solution)/shard_map/ppermute | solution.py:423
  2.5 3.0 %collective-permute-start = (bf16[3,32,512]{2,1,0:T(8,128)(2,1)S(1)}, bf16[3,32,512]{2,1,0:T(8,128)(2,1)S(1)}, u32[]{:S(2)}, u32[]{:S(2)}) collective-permute-start(bf16[3,32,512]{2,1,0:T(8,128)(2,1)S(1)} %get-tuple-element.25), channel_id=1, source_target_pairs={{0,1},{1,0},{2,3},{3,2},{4,5},{5,4},{6,7},{7,6},{8,9},{9,8},{10,11... | collective-permute-start | bytes 294920 | tf_op jit(solution)/shard_map/ppermute | solution.py:421
  5.5 2.0 %prepare.1 = (bf16[1536,256]{1,0:T(8,128)(2,1)S(1)}, bf16[128,768]{1,0:T(8,128)(2,1)S(1)}, bf16[32,1280]{1,0:T(8,128)(2,1)S(1)}, bf16[512,1024]{1,0:T(8,128)(2,1)S(1)}, bf16[32,32,256]{2,1,0:T(8,128)(2,1)S(1)}) custom-call(bf16[9,64]{1,0:T(8,128)(2,1)} %tap1_ref.1, bf16[576,64]{1,0:T(8,128)(2,1)} %bitcast.14, bf16[9,64]{1,0:T(8,128)(2,1)} %tap3_ref.1, ...), custom_call_target="tpu_custom_call" | custom-call | tf_op jit(solution)/shard_map/prepare/pallas_call | solution.py:119
  7.5 0.0 collective-permute-done.1.refs_3_
  7.5 0.0 collective-permute-done.refs_2_
  7.5 0.0 copy-start
  7.6 26.8 %denoise.1 = (bf16[32,8,512]{2,1,0:T(8,128)(2,1)S(1)}, bf16[32,8,640]{2,1,0:T(8,128)(2,1)S(1)}) custom-call(s32[2]{0:T(128)} %refs_0_.1, s32[2]{0:T(128)} %bitcast.19, bf16[3,32,512]{2,1,0:T(8,128)(2,1)S(1)} %collective-permute-done.refs_2_, bf16[3,32,512]{2,1,0:T(8,128)(2,1)S(1)} %collective-permute-done.1.refs_3_, ...), custom_call_target="tpu_custom_call" | custom-call | flops 9965666304 | bytes 4194304 | tf_op jit(solution)/shard_map/denoise/pallas_call | solution.py:343
  34.3 18.3 %all_to_all.5.came_ref = bf16[32,8,640]{2,1,0:T(8,128)(2,1)S(1)} all-to-all(bf16[32,8,640]{2,1,0:T(8,128)(2,1)S(1)} %get-tuple-element.19), channel_id=1, replica_groups=mesh['grp'=4,'tile'=32] {'tile'}, dimensions={0} | all-to-all | bytes 655360 | tf_op jit(solution)/shard_map/all_to_all | solution.py:426
  52.6 0.0 copy-done
  52.6 1.6 %stack.1 = (f32[8,4,512]{2,1,0:T(4,128)S(1)}, f32[8,4,512]{2,1,0:T(4,128)S(1)}, f32[8,4,512]{2,1,0:T(4,128)S(1)}, f32[8,4,512]{2,1,0:T(4,128)S(1)}) custom-call(bf16[32,8,640]{2,1,0:T(8,128)(2,1)S(1)} %all_to_all.5.came_ref, bf16[4096,512]{1,0:T(8,128)(2,1)S(1)} %bitcast.12), custom_call_target="tpu_custom_call" | custom-call | tf_op jit(solution)/shard_map/stack/pallas_call | solution.py:391
  54.2 4.0 %collective-permute-start.2 = (f32[8,4,512]{2,1,0:T(4,128)S(1)}, f32[8,4,512]{2,1,0:T(4,128)S(1)}, u32[]{:S(2)}, u32[]{:S(2)}) collective-permute-start(f32[8,4,512]{2,1,0:T(4,128)S(1)} %get-tuple-element.21), channel_id=1, source_target_pairs={{0,64},{32,96},{64,0},{96,32},{1,65},{33,97},{65,1},{97,33},{2,66}... | collective-permute-start | bytes 196616 | tf_op jit(solution)/shard_map/ppermute | solution.py:429
  58.2 1.0 %collective-permute-start.3 = (f32[8,4,512]{2,1,0:T(4,128)S(1)}, f32[8,4,512]{2,1,0:T(4,128)S(1)}, u32[]{:S(2)}, u32[]{:S(2)}) collective-permute-start(f32[8,4,512]{2,1,0:T(4,128)S(1)} %get-tuple-element.22), channel_id=1, source_target_pairs={{0,32},{32,0},{64,96},{96,64},{1,33},{33,1},{65,97},{97,65},{2,34}... | collective-permute-start | bytes 196616 | tf_op jit(solution)/shard_map/ppermute | solution.py:429
  59.2 0.0 collective-permute-start.4
  59.2 0.7 %copy.17 = bf16[32,8,512]{2,1,0:T(8,128)(2,1)} copy(bf16[32,8,512]{2,1,0:T(8,128)(2,1)S(1)} %get-tuple-element.28) | data formatting | bytes 524288
  59.9 0.7 %collective-permute-done.2 = f32[8,4,512]{2,1,0:T(4,128)S(1)} collective-permute-done((f32[8,4,512]{2,1,0:T(4,128)S(1)}, f32[8,4,512]{2,1,0:T(4,128)S(1)}, u32[]{:S(2)}, u32[]{:S(2)}) %collective-permute-start.2) | collective-permute-done | bytes 65568 | tf_op jit(solution)/shard_map/ppermute | solution.py:429
  60.6 2.2 %collective-permute-done.3 = f32[8,4,512]{2,1,0:T(4,128)S(1)} collective-permute-done((f32[8,4,512]{2,1,0:T(4,128)S(1)}, f32[8,4,512]{2,1,0:T(4,128)S(1)}, u32[]{:S(2)}, u32[]{:S(2)}) %collective-permute-start.3) | collective-permute-done | bytes 65568 | tf_op jit(solution)/shard_map/ppermute | solution.py:429
  62.8 1.9 %collective-permute-done.4 = f32[8,4,512]{2,1,0:T(4,128)S(1)} collective-permute-done((f32[8,4,512]{2,1,0:T(4,128)S(1)}, f32[8,4,512]{2,1,0:T(4,128)S(1)}, u32[]{:S(2)}, u32[]{:S(2)}) %collective-permute-start.4) | collective-permute-done | bytes 65568 | tf_op jit(solution)/shard_map/ppermute | solution.py:429
  64.7 0.6 add_add_fusion
  (1 shorter events, 0.0 us)
Async XLA Ops:
  1.8 5.7 %collective-permute-start.1 = (bf16[3,32,512]{2,1,0:T(8,128)(2,1)S(1)}, bf16[3,32,512]{2,1,0:T(8,128)(2,1)S(1)}, u32[]{:S(2)}, u32[]{:S(2)}) collective-permute-start(bf16[3,32,512]{2,1,0:T(8,128)(2,1)S(1)} %get-tuple-element.24), channel_id=1, source_target_pairs={{1,2},{3,4},{5,6},{7,8},{9,10},{11,12},{13,14},{15,16},{17,18},{19... | collective-permute-start | bytes 294920 | tf_op jit(solution)/shard_map/ppermute | solution.py:423
  2.5 5.0 %collective-permute-start = (bf16[3,32,512]{2,1,0:T(8,128)(2,1)S(1)}, bf16[3,32,512]{2,1,0:T(8,128)(2,1)S(1)}, u32[]{:S(2)}, u32[]{:S(2)}) collective-permute-start(bf16[3,32,512]{2,1,0:T(8,128)(2,1)S(1)} %get-tuple-element.25), channel_id=1, source_target_pairs={{0,1},{1,0},{2,3},{3,2},{4,5},{5,4},{6,7},{7,6},{8,9},{9,8},{10,11... | collective-permute-start | bytes 294920 | tf_op jit(solution)/shard_map/ppermute | solution.py:421
  7.5 45.1 %copy-start = (bf16[8,512,512]{2,1,0:T(8,128)(2,1)S(1)}, bf16[8,512,512]{2,1,0:T(8,128)(2,1)}, u32[]{:S(2)}) copy-start(bf16[8,512,512]{2,1,0:T(8,128)(2,1)} %param.11) | copy-start | bytes 12582916
  54.2 6.4 %collective-permute-start.2 = (f32[8,4,512]{2,1,0:T(4,128)S(1)}, f32[8,4,512]{2,1,0:T(4,128)S(1)}, u32[]{:S(2)}, u32[]{:S(2)}) collective-permute-start(f32[8,4,512]{2,1,0:T(4,128)S(1)} %get-tuple-element.21), channel_id=1, source_target_pairs={{0,64},{32,96},{64,0},{96,32},{1,65},{33,97},{65,1},{97,33},{2,66}... | collective-permute-start | bytes 196616 | tf_op jit(solution)/shard_map/ppermute | solution.py:429
  58.2 4.6 %collective-permute-start.3 = (f32[8,4,512]{2,1,0:T(4,128)S(1)}, f32[8,4,512]{2,1,0:T(4,128)S(1)}, u32[]{:S(2)}, u32[]{:S(2)}) collective-permute-start(f32[8,4,512]{2,1,0:T(4,128)S(1)} %get-tuple-element.22), channel_id=1, source_target_pairs={{0,32},{32,0},{64,96},{96,64},{1,33},{33,1},{65,97},{97,65},{2,34}... | collective-permute-start | bytes 196616 | tf_op jit(solution)/shard_map/ppermute | solution.py:429
  59.2 5.5 %collective-permute-start.4 = (f32[8,4,512]{2,1,0:T(4,128)S(1)}, f32[8,4,512]{2,1,0:T(4,128)S(1)}, u32[]{:S(2)}, u32[]{:S(2)}) collective-permute-start(f32[8,4,512]{2,1,0:T(4,128)S(1)} %get-tuple-element.23), channel_id=1, source_target_pairs={{0,96},{32,64},{64,32},{96,0},{1,97},{33,65},{65,33},{97,1},{2,98}... | collective-permute-start | bytes 196616 | tf_op jit(solution)/shard_map/ppermute | solution.py:429

commit v10 on v9

--- a/solution.py
+++ b/solution.py
@@ -92,11 +92,13 @@
         row = [t for pair in zip(kinds[2 * kind], kinds[2 * kind + 1]) for t in pair]
         row = jnp.concatenate(row, axis=1)
         for receiver in range(RD):
-            at = kind * RD + receiver
+            at = RD + receiver // 2 * RD + 2 * kind + receiver % 2
             wide[at : at + 1, receiver * 2 * CH : (receiver + 3) * 2 * CH] = row
     wide[:, : 2 * CH] = wide[:, : 2 * CH] * low
     wide[:, (INNER - 1) * 2 * CH :] = wide[:, (INNER - 1) * 2 * CH :] * high
-    last_ref[...] = wide[...].astype(BF16)
+    for n in range(INNER // 2):
+        rows = slice(2 * n * RD, 2 * (n + 1) * RD)
+        last_ref[rows, :] = wide[n * RD : (n + 2) * RD, n * UNIT : (n + 1) * UNIT].astype(BF16)
 
     time = lax.broadcasted_iota(jnp.int32, (NT, 4 * HALF), 0)
     lane = lax.broadcasted_iota(jnp.int32, (NT, 4 * HALF), 1)
@@ -112,14 +114,14 @@
     shapes = (
         (OUTER * 2 * CH, UNIT),
         (2 * CH, 3 * UNIT),
-        (4 * RD, INNER * 2 * CH),
+        (INNER * RD, UNIT),
         (NT, 4 * HALF),
         (own.shape[0], 4 * RD, HALF),
     )
     return pl.pallas_call(
         prepare_body,
         out_shape=tuple(jax.ShapeDtypeStruct(s, BF16) for s in shapes),
-        scratch_shapes=[pltpu.VMEM(shapes[2], F32)],
+        scratch_shapes=[pltpu.VMEM(((INNER // 2 + 1) * RD, INNER * 2 * CH), F32)],
         compiler_params=pltpu.CompilerParams(vmem_limit_bytes=24 << 20),
         name="prepare",
     )(weight_first, weight_middle, weight_last, own)
@@ -219,11 +221,13 @@
         def act():
             for unit in range(UNITS):
                 shot = pair * UNITS + unit
-                parts = pltpu.matmul_pop(accs[unit][7])
+                parts = [pltpu.matmul_pop(acc) for acc in accs[unit][7:]]
+                sums = [low[RD:] + high[:RD] for low, high in zip(parts, parts[1:])]
+                kinds = [jnp.concatenate([p[2 * k : 2 * k + 2] for p in sums], axis=0) for k in range(4)]
                 seen = own[shot].astype(F32)
                 rows = pl.ds(pl.multiple_of(shot * RD, RD), RD)
-                even = parts[:RD] + delayed(parts[2 * RD : 3 * RD])
-                odd = parts[RD : 2 * RD] + advanced(parts[3 * RD :])
+                even = kinds[0] + delayed(kinds[2])
+                odd = kinds[1] + advanced(kinds[3])
                 cleaned[rows, :HALF] = seen[RD : 2 * RD] - even
                 cleaned[rows, HALF:] = seen[2 * RD : 3 * RD] - odd
 
@@ -252,7 +256,8 @@
 
     def last_job(h2, number):
         lanes = slice(number * UNIT, (number + 1) * UNIT)
-        products = [(lambda unit: accs[unit][7], lambda: last_ref[:, lanes])]
+        rows = slice(2 * number * RD, 2 * (number + 1) * RD)
+        products = [(lambda unit: accs[unit][7 + number], lambda: last_ref[rows, :])]
         return lambda unit: h2[unit, lanes, :], products, []
 
     def stage(now, later, before):
@@ -324,11 +329,11 @@
 
 def denoise_body(*refs):
     pl.run_scoped(
-        lambda *accs: denoise_loop(*refs, (accs[:8], accs[8:])),
+        lambda *accs: denoise_loop(*refs, (accs[: len(accs) // 2], accs[len(accs) // 2 :])),
         *[
-            pltpu.ACC(unit)((BLK if number < 7 else 4 * RD, UNIT), F32)
+            pltpu.ACC(unit)((BLK if number < 7 else 2 * RD, UNIT), F32)
             for unit in range(UNITS)
-            for number in range(8)
+            for number in range(7 + INNER // 2)
         ],
     )
 

time: 65.5 us -> 65.2 us (level)
  no operation moved by 1% of the time
where the time goes in v10:
time: 65.2 us; the launch traced here: 65 us
  Pallas kernels  30 us (46%)
  blocking collectives  18.3 us (28%)
  starting transfers between devices  8.66 us (13%)
  waiting for transfers between devices  4.77 us (7%)
  local copies, waits for them, and re-layouts  1.85 us (3%)
  between operations  0.71 us (1%)
  other arithmetic  0.7 us (1%)
    pallas_call x1, Pallas kernels, denoise(): pl.pallas_call(denoise_body, out_shape=(pltpu.VMEM((shots, RD, NT), BF16)...  26.5 us
    all_to_all x1, blocking collectives, on_device(): came = lax.all_to_all(sent, 'tile', 0, 0, tiled=True)  18.3 us
    ppermute x3, starting transfers between devices, on_device(): lax.ppermute(parts[apart - 1], 'grp', [(g, g ^ apart) for g in range(grou...  4.98 us
    ppermute x3, waiting for transfers between devices, on_device(): lax.ppermute(parts[apart - 1], 'grp', [(g, g ^ apart) for g in range(grou...  4.77 us
    ppermute x1, starting transfers between devices, on_device(): near = lax.ppermute(near, 'tile', [(i, i ^ 1) for i in range(tiles)])  3.01 us
    pallas_call x1, Pallas kernels, prepare(): pl.pallas_call(prepare_body, out_shape=tuple((jax.ShapeDtypeStruct(s, BF1...  1.97 us
    pallas_call x1, Pallas kernels, stack(): pl.pallas_call(stack_body, out_shape=(part,) * groups, compiler_params=pl...  1.57 us
  transfers between devices with their start and end apart: 5, of which 3 were waited for; matrix products, arithmetic and copies ran while one was open for 1% of the time, Pallas kernels for 3%

profile of v10, /device:TPU:0, one launch (start us, length us, event | category | flops | bytes accessed | tf_op | source)
XLA Modules:
  0.0 65.0 jit_solution(4911125955111210900)
XLA Ops:
  0.6 1.1 %fusion = (bf16[32,3,512]{2,1,0:T(4,128)(2,1)S(1)}, bf16[32,3,512]{2,1,0:T(4,128)(2,1)S(1)}) fusion(bf16[32,8,512]{2,1,0:T(8,128)(2,1)} %own_ref.1), kind=kLoop, calls=%fused_computation.3 | loop fusion | bytes 393216 | tf_op jit(solution)/shard_map/slice | solution.py:406
  1.8 0.7 %collective-permute-start.1 = (bf16[3,32,512]{2,1,0:T(8,128)(2,1)S(1)}, bf16[3,32,512]{2,1,0:T(8,128)(2,1)S(1)}, u32[]{:S(2)}, u32[]{:S(2)}) collective-permute-start(bf16[3,32,512]{2,1,0:T(8,128)(2,1)S(1)} %get-tuple-element.24), channel_id=1, source_target_pairs={{1,2},{3,4},{5,6},{7,8},{9,10},{11,12},{13,14},{15,16},{17,18},{19... | collective-permute-start | bytes 294920 | tf_op jit(solution)/shard_map/ppermute | solution.py:428
  2.5 3.0 %collective-permute-start = (bf16[3,32,512]{2,1,0:T(8,128)(2,1)S(1)}, bf16[3,32,512]{2,1,0:T(8,128)(2,1)S(1)}, u32[]{:S(2)}, u32[]{:S(2)}) collective-permute-start(bf16[3,32,512]{2,1,0:T(8,128)(2,1)S(1)} %get-tuple-element.25), channel_id=1, source_target_pairs={{0,1},{1,0},{2,3},{3,2},{4,5},{5,4},{6,7},{7,6},{8,9},{9,8},{10,11... | collective-permute-start | bytes 294920 | tf_op jit(solution)/shard_map/ppermute | solution.py:426
  5.5 2.0 %prepare.1 = (bf16[1536,256]{1,0:T(8,128)(2,1)S(1)}, bf16[128,768]{1,0:T(8,128)(2,1)S(1)}, bf16[80,256]{1,0:T(8,128)(2,1)S(1)}, bf16[512,1024]{1,0:T(8,128)(2,1)S(1)}, bf16[32,32,256]{2,1,0:T(8,128)(2,1)S(1)}) custom-call(bf16[9,64]{1,0:T(8,128)(2,1)} %tap1_ref.1, bf16[576,64]{1,0:T(8,128)(2,1)} %bitcast.14, bf16[9,64]{1,0:T(8,128)(2,1)} %tap3_ref.1, ...), custom_call_target="tpu_custom_call" | custom-call | tf_op jit(solution)/shard_map/prepare/pallas_call | solution.py:121
  7.5 0.0 collective-permute-done.1.refs_3_
  7.5 0.0 collective-permute-done.refs_2_
  7.5 0.0 copy-start
  7.5 26.5 %denoise.1 = (bf16[32,8,512]{2,1,0:T(8,128)(2,1)S(1)}, bf16[32,8,640]{2,1,0:T(8,128)(2,1)S(1)}) custom-call(s32[2]{0:T(128)} %refs_0_.1, s32[2]{0:T(128)} %bitcast.19, bf16[3,32,512]{2,1,0:T(8,128)(2,1)S(1)} %collective-permute-done.refs_2_, bf16[3,32,512]{2,1,0:T(8,128)(2,1)S(1)} %collective-permute-done.1.refs_3_, ...), custom_call_target="tpu_custom_call" | custom-call | flops 9965666304 | bytes 4194304 | tf_op jit(solution)/shard_map/denoise/pallas_call | solution.py:348
  34.0 18.3 %all_to_all.5.came_ref = bf16[32,8,640]{2,1,0:T(8,128)(2,1)S(1)} all-to-all(bf16[32,8,640]{2,1,0:T(8,128)(2,1)S(1)} %get-tuple-element.19), channel_id=1, replica_groups=mesh['grp'=4,'tile'=32] {'tile'}, dimensions={0} | all-to-all | bytes 655360 | tf_op jit(solution)/shard_map/all_to_all | solution.py:431
  52.3 0.0 copy-done
  52.4 1.6 %stack.1 = (f32[8,4,512]{2,1,0:T(4,128)S(1)}, f32[8,4,512]{2,1,0:T(4,128)S(1)}, f32[8,4,512]{2,1,0:T(4,128)S(1)}, f32[8,4,512]{2,1,0:T(4,128)S(1)}) custom-call(bf16[32,8,640]{2,1,0:T(8,128)(2,1)S(1)} %all_to_all.5.came_ref, bf16[4096,512]{1,0:T(8,128)(2,1)S(1)} %bitcast.12), custom_call_target="tpu_custom_call" | custom-call | tf_op jit(solution)/shard_map/stack/pallas_call | solution.py:396
  53.9 4.0 %collective-permute-start.2 = (f32[8,4,512]{2,1,0:T(4,128)S(1)}, f32[8,4,512]{2,1,0:T(4,128)S(1)}, u32[]{:S(2)}, u32[]{:S(2)}) collective-permute-start(f32[8,4,512]{2,1,0:T(4,128)S(1)} %get-tuple-element.21), channel_id=1, source_target_pairs={{0,64},{32,96},{64,0},{96,32},{1,65},{33,97},{65,1},{97,33},{2,66}... | collective-permute-start | bytes 196616 | tf_op jit(solution)/shard_map/ppermute | solution.py:434
  57.9 1.0 %collective-permute-start.3 = (f32[8,4,512]{2,1,0:T(4,128)S(1)}, f32[8,4,512]{2,1,0:T(4,128)S(1)}, u32[]{:S(2)}, u32[]{:S(2)}) collective-permute-start(f32[8,4,512]{2,1,0:T(4,128)S(1)} %get-tuple-element.22), channel_id=1, source_target_pairs={{0,32},{32,0},{64,96},{96,64},{1,33},{33,1},{65,97},{97,65},{2,34}... | collective-permute-start | bytes 196616 | tf_op jit(solution)/shard_map/ppermute | solution.py:434
  58.9 0.0 collective-permute-start.4
  58.9 0.7 %copy.17 = bf16[32,8,512]{2,1,0:T(8,128)(2,1)} copy(bf16[32,8,512]{2,1,0:T(8,128)(2,1)S(1)} %get-tuple-element.28) | data formatting | bytes 524288
  59.6 0.8 %collective-permute-done.2 = f32[8,4,512]{2,1,0:T(4,128)S(1)} collective-permute-done((f32[8,4,512]{2,1,0:T(4,128)S(1)}, f32[8,4,512]{2,1,0:T(4,128)S(1)}, u32[]{:S(2)}, u32[]{:S(2)}) %collective-permute-start.2) | collective-permute-done | bytes 65568 | tf_op jit(solution)/shard_map/ppermute | solution.py:434
  60.4 2.2 %collective-permute-done.3 = f32[8,4,512]{2,1,0:T(4,128)S(1)} collective-permute-done((f32[8,4,512]{2,1,0:T(4,128)S(1)}, f32[8,4,512]{2,1,0:T(4,128)S(1)}, u32[]{:S(2)}, u32[]{:S(2)}) %collective-permute-start.3) | collective-permute-done | bytes 65568 | tf_op jit(solution)/shard_map/ppermute | solution.py:434
  62.5 1.9 %collective-permute-done.4 = f32[8,4,512]{2,1,0:T(4,128)S(1)} collective-permute-done((f32[8,4,512]{2,1,0:T(4,128)S(1)}, f32[8,4,512]{2,1,0:T(4,128)S(1)}, u32[]{:S(2)}, u32[]{:S(2)}) %collective-permute-start.4) | collective-permute-done | bytes 65568 | tf_op jit(solution)/shard_map/ppermute | solution.py:434
  64.4 0.6 add_add_fusion
  (1 shorter events, 0.0 us)
Async XLA Ops:
  1.8 5.7 %collective-permute-start.1 = (bf16[3,32,512]{2,1,0:T(8,128)(2,1)S(1)}, bf16[3,32,512]{2,1,0:T(8,128)(2,1)S(1)}, u32[]{:S(2)}, u32[]{:S(2)}) collective-permute-start(bf16[3,32,512]{2,1,0:T(8,128)(2,1)S(1)} %get-tuple-element.24), channel_id=1, source_target_pairs={{1,2},{3,4},{5,6},{7,8},{9,10},{11,12},{13,14},{15,16},{17,18},{19... | collective-permute-start | bytes 294920 | tf_op jit(solution)/shard_map/ppermute | solution.py:428
  2.5 5.0 %collective-permute-start = (bf16[3,32,512]{2,1,0:T(8,128)(2,1)S(1)}, bf16[3,32,512]{2,1,0:T(8,128)(2,1)S(1)}, u32[]{:S(2)}, u32[]{:S(2)}) collective-permute-start(bf16[3,32,512]{2,1,0:T(8,128)(2,1)S(1)} %get-tuple-element.25), channel_id=1, source_target_pairs={{0,1},{1,0},{2,3},{3,2},{4,5},{5,4},{6,7},{7,6},{8,9},{9,8},{10,11... | collective-permute-start | bytes 294920 | tf_op jit(solution)/shard_map/ppermute | solution.py:426
  7.5 44.8 %copy-start = (bf16[8,512,512]{2,1,0:T(8,128)(2,1)S(1)}, bf16[8,512,512]{2,1,0:T(8,128)(2,1)}, u32[]{:S(2)}) copy-start(bf16[8,512,512]{2,1,0:T(8,128)(2,1)} %param.11) | copy-start | bytes 12582916
  53.9 6.5 %collective-permute-start.2 = (f32[8,4,512]{2,1,0:T(4,128)S(1)}, f32[8,4,512]{2,1,0:T(4,128)S(1)}, u32[]{:S(2)}, u32[]{:S(2)}) collective-permute-start(f32[8,4,512]{2,1,0:T(4,128)S(1)} %get-tuple-element.21), channel_id=1, source_target_pairs={{0,64},{32,96},{64,0},{96,32},{1,65},{33,97},{65,1},{97,33},{2,66}... | collective-permute-start | bytes 196616 | tf_op jit(solution)/shard_map/ppermute | solution.py:434
  57.9 4.6 %collective-permute-start.3 = (f32[8,4,512]{2,1,0:T(4,128)S(1)}, f32[8,4,512]{2,1,0:T(4,128)S(1)}, u32[]{:S(2)}, u32[]{:S(2)}) collective-permute-start(f32[8,4,512]{2,1,0:T(4,128)S(1)} %get-tuple-element.22), channel_id=1, source_target_pairs={{0,32},{32,0},{64,96},{96,64},{1,33},{33,1},{65,97},{97,65},{2,34}... | collective-permute-start | bytes 196616 | tf_op jit(solution)/shard_map/ppermute | solution.py:434
  58.9 5.5 %collective-permute-start.4 = (f32[8,4,512]{2,1,0:T(4,128)S(1)}, f32[8,4,512]{2,1,0:T(4,128)S(1)}, u32[]{:S(2)}, u32[]{:S(2)}) collective-permute-start(f32[8,4,512]{2,1,0:T(4,128)S(1)} %get-tuple-element.23), channel_id=1, source_target_pairs={{0,96},{32,64},{64,32},{96,0},{1,97},{33,65},{65,33},{97,1},{2,98}... | collective-permute-start | bytes 196616 | tf_op jit(solution)/shard_map/ppermute | solution.py:434

commit v11 on v10

--- a/solution.py
+++ b/solution.py
@@ -20,7 +20,7 @@
 INNER = RD + 2
 EDGE = 3
 SIDE = 16
-STAGES = 4
+STAGES = 6
 F32 = jnp.float32
 BF16 = jnp.bfloat16
 

time: 65.2 us -> 65 us (level)
  no operation moved by 1% of the time
where the time goes in v11:
time: 65 us; the launch traced here: 64.9 us
  Pallas kernels  29.9 us (46%)
  blocking collectives  18.3 us (28%)
  starting transfers between devices  8.66 us (13%)
  waiting for transfers between devices  4.77 us (7%)
  local copies, waits for them, and re-layouts  1.85 us (3%)
  between operations  0.71 us (1%)
  other arithmetic  0.7 us (1%)
    pallas_call x1, Pallas kernels, denoise(): pl.pallas_call(denoise_body, out_shape=(pltpu.VMEM((shots, RD, NT), BF16)...  26.3 us
    all_to_all x1, blocking collectives, on_device(): came = lax.all_to_all(sent, 'tile', 0, 0, tiled=True)  18.3 us
    ppermute x3, starting transfers between devices, on_device(): lax.ppermute(parts[apart - 1], 'grp', [(g, g ^ apart) for g in range(grou...  4.98 us
    ppermute x3, waiting for transfers between devices, on_device(): lax.ppermute(parts[apart - 1], 'grp', [(g, g ^ apart) for g in range(grou...  4.77 us
    ppermute x1, starting transfers between devices, on_device(): near = lax.ppermute(near, 'tile', [(i, i ^ 1) for i in range(tiles)])  3.01 us
    pallas_call x1, Pallas kernels, prepare(): pl.pallas_call(prepare_body, out_shape=tuple((jax.ShapeDtypeStruct(s, BF1...  1.97 us
    pallas_call x1, Pallas kernels, stack(): pl.pallas_call(stack_body, out_shape=(part,) * groups, compiler_params=pl...  1.57 us
  transfers between devices with their start and end apart: 5, of which 3 were waited for; matrix products, arithmetic and copies ran while one was open for 1% of the time, Pallas kernels for 3%

profile of v11, /device:TPU:0, one launch (start us, length us, event | category | flops | bytes accessed | tf_op | source)
XLA Modules:
  0.0 64.9 jit_solution(9551726747019275269)
XLA Ops:
  0.6 1.1 %fusion = (bf16[32,3,512]{2,1,0:T(4,128)(2,1)S(1)}, bf16[32,3,512]{2,1,0:T(4,128)(2,1)S(1)}) fusion(bf16[32,8,512]{2,1,0:T(8,128)(2,1)} %own_ref.1), kind=kLoop, calls=%fused_computation.3 | loop fusion | bytes 393216 | tf_op jit(solution)/shard_map/slice | solution.py:406
  1.8 0.7 %collective-permute-start.1 = (bf16[3,32,512]{2,1,0:T(8,128)(2,1)S(1)}, bf16[3,32,512]{2,1,0:T(8,128)(2,1)S(1)}, u32[]{:S(2)}, u32[]{:S(2)}) collective-permute-start(bf16[3,32,512]{2,1,0:T(8,128)(2,1)S(1)} %get-tuple-element.24), channel_id=1, source_target_pairs={{1,2},{3,4},{5,6},{7,8},{9,10},{11,12},{13,14},{15,16},{17,18},{19... | collective-permute-start | bytes 294920 | tf_op jit(solution)/shard_map/ppermute | solution.py:428
  2.5 3.0 %collective-permute-start = (bf16[3,32,512]{2,1,0:T(8,128)(2,1)S(1)}, bf16[3,32,512]{2,1,0:T(8,128)(2,1)S(1)}, u32[]{:S(2)}, u32[]{:S(2)}) collective-permute-start(bf16[3,32,512]{2,1,0:T(8,128)(2,1)S(1)} %get-tuple-element.25), channel_id=1, source_target_pairs={{0,1},{1,0},{2,3},{3,2},{4,5},{5,4},{6,7},{7,6},{8,9},{9,8},{10,11... | collective-permute-start | bytes 294920 | tf_op jit(solution)/shard_map/ppermute | solution.py:426
  5.5 2.0 %prepare.1 = (bf16[1536,256]{1,0:T(8,128)(2,1)S(1)}, bf16[128,768]{1,0:T(8,128)(2,1)S(1)}, bf16[80,256]{1,0:T(8,128)(2,1)S(1)}, bf16[512,1024]{1,0:T(8,128)(2,1)S(1)}, bf16[32,32,256]{2,1,0:T(8,128)(2,1)S(1)}) custom-call(bf16[9,64]{1,0:T(8,128)(2,1)} %tap1_ref.1, bf16[576,64]{1,0:T(8,128)(2,1)} %bitcast.14, bf16[9,64]{1,0:T(8,128)(2,1)} %tap3_ref.1, ...), custom_call_target="tpu_custom_call" | custom-call | tf_op jit(solution)/shard_map/prepare/pallas_call | solution.py:121
  7.5 0.0 collective-permute-done.1.refs_3_
  7.5 0.0 collective-permute-done.refs_2_
  7.5 0.0 copy-start
  7.5 26.3 %denoise.1 = (bf16[32,8,512]{2,1,0:T(8,128)(2,1)S(1)}, bf16[32,8,640]{2,1,0:T(8,128)(2,1)S(1)}) custom-call(s32[2]{0:T(128)} %refs_0_.1, s32[2]{0:T(128)} %bitcast.19, bf16[3,32,512]{2,1,0:T(8,128)(2,1)S(1)} %collective-permute-done.refs_2_, bf16[3,32,512]{2,1,0:T(8,128)(2,1)S(1)} %collective-permute-done.1.refs_3_, ...), custom_call_target="tpu_custom_call" | custom-call | flops 9965666304 | bytes 4194304 | tf_op jit(solution)/shard_map/denoise/pallas_call | solution.py:348
  33.9 18.3 %all_to_all.5.came_ref = bf16[32,8,640]{2,1,0:T(8,128)(2,1)S(1)} all-to-all(bf16[32,8,640]{2,1,0:T(8,128)(2,1)S(1)} %get-tuple-element.19), channel_id=1, replica_groups=mesh['grp'=4,'tile'=32] {'tile'}, dimensions={0} | all-to-all | bytes 655360 | tf_op jit(solution)/shard_map/all_to_all | solution.py:431
  52.2 0.0 copy-done
  52.2 1.6 %stack.1 = (f32[8,4,512]{2,1,0:T(4,128)S(1)}, f32[8,4,512]{2,1,0:T(4,128)S(1)}, f32[8,4,512]{2,1,0:T(4,128)S(1)}, f32[8,4,512]{2,1,0:T(4,128)S(1)}) custom-call(bf16[32,8,640]{2,1,0:T(8,128)(2,1)S(1)} %all_to_all.5.came_ref, bf16[4096,512]{1,0:T(8,128)(2,1)S(1)} %bitcast.12), custom_call_target="tpu_custom_call" | custom-call | tf_op jit(solution)/shard_map/stack/pallas_call | solution.py:396
  53.7 4.0 %collective-permute-start.2 = (f32[8,4,512]{2,1,0:T(4,128)S(1)}, f32[8,4,512]{2,1,0:T(4,128)S(1)}, u32[]{:S(2)}, u32[]{:S(2)}) collective-permute-start(f32[8,4,512]{2,1,0:T(4,128)S(1)} %get-tuple-element.21), channel_id=1, source_target_pairs={{0,64},{32,96},{64,0},{96,32},{1,65},{33,97},{65,1},{97,33},{2,66}... | collective-permute-start | bytes 196616 | tf_op jit(solution)/shard_map/ppermute | solution.py:434
  57.7 1.0 %collective-permute-start.3 = (f32[8,4,512]{2,1,0:T(4,128)S(1)}, f32[8,4,512]{2,1,0:T(4,128)S(1)}, u32[]{:S(2)}, u32[]{:S(2)}) collective-permute-start(f32[8,4,512]{2,1,0:T(4,128)S(1)} %get-tuple-element.22), channel_id=1, source_target_pairs={{0,32},{32,0},{64,96},{96,64},{1,33},{33,1},{65,97},{97,65},{2,34}... | collective-permute-start | bytes 196616 | tf_op jit(solution)/shard_map/ppermute | solution.py:434
  58.7 0.0 collective-permute-start.4
  58.7 0.7 %copy.17 = bf16[32,8,512]{2,1,0:T(8,128)(2,1)} copy(bf16[32,8,512]{2,1,0:T(8,128)(2,1)S(1)} %get-tuple-element.28) | data formatting | bytes 524288
  59.4 0.8 %collective-permute-done.2 = f32[8,4,512]{2,1,0:T(4,128)S(1)} collective-permute-done((f32[8,4,512]{2,1,0:T(4,128)S(1)}, f32[8,4,512]{2,1,0:T(4,128)S(1)}, u32[]{:S(2)}, u32[]{:S(2)}) %collective-permute-start.2) | collective-permute-done | bytes 65568 | tf_op jit(solution)/shard_map/ppermute | solution.py:434
  60.2 2.2 %collective-permute-done.3 = f32[8,4,512]{2,1,0:T(4,128)S(1)} collective-permute-done((f32[8,4,512]{2,1,0:T(4,128)S(1)}, f32[8,4,512]{2,1,0:T(4,128)S(1)}, u32[]{:S(2)}, u32[]{:S(2)}) %collective-permute-start.3) | collective-permute-done | bytes 65568 | tf_op jit(solution)/shard_map/ppermute | solution.py:434
  62.4 1.9 %collective-permute-done.4 = f32[8,4,512]{2,1,0:T(4,128)S(1)} collective-permute-done((f32[8,4,512]{2,1,0:T(4,128)S(1)}, f32[8,4,512]{2,1,0:T(4,128)S(1)}, u32[]{:S(2)}, u32[]{:S(2)}) %collective-permute-start.4) | collective-permute-done | bytes 65568 | tf_op jit(solution)/shard_map/ppermute | solution.py:434
  64.2 0.6 add_add_fusion
  (1 shorter events, 0.0 us)
Async XLA Ops:
  1.8 5.7 %collective-permute-start.1 = (bf16[3,32,512]{2,1,0:T(8,128)(2,1)S(1)}, bf16[3,32,512]{2,1,0:T(8,128)(2,1)S(1)}, u32[]{:S(2)}, u32[]{:S(2)}) collective-permute-start(bf16[3,32,512]{2,1,0:T(8,128)(2,1)S(1)} %get-tuple-element.24), channel_id=1, source_target_pairs={{1,2},{3,4},{5,6},{7,8},{9,10},{11,12},{13,14},{15,16},{17,18},{19... | collective-permute-start | bytes 294920 | tf_op jit(solution)/shard_map/ppermute | solution.py:428
  2.5 5.0 %collective-permute-start = (bf16[3,32,512]{2,1,0:T(8,128)(2,1)S(1)}, bf16[3,32,512]{2,1,0:T(8,128)(2,1)S(1)}, u32[]{:S(2)}, u32[]{:S(2)}) collective-permute-start(bf16[3,32,512]{2,1,0:T(8,128)(2,1)S(1)} %get-tuple-element.25), channel_id=1, source_target_pairs={{0,1},{1,0},{2,3},{3,2},{4,5},{5,4},{6,7},{7,6},{8,9},{9,8},{10,11... | collective-permute-start | bytes 294920 | tf_op jit(solution)/shard_map/ppermute | solution.py:426
  7.5 44.7 %copy-start = (bf16[8,512,512]{2,1,0:T(8,128)(2,1)S(1)}, bf16[8,512,512]{2,1,0:T(8,128)(2,1)}, u32[]{:S(2)}) copy-start(bf16[8,512,512]{2,1,0:T(8,128)(2,1)} %param.11) | copy-start | bytes 12582916
  53.7 6.5 %collective-permute-start.2 = (f32[8,4,512]{2,1,0:T(4,128)S(1)}, f32[8,4,512]{2,1,0:T(4,128)S(1)}, u32[]{:S(2)}, u32[]{:S(2)}) collective-permute-start(f32[8,4,512]{2,1,0:T(4,128)S(1)} %get-tuple-element.21), channel_id=1, source_target_pairs={{0,64},{32,96},{64,0},{96,32},{1,65},{33,97},{65,1},{97,33},{2,66}... | collective-permute-start | bytes 196616 | tf_op jit(solution)/shard_map/ppermute | solution.py:434
  57.7 4.6 %collective-permute-start.3 = (f32[8,4,512]{2,1,0:T(4,128)S(1)}, f32[8,4,512]{2,1,0:T(4,128)S(1)}, u32[]{:S(2)}, u32[]{:S(2)}) collective-permute-start(f32[8,4,512]{2,1,0:T(4,128)S(1)} %get-tuple-element.22), channel_id=1, source_target_pairs={{0,32},{32,0},{64,96},{96,64},{1,33},{33,1},{65,97},{97,65},{2,34}... | collective-permute-start | bytes 196616 | tf_op jit(solution)/shard_map/ppermute | solution.py:434
  58.7 5.5 %collective-permute-start.4 = (f32[8,4,512]{2,1,0:T(4,128)S(1)}, f32[8,4,512]{2,1,0:T(4,128)S(1)}, u32[]{:S(2)}, u32[]{:S(2)}) collective-permute-start(f32[8,4,512]{2,1,0:T(4,128)S(1)} %get-tuple-element.23), channel_id=1, source_target_pairs={{0,96},{32,64},{64,32},{96,0},{1,97},{33,65},{65,33},{97,1},{2,98}... | collective-permute-start | bytes 196616 | tf_op jit(solution)/shard_map/ppermute | solution.py:434
